TPU v7x, 128 devices: a whole 4x4x4 slice. The times are simulated.
128 devices in a mesh: row: 16 (over x, z), col: 8 (over y, core).
Axes of the slice: x: 4, y: 4, z: 4, core: 2. Of those that a mesh axis runs over, the one named last changes fastest.
Arguments:
- qkv: bfloat16 [3, 1408, 32768], P(None, 'col', 'row'), may hold values from -12.1 to 12.1
- residual_in: bfloat16 [1408, 32768], P('col', 'row'), may hold values from -3 to 3
- out_weight: bfloat16 [1408, 1408], replicated, may hold values from -0.625 to 0.625
- merge_weight: bfloat16 [1408, 5632], P('col'), may hold values from -0.078125 to 0.078125
- merge_gain: float32 [1408], replicated, may hold values from 0.1 to 1.9
- image_groups: int32 [64], replicated, may hold values from 1 to 256, 8192 in all
- dest_row: int32 [8192], P('row'), may hold values from 0 to 8191, as said below
Outputs:
- layer_out: bfloat16 [1408, 32768], P('col', 'row')
- image_rows: bfloat16 [1408, 8192], P('col', 'row')
Inputs may be any that keep to these rules, and one draw needn't show every extreme that they name: dest_row is a permutation of 0 to 8191. Of the 512 entries held by each index of row, exactly 32 fall in each aligned block of 512 output rows.
All inputs are finite; a program needn't handle non-finite values.
Results may differ from a plain program's by a relative error of at most 0.0064.
Values may be sent and summed in bfloat16 or wider, within the bound.
A program may use at most 128 MiB of HBM per device.

v0:
```python
import math

import jax
import jax.numpy as jnp
from jax import lax
from jax.sharding import PartitionSpec as P

HEAD_DIM = 88


def with_halo(cells, sides, width):
    for axis, dim in sides:
        count = lax.axis_size(axis)
        ends = count - 1
        head = lax.slice_in_dim(cells, 0, width, axis=dim)
        tail = lax.slice_in_dim(cells, cells.shape[dim] - width, cells.shape[dim], axis=dim)
        cells = jnp.concatenate(
            [
                lax.ppermute(tail, axis, [(i, (i + 1) % count) for i in range(ends)]),
                cells,
                lax.ppermute(head, axis, [((i + 1) % count, i) for i in range(ends)]),
            ],
            axis=dim,
        )
    return cells


def image_labels(positions, image_ends, all_tokens):
    inside = (positions >= 0) & (positions < all_tokens)
    counted = jnp.sum((positions[:, None] >= image_ends[None, :]).astype(jnp.int32), axis=1)
    return jnp.where(inside, counted, -1)


def body(qkv, residual_in, out_weight, merge_weight, merge_gain, image_groups, dest_row):
    width_here = qkv.shape[1]
    tok_rows = qkv.shape[2]
    heads_here = width_here // HEAD_DIM
    full_width = out_weight.shape[0]
    reach_rows = tok_rows // 2
    block_rows = min(1024, tok_rows)
    block_count = tok_rows // block_rows
    window = block_rows + 2 * reach_rows
    row_count = lax.axis_size("row")
    row_id = lax.axis_index("row")
    col_id = lax.axis_index("col")
    all_tokens = tok_rows * row_count
    score_scale = 1.0 / math.sqrt(HEAD_DIM)
    image_ends = jnp.cumsum(image_groups) * 4
    extended = with_halo(qkv[1:], (("row", 2),), reach_rows)
    positions = (
        row_id * tok_rows - reach_rows + jnp.arange(tok_rows + 2 * reach_rows, dtype=jnp.int32)
    )
    labels = image_labels(positions, image_ends, all_tokens)

    def attend(block_id):
        first_row = block_id * block_rows
        queries = lax.dynamic_slice_in_dim(qkv[0], first_row, block_rows, 1).reshape(
            heads_here, HEAD_DIM, block_rows
        )
        key_block = lax.dynamic_slice_in_dim(extended[0], first_row, window, 1).reshape(
            heads_here, HEAD_DIM, window
        )
        value_block = lax.dynamic_slice_in_dim(extended[1], first_row, window, 1).reshape(
            heads_here, HEAD_DIM, window
        )
        query_labels = lax.dynamic_slice_in_dim(labels, first_row + reach_rows, block_rows, 0)
        key_labels = lax.dynamic_slice_in_dim(labels, first_row, window, 0)
        scores = (
            jnp.einsum("hdq,hdk->hqk", queries, key_block, preferred_element_type=jnp.float32)
            * score_scale
        )
        same_image = (query_labels[:, None] == key_labels[None, :])[None]
        scores = jnp.where(same_image, scores, -1e30)
        row_max = jnp.max(scores, axis=2, keepdims=True)
        exponent = jnp.exp(scores - row_max)
        totals = jnp.sum(exponent, axis=2)
        weights = exponent.astype(jnp.bfloat16)
        weighted = jnp.einsum(
            "hqk,hdk->hdq", weights, value_block, preferred_element_type=jnp.float32
        )
        weighted = weighted / totals[:, None, :]
        return weighted.astype(jnp.bfloat16).reshape(width_here, block_rows)

    attended = lax.map(attend, jnp.arange(block_count, dtype=jnp.int32))
    attended = jnp.transpose(attended, (1, 0, 2)).reshape(width_here, tok_rows)
    head_weight = lax.dynamic_slice_in_dim(out_weight, col_id * width_here, width_here, 0)
    partial_value = lax.dot_general(
        head_weight, attended, (((0,), (0,)), ((), ())), preferred_element_type=jnp.float32
    )
    projected = lax.psum_scatter(partial_value, "col", scatter_dimension=0, tiled=True)
    layer_out = (residual_in.astype(jnp.float32) + projected).astype(jnp.bfloat16)
    full_rows = lax.all_gather(layer_out, "col", axis=0, tiled=True)
    values32 = full_rows.astype(jnp.float32)
    centre = jnp.mean(values32, axis=0, keepdims=True)
    spread = jnp.mean(jnp.square(values32 - centre), axis=0, keepdims=True)
    normed = ((values32 - centre) * lax.rsqrt(spread + 1e-06) * merge_gain[:, None]).astype(
        jnp.bfloat16
    )
    group_rows = tok_rows // 4
    grouped = normed.reshape(full_width, group_rows, 4)
    weight_parts = merge_weight.reshape(width_here, 4, full_width)
    merged = jnp.einsum(
        "ojf,fgj->og", weight_parts, grouped, preferred_element_type=jnp.float32
    ).astype(jnp.bfloat16)
    empty_rows = jnp.zeros((width_here, group_rows), jnp.bfloat16)
    every_row, every_dest = (
        lax.all_gather(merged, "row", axis=1, tiled=True),
        lax.all_gather(dest_row, "row", axis=0, tiled=True),
    )
    slot_index = every_dest - row_id * group_rows
    slot_index = jnp.where((slot_index >= 0) & (slot_index < group_rows), slot_index, group_rows)
    image_rows = empty_rows.at[:, slot_index].set(every_row, mode="drop")
    return (layer_out, image_rows)


def solution(mesh):
    return jax.shard_map(
        body,
        mesh=mesh,
        in_specs=(P(None, "col", "row"), P("col", "row"), P(), P("col", None), P(), P(), P("row")),
        out_specs=(P("col", "row"), P("col", "row")),
        check_vma=False,
    )
```

profile of v0, /device:TPU:0, one launch (start us, length us, event | category | flops | bytes accessed | tf_op | source)
XLA Modules:
  0.0 381.6 jit_solution(7010875313808431647)
XLA Ops:
  7.2 0.0 slice-start
  7.2 0.0 copy-start.5
  7.2 0.0 reduce-scatter.2.cloned.1.call-start
  7.2 2.4 fusion.44
  9.7 3.9 %collective-permute-start = (bf16[2,176,1024]{2,1,0:T(8,128)(2,1)}, bf16[2,176,1024]{2,1,0:T(8,128)(2,1)S(1)}, u32[]{:S(2)}, u32[]{:S(2)}) collective-permute-start(bf16[2,176,1024]{2,1,0:T(8,128)(2,1)} %get-tuple-element.106), channel_id=1, source_target_pairs={{0,8},{8,16},{16,24},{24,32},{32,40},{40,48},{48,56},{56,64},{64,7... | collective-permute-start | bytes 2162696 | tf_op jit(solution)/shard_map/ppermute | solution.py:19
  13.6 1.3 collective-permute-start.1
  14.9 0.0 copy-done.5
  15.0 0.1 copy.28
  15.1 0.1 reduce-window.8
  15.2 0.1 multiply_reduce_fusion
  15.3 0.2 convert_reduce_fusion.1
  15.5 13.8 %collective-permute-done = bf16[2,176,1024]{2,1,0:T(8,128)(2,1)S(1)} collective-permute-done((bf16[2,176,1024]{2,1,0:T(8,128)(2,1)}, bf16[2,176,1024]{2,1,0:T(8,128)(2,1)S(1)}, u32[]{:S(2)}, u32[]{:S(2)}) %collective-permute-start) | collective-permute-done | bytes 720928 | tf_op jit(solution)/shard_map/ppermute | solution.py:19
  29.3 4.1 %collective-permute-done.1 = bf16[2,176,1024]{2,1,0:T(8,128)(2,1)} collective-permute-done((bf16[2,176,1024]{2,1,0:T(8,128)(2,1)S(1)}, bf16[2,176,1024]{2,1,0:T(8,128)(2,1)}, u32[]{:S(2)}, u32[]{:S(2)}) %collective-permute-start.1) | collective-permute-done | bytes 720928 | tf_op jit(solution)/shard_map/ppermute | solution.py:21
  33.4 0.0 slice-done
  33.4 3.1 pad_maximum_fusion
  36.4 91.2 %while.12 = (s32[]{:T(128)}, bf16[2,176,1024]{2,1,0:T(8,128)(2,1)}, bf16[2,176,4096]{2,1,0:T(8,128)(2,1)}, s32[2]{0:T(128)S(1)}, s32[4096]{0:T(1024)S(1)}, /*ind...) while((s32[]{:T(128)}, bf16[2,176,1024]{2,1,0:T(8,128)(2,1)}, ...), condition=%wide.region_5.6_spmd, body=%wide.region_2.5_spmd.sunk | while | flops 2287300608 | bytes 108356392 | solution.py:84
  36.4 0.7 dynamic_slice.44
  37.8 2.0 broadcast_compare_fusion.2
  39.8 2.1 fusion.61
  41.9 1.6 constant_dynamic-slice_fusion.5
  43.6 1.2 slice.41
  44.8 12.6 %fusion.62 = (f32[2,1024]{1,0:T(2,128)S(1)}, f32[2,1024,3072]{2,1,0:T(8,128)}) fusion(pred[1024,3072]{1,0:T(8,128)(4,1)S(1)} %broadcast_compare_fusion.2, bf16[2,88,1024]{2,1,0:T(8,128)(2,1)S(1)} %bitcast.59, bf16[2,88,3072]{2,1,0:T(8,128)(2,1)} %bitcast.57), kind=kOutput, calls=%fused_computation.3.clone.1 | convolution fusion | flops 1126168576 | bytes 29761536 | tf_op jit(solution)/shard_map/while/body/eval_jaxpr/hdq,hdk->hqk/dot_general | solution.py:69
  57.4 0.0 copy-start.1
  57.4 12.0 %fusion.63 = f32[2,1024]{1,0:T(2,128)S(1)} fusion(f32[2,1024,3072]{2,1,0:T(8,128)} %get-tuple-element.155, f32[2,1024]{1,0:T(2,128)S(1)} %get-tuple-element.156, pred[1024,3072]{1,0:T(8,128)(4,1)S(1)} %broadcast_compare_fusion.2), kind=kLoop, calls=%fused_computation.4.clone.1 | loop fusion | flops 25163776 | bytes 28327936 | tf_op jit(solution)/shard_map/while/body/eval_jaxpr/reduce_sum | solution.py:76
  69.4 0.0 copy-done.1
  69.4 11.8 %fusion.64 = bf16[2,88,1024]{2,1,0:T(8,128)(2,1)S(1)} fusion(bf16[2,88,3072]{2,1,0:T(8,128)(2,1)S(1)} %bitcast.56, f32[2,1024,3072]{2,1,0:T(8,128)} %get-tuple-element.155, f32[2,1024]{1,0:T(2,128)S(1)} %get-tuple-element.156, pred[1024,3072]{1,0:T(8,128)(4,1)S(1)} %broadcast_compare_fusion.2, f32[2,1024]{1,0:T(2,128)S(1)} %fusion.63), kind=kOutput, calls=%fused_computation.10.clone.1 | convolution fusion | flops 1132822528 | bytes 29769728 | tf_op jit(solution)/shard_map/while/body/eval_jaxpr/hqk,hdk->hdq/dot_general | solution.py:78
  81.3 0.8 bitcast_dynamic-update-slice_fusion.2
  82.0 0.7 dynamic_slice.44
  83.4 2.0 broadcast_compare_fusion.2
  85.4 2.1 fusion.61
  87.5 1.6 constant_dynamic-slice_fusion.5
  89.2 1.2 slice.41
  90.4 12.6 %fusion.62 = (f32[2,1024]{1,0:T(2,128)S(1)}, f32[2,1024,3072]{2,1,0:T(8,128)}) fusion(pred[1024,3072]{1,0:T(8,128)(4,1)S(1)} %broadcast_compare_fusion.2, bf16[2,88,1024]{2,1,0:T(8,128)(2,1)S(1)} %bitcast.59, bf16[2,88,3072]{2,1,0:T(8,128)(2,1)} %bitcast.57), kind=kOutput, calls=%fused_computation.3.clone.1 | convolution fusion | flops 1126168576 | bytes 29761536 | tf_op jit(solution)/shard_map/while/body/eval_jaxpr/hdq,hdk->hqk/dot_general | solution.py:69
  103.0 12.0 %fusion.63 = f32[2,1024]{1,0:T(2,128)S(1)} fusion(f32[2,1024,3072]{2,1,0:T(8,128)} %get-tuple-element.155, f32[2,1024]{1,0:T(2,128)S(1)} %get-tuple-element.156, pred[1024,3072]{1,0:T(8,128)(4,1)S(1)} %broadcast_compare_fusion.2), kind=kLoop, calls=%fused_computation.4.clone.1 | loop fusion | flops 25163776 | bytes 28327936 | tf_op jit(solution)/shard_map/while/body/eval_jaxpr/reduce_sum | solution.py:76
  115.0 0.0 copy-done.1
  115.0 11.8 %fusion.64 = bf16[2,88,1024]{2,1,0:T(8,128)(2,1)S(1)} fusion(bf16[2,88,3072]{2,1,0:T(8,128)(2,1)S(1)} %bitcast.56, f32[2,1024,3072]{2,1,0:T(8,128)} %get-tuple-element.155, f32[2,1024]{1,0:T(2,128)S(1)} %get-tuple-element.156, pred[1024,3072]{1,0:T(8,128)(4,1)S(1)} %broadcast_compare_fusion.2, f32[2,1024]{1,0:T(2,128)S(1)} %fusion.63), kind=kOutput, calls=%fused_computation.10.clone.1 | convolution fusion | flops 1132822528 | bytes 29769728 | tf_op jit(solution)/shard_map/while/body/eval_jaxpr/hqk,hdk->hdq/dot_general | solution.py:78
  126.9 0.8 bitcast_dynamic-update-slice_fusion.2
  127.7 1.2 copy.36
  128.8 7.1 %fusion.38 = f32[1408,2048]{1,0:T(8,128)} fusion(bf16[176,2048]{1,0:T(8,128)(2,1)S(1)} %bitcast.61, bf16[1408,1408]{1,0:T(8,128)(2,1)} %param.11, s32[]{:T(128)S(6)} %select_n.41), kind=kOutput, calls=%fused_computation.34 | convolution fusion | flops 1015021568 | bytes 12750852 | tf_op jit(solution)/shard_map/dot_general | solution.py:87
  135.9 0.0 reduce-scatter.2.cloned.1.call-update
  135.9 0.2 all-gather.4.cloned.1.call-start
  136.2 70.0 %reduce-scatter.2.cloned.1.call-done = f32[176,2048]{1,0:T(8,128)} async-done(((f32[1408,2048]{1,0:T(8,128)}), f32[176,2048]{1,0:T(8,128)}) %reduce-scatter.2.cloned.1.call-update) | async-done | bytes 1441808 | tf_op jit(solution)/shard_map/reduce_scatter | solution.py:90
  206.2 0.0 copy-done.2
  206.2 2.4 add_convert_fusion
  208.6 0.0 all-gather.4.cloned.1.call-update
  208.6 0.0 copy-start.3
  208.6 0.0 all-gather.6.cloned.1.call-start
  208.7 38.4 %all-gather.4.cloned.1.call-done = bf16[1408,2048]{1,0:T(8,128)(2,1)} async-done(((bf16[176,2048]{1,0:T(8,128)(2,1)}), bf16[1408,2048]{1,0:T(8,128)(2,1)}) %all-gather.4.cloned.1.call-update) | async-done | bytes 5767184 | tf_op jit(solution)/shard_map/all_gather | solution.py:92
  247.1 3.7 convert_reduce_fusion
  250.8 0.6 copy-done
  251.4 1.5 fusion.16
  252.9 0.0 copy-done.3
  253.0 4.3 %fusion.18 = bf16[1408,2048]{1,0:T(8,128)(2,1)} fusion(bf16[1408,2048]{1,0:T(8,128)(2,1)S(1)} %copy-done, f32[1408]{0:T(1024)S(1)} %copy-done.3, f32[2048]{0:T(1024)S(1)} %add_rsqrt_fusion, f32[2048]{0:T(1024)S(1)} %broadcast_multiply_fusion), kind=kLoop, calls=%fused_computation.23 | loop fusion | flops 14417920 | bytes 11556352 | tf_op jit(solution)/shard_map/convert_element_type | solution.py:96
  257.2 8.4 %copy.30 = bf16[1408,2048]{0,1:T(8,128)(2,1)} copy(bf16[1408,2048]{1,0:T(8,128)(2,1)} %fusion.18) | data formatting | bytes 11534336 | tf_op jit(solution)/shard_map/convert_element_type | solution.py:96
  265.6 10.6 %reshape.116 = bf16[1408,512,4]{0,2,1:T(4,128)(2,1)} reshape(bf16[1408,2048]{0,1:T(8,128)(2,1)} %copy.30) | data formatting | bytes 11534336 | tf_op jit(solution)/shard_map/reshape | solution.py:100
  276.2 0.0 copy-done.6
  276.2 5.4 %fusion.33 = bf16[176,512]{1,0:T(8,128)(2,1)} fusion(bf16[1408,512,4]{0,2,1:T(4,128)(2,1)} %reshape.116, bf16[22,4,8,1408]{3,2,1,0:T(8,128)(2,1)S(1)} %bitcast.67), kind=kOutput, calls=%fused_computation.32 | convolution fusion | flops 1015111680 | bytes 7929856 | tf_op jit(solution)/shard_map/ojf,fgj->og/dot_general | solution.py:102
  281.6 0.0 all-gather.6.cloned.1.call-update
  281.7 0.0 copy-done.4
  281.7 23.5 %all-gather = s32[16,1,512]{2,1,0:T(1,128)S(1)} all-gather(s32[1,1,512]{2,1,0:T(1,128)S(1)} %bitcast.65), channel_id=1, replica_groups=mesh['row'=16,'col'=8] {'row'}, dimensions={0}, use_global_device_ids=true | all-gather | bytes 34816 | tf_op jit(solution)/shard_map/all_gather | solution.py:108
  305.2 28.1 %all-gather.6.cloned.1.call-done = bf16[176,8192]{1,0:T(8,128)(2,1)} async-done(((bf16[176,512]{1,0:T(8,128)(2,1)}), bf16[176,8192]{1,0:T(8,128)(2,1)}) %all-gather.6.cloned.1.call-update) | async-done | bytes 2883600 | tf_op jit(solution)/shard_map/all_gather | solution.py:107
  333.3 5.8 %copy.33 = bf16[8192,176]{1,0:T(8,128)(2,1)} copy(bf16[8192,176]{0,1:T(8,128)(2,1)} %bitcast.60) | data formatting | bytes 5767168 | tf_op jit(solution)/shard_map/all_gather | solution.py:107
  339.1 35.2 %scatter_custom_fusion = bf16[176,512]{0,1:T(8,128)(2,1)S(1)} fusion(s32[8192]{0:T(1024)S(1)} %compare_select_fusion, bf16[8192,176]{1,0:T(8,128)(2,1)} %copy.33, bf16[]{:T(256)} %constant.97.clone.1), kind=kCustom, calls=%fused_computation.36 | custom fusion | bytes 180736 | tf_op jit(solution)/shard_map/scatter | solution.py:112
  374.3 0.8 copy.34
  (19 shorter events, 0.2 us)
Async XLA Ops:
  7.2 26.2 %slice-start = ((bf16[3,176,2048]{2,1,0:T(8,128)(2,1)}), bf16[2,176,2048]{2,1,0:T(8,128)(2,1)S(1)}, s32[]{:S(2)}) async-start(bf16[3,176,2048]{2,1,0:T(8,128)(2,1)} %param.9), calls=%async_computation.4 | async-start | bytes 2883584 | tf_op jit(solution)/shard_map/slice | solution.py:49
  7.2 7.8 %copy-start.5 = (s32[64]{0:T(128)S(1)}, s32[64]{0:T(128)}, u32[]{:S(2)}) copy-start(s32[64]{0:T(128)} %param.14) | copy-start | bytes 772
  7.2 199.0 %reduce-scatter.2.cloned.1.call-start = ((), (), s32[]{:S(2)}) async-start(), calls=%async_computation.1 | async-start | bytes 12976128 | tf_op jit(solution)/shard_map/reduce_scatter | solution.py:90
  9.7 19.6 %collective-permute-start = (bf16[2,176,1024]{2,1,0:T(8,128)(2,1)}, bf16[2,176,1024]{2,1,0:T(8,128)(2,1)S(1)}, u32[]{:S(2)}, u32[]{:S(2)}) collective-permute-start(bf16[2,176,1024]{2,1,0:T(8,128)(2,1)} %get-tuple-element.106), channel_id=1, source_target_pairs={{0,8},{8,16},{16,24},{24,32},{32,40},{40,48},{48,56},{56,64},{64,7... | collective-permute-start | bytes 2162696 | tf_op jit(solution)/shard_map/ppermute | solution.py:19
  13.6 19.7 %collective-permute-start.1 = (bf16[2,176,1024]{2,1,0:T(8,128)(2,1)S(1)}, bf16[2,176,1024]{2,1,0:T(8,128)(2,1)}, u32[]{:S(2)}, u32[]{:S(2)}) collective-permute-start(bf16[2,176,1024]{2,1,0:T(8,128)(2,1)S(1)} %get-tuple-element.107), channel_id=1, source_target_pairs={{8,0},{16,8},{24,16},{32,24},{40,32},{48,40},{56,48},{64,56},{72,6... | collective-permute-start | bytes 2162696 | tf_op jit(solution)/shard_map/ppermute | solution.py:21
  57.4 12.0 %copy-start.1 = (bf16[1,176,3072]{2,1,0:T(8,128)(2,1)S(1)}, bf16[1,176,3072]{2,1,0:T(8,128)(2,1)}, u32[]{:S(2)}) copy-start(bf16[1,176,3072]{2,1,0:T(8,128)(2,1)} %get-tuple-element.153) | copy-start | bytes 3244036 | tf_op jit(solution)/shard_map/while
  103.0 12.0 %copy-start.1 = (bf16[1,176,3072]{2,1,0:T(8,128)(2,1)S(1)}, bf16[1,176,3072]{2,1,0:T(8,128)(2,1)}, u32[]{:S(2)}) copy-start(bf16[1,176,3072]{2,1,0:T(8,128)(2,1)} %get-tuple-element.153) | copy-start | bytes 3244036 | tf_op jit(solution)/shard_map/while
  135.9 70.3 %copy-start.2 = (bf16[176,2048]{1,0:T(8,128)(2,1)S(1)}, bf16[176,2048]{1,0:T(8,128)(2,1)}, u32[]{:S(2)}) copy-start(bf16[176,2048]{1,0:T(8,128)(2,1)} %param.10) | copy-start | bytes 2162692
  135.9 111.1 %all-gather.4.cloned.1.call-start = ((), (), s32[]{:S(2)}) async-start(), calls=%async_computation.2 | async-start | bytes 6488064 | tf_op jit(solution)/shard_map/all_gather | solution.py:92
  208.6 44.3 %copy-start.3 = (f32[1408]{0:T(1024)S(1)}, f32[1408]{0:T(1024)}, u32[]{:S(2)}) copy-start(f32[1408]{0:T(1024)} %param.13) | copy-start | bytes 16900
  208.6 124.7 %all-gather.6.cloned.1.call-start = ((), (), s32[]{:S(2)}) async-start(), calls=%async_computation.3 | async-start | bytes 3063808 | tf_op jit(solution)/shard_map/all_gather | solution.py:107
  247.1 4.3 %copy-start = (bf16[1408,2048]{1,0:T(8,128)(2,1)S(1)}, bf16[1408,2048]{1,0:T(8,128)(2,1)}, u32[]{:S(2)}) copy-start(bf16[1408,2048]{1,0:T(8,128)(2,1)} %all-gather.4.cloned.1.call-done) | copy-start | bytes 17301508
  265.6 10.7 %copy-start.6 = (bf16[176,5632]{1,0:T(8,128)(2,1)S(1)}, bf16[176,5632]{1,0:T(8,128)(2,1)}, u32[]{:S(2)}) copy-start(bf16[176,5632]{1,0:T(8,128)(2,1)} %param.12) | copy-start | bytes 5947396
  276.2 5.4 %copy-start.4 = (s32[512]{0:T(512)S(1)}, s32[512]{0:T(512)}, u32[]{:S(2)}) copy-start(s32[512]{0:T(512)} %param.15) | copy-start | bytes 6148
Sparse Core Ops, SparseCore 0:
  136.1 70.0 reduce-scatter.1
  208.7 38.2 all-gather.3
  281.8 51.4 all-gather.5
where the time goes:
time: 383 us; the launch traced here: 382 us
  waiting for transfers between devices  154 us (40%)
  local copies, waits for them, and re-layouts  77.9 us (20%)
  matrix products  61.4 us (16%)
  other arithmetic  43.4 us (11%)
  blocking collectives  23.5 us (6%)
  between operations  13.9 us (4%)
  starting transfers between devices  5.53 us (1%)
    reduce_scatter x1, waiting for transfers between devices, body(): lax.psum_scatter(partial_value, 'col', scatter_dimension=0, tiled=True)  70 us
    all_gather x1, waiting for transfers between devices, body(): full_rows = lax.all_gather(layer_out, 'col', axis=0, tiled=True)  38.4 us
    scatter x1, local copies, waits for them, and re-layouts, body(): image_rows = empty_rows.at[:, slot_index].set(every_row, mode='drop')  35.2 us
    all_gather x1, waiting for transfers between devices, body(): lax.all_gather(merged, 'row', axis=1, tiled=True)  28.1 us
    dot_general x2, matrix products, attend(): jnp.einsum('hdq,hdk->hqk', queries, key_block, preferred_element_type=jnp...  25.3 us
    reduce_sum x2, other arithmetic, attend(): totals = jnp.sum(exponent, axis=2)  24 us
    dot_general x2, matrix products, attend(): jnp.einsum('hqk,hdk->hdq', weights, value_block, preferred_element_type=j...  23.7 us
    all_gather x1, blocking collectives, body(): lax.all_gather(dest_row, 'row', axis=0, tiled=True)  23.5 us
  transfers between devices with their start and end apart: 5, of which 5 were waited for; matrix products, arithmetic and copies ran while one was open for 0% of the time, Pallas kernels for 0%

commit v1 on v0

v1 whole, which is shorter than its diff:
```python
import functools
import math

import jax
import jax.numpy as jnp
from jax import lax
from jax.experimental import pallas as pl
from jax.experimental.pallas import tpu as pltpu
from jax.sharding import PartitionSpec as P

HEAD_DIM = 88
QB = 256
KB = 256
STEP = 128
NEG = -1e30


def tile_step(kt, v0, v1, qcat, ok, coef, row, m_ref, l_ref, acc_ref):
    scores = lax.dot_general(
        kt, qcat, (((1,), (0,)), ((), ())), preferred_element_type=jnp.float32
    )
    width = qcat.shape[1] // 2
    for head in range(2):
        part = jnp.where(ok, scores[:, head * width : (head + 1) * width], NEG)
        old = m_ref[row + head]
        new = jnp.maximum(old, jnp.max(part, axis=0, keepdims=True))
        fade = jnp.exp2((old - new) * coef)
        expo = jnp.exp2(part * coef - new * coef)
        l_ref[row + head] = l_ref[row + head] * fade + jnp.sum(expo, axis=0, keepdims=True)
        m_ref[row + head] = new
        values = v1 if head else v0
        acc_ref[row + head] = acc_ref[row + head] * fade + lax.dot_general(
            values,
            expo.astype(jnp.bfloat16),
            (((1,), (0,)), ((), ())),
            preferred_element_type=jnp.float32,
        )


def stage_keys(k_src, v_src, kt_ref, v_ref, count, offset):
    def one(i, carry):
        at = pl.multiple_of(i * 256, 256)
        to = pl.multiple_of(offset + i * 256, 256)
        kt_ref[pl.ds(to, 256), :] = jnp.transpose(k_src[:, pl.ds(at, 256)])
        values = v_src[:, pl.ds(at, 256)].astype(jnp.float32)
        v_ref[0, :, pl.ds(to, 256)] = values[:HEAD_DIM].astype(jnp.bfloat16)
        v_ref[1, :, pl.ds(to, 256)] = values[HEAD_DIM:].astype(jnp.bfloat16)
        return carry

    lax.fori_loop(0, count, one, 0)


def query_pair(q_ref, at):
    block = q_ref[:, pl.ds(at, QB)]
    feature = lax.broadcasted_iota(jnp.int32, block.shape, 0)
    zero = jnp.zeros_like(block)
    return jnp.concatenate(
        [jnp.where(feature < HEAD_DIM, block, zero), jnp.where(feature < HEAD_DIM, zero, block)],
        axis=1,
    )


def local_kernel(coef, lo_ref, n_ref, qkv_ref, start_ref, len_ref, m_ref, l_ref, acc_ref, kt, vt):
    blocks = qkv_ref.shape[2] // QB
    stage_keys(qkv_ref.at[1], qkv_ref.at[2], kt, vt, qkv_ref.shape[2] // 256, 0)

    def per_block(b, carry):
        at = pl.multiple_of(b * QB, QB)
        qcat = query_pair(qkv_ref.at[0], at)
        start = start_ref[0:1, pl.ds(at, QB)]
        length = len_ref[0:1, pl.ds(at, QB)]
        row = b * 2
        for head in range(2):
            m_ref[row + head] = jnp.full((1, QB), NEG, jnp.float32)
            l_ref[row + head] = jnp.zeros((1, QB), jnp.float32)
            acc_ref[row + head] = jnp.zeros((HEAD_DIM, QB), jnp.float32)

        def per_tile(t, inner):
            key = pl.multiple_of(lo_ref[b] * STEP + t * KB, STEP)
            place = lax.broadcasted_iota(jnp.int32, (KB, QB), 0) + (key - start)
            ok = (place >= 0) & (place < length)
            tile_step(
                kt[pl.ds(key, KB), :],
                vt[0, :, pl.ds(key, KB)],
                vt[1, :, pl.ds(key, KB)],
                qcat,
                ok,
                coef,
                row,
                m_ref,
                l_ref,
                acc_ref,
            )
            return inner

        lax.fori_loop(0, n_ref[b], per_tile, 0)
        return carry

    lax.fori_loop(0, blocks, per_block, 0)


def halo_kernel(
    coef,
    first_ref,
    n_ref,
    qkv_ref,
    left_ref,
    right_ref,
    start_ref,
    len_ref,
    m_in,
    l_in,
    acc_in,
    out_ref,
    kt,
    vt,
    m_ref,
    l_ref,
    acc_ref,
):
    reach = left_ref.shape[2]
    tokens = qkv_ref.shape[2]
    blocks = tokens // QB
    stage_keys(left_ref.at[0], left_ref.at[1], kt, vt, reach // 256, 0)
    stage_keys(right_ref.at[0], right_ref.at[1], kt, vt, reach // 256, reach)

    def per_block(b, carry):
        at = pl.multiple_of(b * QB, QB)
        start = start_ref[0:1, pl.ds(at, QB)]
        length = len_ref[0:1, pl.ds(at, QB)]
        row = b * 2
        for head in range(2):
            m_ref[head] = m_in[row + head]
            l_ref[head] = l_in[row + head]
            acc_ref[head] = acc_in[row + head]
        for side in range(2):
            shift = tokens if side else -reach
            base = side * reach

            @pl.when(n_ref[side * blocks + b] > 0)
            def _():
                qcat = query_pair(qkv_ref.at[0], at)

                def per_tile(t, inner):
                    key = pl.multiple_of(first_ref[side * blocks + b] * STEP + t * KB, STEP)
                    place = lax.broadcasted_iota(jnp.int32, (KB, QB), 0) + (key + shift - start)
                    ok = (place >= 0) & (place < length)
                    slot = pl.multiple_of(key + base, STEP)
                    tile_step(
                        kt[pl.ds(slot, KB), :],
                        vt[0, :, pl.ds(slot, KB)],
                        vt[1, :, pl.ds(slot, KB)],
                        qcat,
                        ok,
                        coef,
                        0,
                        m_ref,
                        l_ref,
                        acc_ref,
                    )
                    return inner

                lax.fori_loop(0, n_ref[side * blocks + b], per_tile, 0)

        both = [acc_ref[head] / l_ref[head] for head in range(2)]
        out_ref[:, pl.ds(at, QB)] = jnp.concatenate(both, axis=0).astype(jnp.bfloat16)
        return carry

    lax.fori_loop(0, blocks, per_block, 0)


def attention(qkv, left, right, image_groups, row_id, all_tokens):
    _, width, tokens = qkv.shape
    reach = left.shape[2]
    blocks = tokens // QB
    coef = math.log2(math.e) / math.sqrt(HEAD_DIM)
    ends = jnp.cumsum(image_groups) * 4
    begins = ends - image_groups * 4
    position = row_id * tokens + jnp.arange(tokens, dtype=jnp.int32)
    mine = (position[:, None] >= begins[None, :]) & (position[:, None] < ends[None, :])
    start = jnp.sum(jnp.where(mine, begins[None, :], 0), axis=1) - row_id * tokens
    length = jnp.sum(jnp.where(mine, (image_groups * 4)[None, :], 0), axis=1)
    first = start[::QB]
    last = (start + length)[QB - 1 :: QB]

    def tiles(low, high, extent):
        low_step = low // STEP
        count = jnp.maximum(-((low_step * STEP - high) // KB), 0)
        low_step = jnp.clip(low_step, 0, extent // STEP - count * (KB // STEP))
        return low_step, jnp.where(high > low, count, 0)

    local_lo, local_n = tiles(jnp.maximum(first, 0), jnp.minimum(last, tokens), tokens)
    left_lo, left_n = tiles(
        jnp.clip(first + reach, 0, reach), jnp.full_like(first, reach), reach
    )
    right_lo, right_n = tiles(jnp.zeros_like(first), jnp.clip(last - tokens, 0, reach), reach)
    halo_lo = jnp.concatenate([left_lo, right_lo])
    halo_n = jnp.concatenate([left_n, right_n])
    start2, length2 = start[None, :], length[None, :]
    smem = pl.BlockSpec(memory_space=pltpu.SMEM)
    vmem = pl.BlockSpec(memory_space=pltpu.VMEM)
    stat = jax.ShapeDtypeStruct((2 * blocks, 1, QB), jnp.float32)
    m, l, acc = pl.pallas_call(
        functools.partial(local_kernel, coef),
        out_shape=(stat, stat, jax.ShapeDtypeStruct((2 * blocks, HEAD_DIM, QB), jnp.float32)),
        in_specs=[smem, smem, vmem, vmem, vmem],
        out_specs=(vmem, vmem, vmem),
        scratch_shapes=[
            pltpu.VMEM((tokens, width), jnp.bfloat16),
            pltpu.VMEM((2, HEAD_DIM, tokens), jnp.bfloat16),
        ],
        compiler_params=pltpu.CompilerParams(vmem_limit_bytes=32 << 20),
        cost_estimate=pl.CostEstimate(
            flops=4 * width * tokens * 1200, bytes_accessed=8 << 20, transcendentals=2 * tokens * 1200
        ),
    )(local_lo, local_n, qkv, start2, length2)
    return pl.pallas_call(
        functools.partial(halo_kernel, coef),
        out_shape=jax.ShapeDtypeStruct((width, tokens), jnp.bfloat16),
        in_specs=[smem, smem] + [vmem] * 8,
        out_specs=vmem,
        scratch_shapes=[
            pltpu.VMEM((2 * reach, width), jnp.bfloat16),
            pltpu.VMEM((2, HEAD_DIM, 2 * reach), jnp.bfloat16),
            pltpu.VMEM((2, 1, QB), jnp.float32),
            pltpu.VMEM((2, 1, QB), jnp.float32),
            pltpu.VMEM((2, HEAD_DIM, QB), jnp.float32),
        ],
        compiler_params=pltpu.CompilerParams(vmem_limit_bytes=32 << 20),
        cost_estimate=pl.CostEstimate(
            flops=4 * width * tokens * 300, bytes_accessed=8 << 20, transcendentals=2 * tokens * 300
        ),
    )(halo_lo, halo_n, qkv, left, right, start2, length2, m, l, acc)


def body(qkv, residual_in, out_weight, merge_weight, merge_gain, image_groups, dest_row):
    width_here = qkv.shape[1]
    tok_rows = qkv.shape[2]
    full_width = out_weight.shape[0]
    reach = tok_rows // 2
    rows = lax.axis_size("row")
    cols = lax.axis_size("col")
    row_id = lax.axis_index("row")
    all_tokens = tok_rows * rows
    chunk = tok_rows // cols
    group_rows = tok_rows // 4
    share = group_rows // rows

    left = lax.ppermute(
        qkv[1:, :, tok_rows - reach :], "row", [(i, i + 1) for i in range(rows - 1)]
    )
    right = lax.ppermute(qkv[1:, :, :reach], "row", [(i + 1, i) for i in range(rows - 1)])
    residual = lax.all_to_all(residual_in, "col", 1, 0, tiled=True)

    owner = dest_row // group_rows
    ids = jnp.arange(group_rows, dtype=jnp.int32)
    earlier = (owner[None, :] == owner[:, None]) & (ids[None, :] < ids[:, None])
    spot = owner * share + jnp.sum(earlier.astype(jnp.int32), axis=1)
    slots = jnp.arange(group_rows, dtype=jnp.int32)
    picked = spot[:, None] == slots[None, :]
    sent_dest = jnp.sum(jnp.where(picked, (dest_row % group_rows)[:, None], 0), axis=0)
    got_dest = lax.all_to_all(sent_dest, "row", 0, 0, tiled=True)
    placed = (got_dest[:, None] == slots[None, :]).astype(jnp.bfloat16)
    picked = picked.astype(jnp.bfloat16)

    attended = attention(qkv, left, right, image_groups, row_id, all_tokens)
    attended = lax.all_to_all(attended, "col", 1, 0, tiled=True)
    projected = lax.dot_general(
        out_weight, attended, (((0,), (0,)), ((), ())), preferred_element_type=jnp.float32
    )
    layer_rows = (residual.astype(jnp.float32) + projected).astype(jnp.bfloat16)
    layer_out = lax.all_to_all(layer_rows, "col", 0, 1, tiled=True)
    values32 = layer_rows.astype(jnp.float32)
    centre = jnp.mean(values32, axis=0, keepdims=True)
    spread = jnp.mean(jnp.square(values32 - centre), axis=0, keepdims=True)
    normed = ((values32 - centre) * lax.rsqrt(spread + 1e-06) * merge_gain[:, None]).astype(
        jnp.bfloat16
    )
    t = jnp.arange(chunk, dtype=jnp.int32)
    order = ((t % 4) * (chunk // 4) + t // 4)[:, None] == t[None, :]
    by_part = jnp.dot(normed, order.astype(jnp.bfloat16)).astype(jnp.bfloat16)
    by_part = by_part.reshape(full_width, 4, chunk // 4).transpose(1, 0, 2)
    gathered = lax.all_gather(by_part, "col", axis=2, tiled=True)
    parts = merge_weight.reshape(width_here, 4, full_width)
    merged = sum(
        jnp.dot(parts[:, j], gathered[j], preferred_element_type=jnp.float32) for j in range(4)
    ).astype(jnp.bfloat16)
    sorted_rows = lax.dot_general(
        picked, merged, (((0,), (1,)), ((), ())), preferred_element_type=jnp.float32
    ).astype(jnp.bfloat16)
    got_rows = lax.all_to_all(sorted_rows, "row", 0, 0, tiled=True)
    image_rows = lax.dot_general(
        got_rows, placed, (((0,), (0,)), ((), ())), preferred_element_type=jnp.float32
    ).astype(jnp.bfloat16)
    return (layer_out, image_rows)


def solution(mesh):
    return jax.shard_map(
        body,
        mesh=mesh,
        in_specs=(P(None, "col", "row"), P("col", "row"), P(), P("col", None), P(), P(), P("row")),
        out_specs=(P("col", "row"), P("col", "row")),
        check_vma=False,
    )
```

time: 383 us -> 153 us (0.40)
  waiting for transfers between devices: 154 us -> 43.4 us
  local copies, waits for them, and re-layouts: 77.9 us -> 17.3 us
  matrix products: 61.4 us -> 14.7 us
  other arithmetic: 43.4 us -> 3.37 us
  starting transfers between devices: 5.53 us -> 38.5 us
  blocking collectives: 23.5 us -> 0 us
  Pallas kernels: 0 us -> 20.2 us
    reduce_scatter x1 -> x0, waiting for transfers between devices: 70 us -> none  [body(): lax.psum_scatter(partial_value, 'col', scatter_dimension=0, tiled=True)]
    dot_general x6 -> x7, matrix products: 61.4 us -> 14.7 us  [the longest x3 6.12 us: body(): jnp.dot(parts[:, j], gathered[j], preferred_element_type=jnp.float32)]
    all_gather x2 -> x1, waiting for transfers between devices: 66.5 us -> 21.1 us  [body(): gathered = lax.all_gather(by_part, 'col', axis=2, tiled=True)]
    scatter x1 -> x0, local copies, waits for them, and re-layouts: 35.2 us -> none  [body(): image_rows = empty_rows.at[:, slot_index].set(every_row, mode='drop')]
    all_to_all x0 -> x5, starting transfers between devices: none -> 33.3 us  [the longest x1 13.3 us: body(): got_dest = lax.all_to_all(sent_dest, 'row', 0, 0, tiled=True)]
    reduce_sum x4 -> x3, other arithmetic: 27.9 us -> 0.68 us  [the longest x1 0.25 us: body(): spot = owner * share + jnp.sum(earlier.astype(jnp.int32), axis=1)]
    all_gather x1 -> x0, blocking collectives: 23.5 us -> none  [body(): lax.all_gather(dest_row, 'row', axis=0, tiled=True)]
    all_to_all x0 -> x5, waiting for transfers between devices: none -> 22.3 us  [the longest x1 10.8 us: body(): attended = lax.all_to_all(attended, 'col', 1, 0, tiled=True)]
  transfers between devices with their start and end apart: 5 -> 8, of which waited for: 5 -> 4; matrix products, arithmetic and copies ran while one was open for 0% -> 17% of each run, Pallas kernels for 0% -> 13%
where the time goes in v1:
time: 153 us; the launch traced here: 152 us
  waiting for transfers between devices  43.4 us (28%)
  starting transfers between devices  38.5 us (25%)
  Pallas kernels  20.2 us (13%)
  local copies, waits for them, and re-layouts  17.3 us (11%)
  matrix products  14.7 us (10%)
  between operations  14.4 us (9%)
  other arithmetic  3.37 us (2%)
    all_gather x1, waiting for transfers between devices, body(): gathered = lax.all_gather(by_part, 'col', axis=2, tiled=True)  21.1 us
    pallas_call x1, Pallas kernels, attention(): pl.pallas_call(functools.partial(local_kernel, coef), out_shape=(stat, st...  15 us
    all_to_all x1, starting transfers between devices, body(): got_dest = lax.all_to_all(sent_dest, 'row', 0, 0, tiled=True)  13.3 us
    all_to_all x1, waiting for transfers between devices, body(): attended = lax.all_to_all(attended, 'col', 1, 0, tiled=True)  10.8 us
    all_to_all x1, starting transfers between devices, body(): got_rows = lax.all_to_all(sorted_rows, 'row', 0, 0, tiled=True)  6.94 us
    all_to_all x1, waiting for transfers between devices, body(): got_rows = lax.all_to_all(sorted_rows, 'row', 0, 0, tiled=True)  6.31 us
    dot_general x3, matrix products, body(): jnp.dot(parts[:, j], gathered[j], preferred_element_type=jnp.float32)  6.12 us
    pallas_call x1, Pallas kernels, attention(): pl.pallas_call(functools.partial(halo_kernel, coef), out_shape=jax.ShapeD...  5.25 us
  transfers between devices with their start and end apart: 8, of which 4 were waited for; matrix products, arithmetic and copies ran while one was open for 17% of the time, Pallas kernels for 13%

profile of v1, /device:TPU:0, one launch (start us, length us, event | category | flops | bytes accessed | tf_op | source)
XLA Modules:
  0.0 151.9 jit_solution(14545480277189202599)
XLA Ops:
  7.2 0.0 copy-start.5
  7.2 2.6 %fusion.41 = (bf16[2,176,1024]{2,1,0:T(8,128)(2,1)}, bf16[2,176,1024]{2,1,0:T(8,128)(2,1)}) fusion(bf16[3,176,2048]{2,1,0:T(8,128)(2,1)} %qkv_ref.3), kind=kLoop, calls=%fused_computation.107 | loop fusion | bytes 2883584 | tf_op jit(solution)/shard_map/slice | solution.py:252
  9.8 3.9 %collective-permute-start = (bf16[2,176,1024]{2,1,0:T(8,128)(2,1)}, bf16[2,176,1024]{2,1,0:T(8,128)(2,1)S(1)}, u32[]{:S(2)}, u32[]{:S(2)}) collective-permute-start(bf16[2,176,1024]{2,1,0:T(8,128)(2,1)} %get-tuple-element.21), channel_id=1, source_target_pairs={{0,8},{8,16},{16,24},{24,32},{32,40},{40,48},{48,56},{56,64},{64,7... | collective-permute-start | bytes 2162696 | tf_op jit(solution)/shard_map/ppermute | solution.py:249
  13.8 1.3 collective-permute-start.1
  15.1 0.0 copy-done.5
  15.1 0.0 copy-start.6
  15.1 0.0 copy-start
  15.1 0.9 copy.67
  16.0 4.5 %all-to-all-start = ((bf16[176,8,256]{2,0,1:T(8,128)(2,1)}), bf16[176,8,256]{2,0,1:T(8,128)(2,1)}, u32[]{:S(2)}, u32[]{:S(2)}) async-start(bf16[176,8,256]{2,0,1:T(8,128)(2,1)} %bitcast.78), calls=%async_computation | async-start | bytes 1441792 | tf_op jit(solution)/shard_map/all_to_all | solution.py:253
  20.5 0.0 copy-done.6
  20.5 0.1 copy.33
  20.6 0.1 reduce-window.7
  20.7 0.1 multiply_reduce_fusion
  20.8 0.2 select_reduce_fusion.1
  21.0 0.1 slice.36
  21.1 0.1 slice.37
  21.3 0.1 pad_add_fusion.first_ref
  21.4 0.1 pad_add_fusion.1.n_ref
  21.4 0.0 copy-done
  21.4 15.0 %shard_map.86 = (f32[16,1,256]{2,1,0:T(1,128)S(1)}, f32[16,1,256]{2,1,0:T(1,128)S(1)}, f32[16,88,256]{2,1,0:T(8,128)S(1)}) custom-call(s32[8]{0:T(128)S(1)} %maximum_minimum_fusion.lo_ref, s32[8]{0:T(128)S(1)} %get-tuple-element.10.n_ref, bf16[3,176,2048]{2,1,0:T(8,128)(2,1)S(1)} %copy-done, s32[1,2048]{1,0:T(1,128)S(1)} %bitcast.75, s32[1,2048]{1,0:T(1,128)S(1)} %bitcast.73), custom_call_target="tpu_custom_call" | custom-call | flops 1730150400 | bytes 8388608 | tf_op jit(solution)/shard_map/pallas_call | solution.py:203
  36.4 0.0 collective-permute-done.left_ref
  36.4 0.0 collective-permute-done.1.right_ref
  36.4 5.2 %shard_map.87 = bf16[176,2048]{1,0:T(8,128)(2,1)S(1)} custom-call(s32[16]{0:T(128)S(1)} %pad_add_fusion.first_ref, s32[16]{0:T(128)S(1)} %pad_add_fusion.1.n_ref, bf16[3,176,2048]{2,1,0:T(8,128)(2,1)S(1)} %copy-done, bf16[2,176,1024]{2,1,0:T(8,128)(2,1)S(1)} %collective-permute-done.left_ref, bf16[2,176,1024]{2,1,0:T(8,128)(2,1)} %collective-permute-done.1.right_ref, ...), custom_call_target="tpu_custom_call" | custom-call | flops 432537600 | bytes 8388608 | tf_op jit(solution)/shard_map/pallas_call | solution.py:217
  41.7 0.9 copy.66
  42.6 0.0 all-to-all-done
  42.6 4.8 %all-to-all-start.1 = ((bf16[176,8,256]{2,0,1:T(8,128)(2,1)}), bf16[176,8,256]{2,0,1:T(8,128)(2,1)}, u32[]{:S(2)}, u32[]{:S(2)}) async-start(bf16[176,8,256]{2,0,1:T(8,128)(2,1)} %bitcast.70), calls=%async_computation.1 | async-start | bytes 1441792 | tf_op jit(solution)/shard_map/all_to_all | solution.py:267
  47.4 0.0 all-gather.2.cloned.1.call-start
  47.5 1.2 convert_element_type.45
  48.7 0.4 copy.35
  49.1 10.8 %all-to-all-done.1 = bf16[176,8,256]{2,0,1:T(8,128)(2,1)} async-done(((bf16[176,8,256]{2,0,1:T(8,128)(2,1)}), bf16[176,8,256]{2,0,1:T(8,128)(2,1)}, u32[]{:S(2)}, u32[]{:S(2)}) %all-to-all-start.1) | async-done | bytes 720928 | tf_op jit(solution)/shard_map/all_to_all | solution.py:267
  60.0 3.8 %convert_reduce_fusion = (f32[256]{0:T(256)S(1)}, bf16[1408,256]{0,1:T(8,128)(2,1)S(1)}) fusion(f32[1408,256]{0,1:T(8,128)S(1)} %copy.35, bf16[1408,256]{1,0:T(8,128)(2,1)} %bitcast.6, bf16[1408,1408]{1,0:T(8,128)(2,1)} %param.9), kind=kOutput, calls=%fused_computation.4 | convolution fusion | flops 1016463104 | bytes 6849536 | tf_op jit(solution)/shard_map/dot_general | solution.py:268
  63.8 0.3 fusion.4
  64.2 0.0 copy-done.8
  64.2 0.0 copy-start.7
  64.2 1.4 fusion.16
  65.6 0.0 all-gather.2.cloned.1.call-update
  65.7 0.0 copy-done.7
  65.7 0.2 convert_reduce_fusion.1
  66.0 0.2 select_reduce_fusion
  66.2 0.7 all_to_all.65
  66.9 13.3 %all-to-all-start.4 = ((s32[16,32,1]{1,2,0:T(1,128)}), s32[16,32,1]{1,2,0:T(1,128)S(1)}, u32[]{:S(2)}, u32[]{:S(2)}) async-start(s32[16,32,1]{1,2,0:T(1,128)} %bitcast.18), calls=%async_computation.4 | async-start | bytes 16384 | tf_op jit(solution)/shard_map/all_to_all | solution.py:262
  80.2 3.6 %reshape.104 = bf16[176,4,1408]{2,1,0:T(4,128)(2,1)S(1)} reshape(bf16[176,5632]{1,0:T(8,128)(2,1)} %param.10) | data formatting | bytes 3964928 | tf_op jit(solution)/shard_map/reshape | solution.py:284
  83.8 4.3 %fusion.42 = (bf16[176,1,1408]{2,1,0:T(2,128)(2,1)}, bf16[176,1,1408]{2,1,0:T(2,128)(2,1)}, bf16[176,1,1408]{2,1,0:T(2,128)(2,1)}, bf16[176,1,1408]{2,1,0:T(2,128)(2,1)}) fusion(bf16[176,4,1408]{2,1,0:T(4,128)(2,1)S(1)} %reshape.104), kind=kLoop, calls=%fused_computation.108 | loop fusion | bytes 3964928 | tf_op jit(solution)/shard_map/slice | solution.py:286
  88.1 1.1 copy.36
  89.2 21.1 %all-gather.2.cloned.1.call-done = bf16[4,1408,512]{1,2,0:T(8,128)(2,1)} async-done(((bf16[4,1408,64]{1,2,0:T(8,128)(2,1)}), bf16[4,1408,512]{1,2,0:T(8,128)(2,1)}) %all-gather.2.cloned.1.call-update) | async-done | bytes 5767184 | tf_op jit(solution)/shard_map/all_gather | solution.py:283
  110.4 0.0 copy-done.4
  110.4 2.0 %fusion.7 = f32[512,176]{0,1:T(8,128)S(1)} fusion(bf16[4,1408,512]{1,2,0:T(8,128)(2,1)} %all-gather.2.cloned.1.call-done, bf16[176,1,1408]{2,1,0:T(2,128)(2,1)S(1)} %copy-done.4), kind=kOutput, calls=%fused_computation.11 | convolution fusion | flops 253755392 | bytes 2297856 | tf_op jit(solution)/shard_map/dot_general | solution.py:286
  112.4 0.0 copy-start.3
  112.4 0.0 all-to-all-done.4
  112.4 3.7 %all-to-all-start.2 = ((bf16[8,176,256]{2,1,0:T(8,128)(2,1)}), bf16[8,176,256]{2,1,0:T(8,128)(2,1)S(1)}, u32[]{:S(2)}, u32[]{:S(2)}) async-start(bf16[8,176,256]{2,1,0:T(8,128)(2,1)} %bitcast.8), calls=%async_computation.2 | async-start | bytes 1441792 | tf_op jit(solution)/shard_map/all_to_all | solution.py:272
  116.1 0.0 copy-done.3
  116.1 0.0 copy-start.2
  116.1 2.1 %fusion.8 = f32[512,176]{0,1:T(8,128)S(1)} fusion(bf16[4,1408,512]{1,2,0:T(8,128)(2,1)} %all-gather.2.cloned.1.call-done, bf16[176,1,1408]{2,1,0:T(2,128)(2,1)S(1)} %copy-done.3), kind=kOutput, calls=%fused_computation.13 | convolution fusion | flops 253755392 | bytes 2297856 | tf_op jit(solution)/shard_map/dot_general | solution.py:286
  118.2 2.1 %fusion.9 = f32[512,176]{0,1:T(8,128)S(1)} fusion(bf16[4,1408,512]{1,2,0:T(8,128)(2,1)} %all-gather.2.cloned.1.call-done, bf16[176,1,1408]{2,1,0:T(2,128)(2,1)S(1)} %copy-done.2), kind=kOutput, calls=%fused_computation.15 | convolution fusion | flops 253755392 | bytes 2297856 | tf_op jit(solution)/shard_map/dot_general | solution.py:286
  120.3 2.2 %convolution_convert_fusion.1 = bf16[512,176]{0,1:T(8,128)(2,1)S(1)} fusion(f32[512,176]{0,1:T(8,128)S(1)} %fusion.7, f32[512,176]{0,1:T(8,128)S(1)} %fusion.8, f32[512,176]{0,1:T(8,128)S(1)} %fusion.9, bf16[4,1408,512]{1,2,0:T(8,128)(2,1)} %all-gather.2.cloned.1.call-done, s32[512]{0:T(512)S(1)} %multiply_add_fusion, bf16[176,1,1408]{2,1,0:T(2,128)(2,1)S(1)} %copy-done.1), kind=kOutput, calls=%fused_computation.23 | convolution fusion | flops 346742784 | bytes 3201024 | tf_op jit(solution)/shard_map/dot_general | solution.py:288
  122.5 0.8 copy.38
  123.3 5.1 %all-to-all-done.2 = bf16[8,176,256]{2,1,0:T(8,128)(2,1)S(1)} async-done(((bf16[8,176,256]{2,1,0:T(8,128)(2,1)}), bf16[8,176,256]{2,1,0:T(8,128)(2,1)S(1)}, u32[]{:S(2)}, u32[]{:S(2)}) %all-to-all-start.2) | async-done | bytes 720928 | tf_op jit(solution)/shard_map/all_to_all | solution.py:272
  128.5 6.9 %all-to-all-start.3 = ((bf16[16,32,176]{2,1,0:T(8,128)(2,1)}), bf16[16,32,176]{2,1,0:T(8,128)(2,1)S(1)}, u32[]{:S(2)}, u32[]{:S(2)}) async-start(bf16[16,32,176]{2,1,0:T(8,128)(2,1)} %bitcast.16), calls=%async_computation.3 | async-start | bytes 524288 | tf_op jit(solution)/shard_map/all_to_all | solution.py:291
  135.4 0.5 broadcast.258
  135.9 0.7 reduce.5
  136.6 0.1 eq.62
  136.7 0.9 copy.46
  137.6 6.3 %all-to-all-done.3 = bf16[16,32,176]{2,1,0:T(8,128)(2,1)S(1)} async-done(((bf16[16,32,176]{2,1,0:T(8,128)(2,1)}), bf16[16,32,176]{2,1,0:T(8,128)(2,1)S(1)}, u32[]{:S(2)}, u32[]{:S(2)}) %all-to-all-start.3) | async-done | bytes 180256 | tf_op jit(solution)/shard_map/all_to_all | solution.py:291
  143.9 1.1 convolution_convert_fusion
  (16 shorter events, 0.1 us)
Async XLA Ops:
  7.2 7.9 %copy-start.5 = (bf16[176,2048]{1,0:T(8,128)(2,1)S(1)}, bf16[176,2048]{1,0:T(8,128)(2,1)}, u32[]{:S(2)}) copy-start(bf16[176,2048]{1,0:T(8,128)(2,1)} %param.8) | copy-start | bytes 2162692
  9.8 26.6 %collective-permute-start = (bf16[2,176,1024]{2,1,0:T(8,128)(2,1)}, bf16[2,176,1024]{2,1,0:T(8,128)(2,1)S(1)}, u32[]{:S(2)}, u32[]{:S(2)}) collective-permute-start(bf16[2,176,1024]{2,1,0:T(8,128)(2,1)} %get-tuple-element.21), channel_id=1, source_target_pairs={{0,8},{8,16},{16,24},{24,32},{32,40},{40,48},{48,56},{56,64},{64,7... | collective-permute-start | bytes 2162696 | tf_op jit(solution)/shard_map/ppermute | solution.py:249
  13.8 22.7 %collective-permute-start.1 = (bf16[2,176,1024]{2,1,0:T(8,128)(2,1)}, bf16[2,176,1024]{2,1,0:T(8,128)(2,1)}, u32[]{:S(2)}, u32[]{:S(2)}) collective-permute-start(bf16[2,176,1024]{2,1,0:T(8,128)(2,1)} %get-tuple-element.20), channel_id=1, source_target_pairs={{8,0},{16,8},{24,16},{32,24},{40,32},{48,40},{56,48},{64,56},{72,6... | collective-permute-start | bytes 2162696 | tf_op jit(solution)/shard_map/ppermute | solution.py:252
  15.1 5.4 %copy-start.6 = (s32[64]{0:T(128)S(1)}, s32[64]{0:T(128)}, u32[]{:S(2)}) copy-start(s32[64]{0:T(128)} %param.12) | copy-start | bytes 772
  15.1 6.4 %copy-start = (bf16[3,176,2048]{2,1,0:T(8,128)(2,1)S(1)}, bf16[3,176,2048]{2,1,0:T(8,128)(2,1)}, u32[]{:S(2)}) copy-start(bf16[3,176,2048]{2,1,0:T(8,128)(2,1)} %qkv_ref.3) | copy-start | bytes 6488068
  16.0 26.6 %all-to-all-start = ((bf16[176,8,256]{2,0,1:T(8,128)(2,1)}), bf16[176,8,256]{2,0,1:T(8,128)(2,1)}, u32[]{:S(2)}, u32[]{:S(2)}) async-start(bf16[176,8,256]{2,0,1:T(8,128)(2,1)} %bitcast.78), calls=%async_computation | async-start | bytes 1441792 | tf_op jit(solution)/shard_map/all_to_all | solution.py:253
  42.6 17.4 %all-to-all-start.1 = ((bf16[176,8,256]{2,0,1:T(8,128)(2,1)}), bf16[176,8,256]{2,0,1:T(8,128)(2,1)}, u32[]{:S(2)}, u32[]{:S(2)}) async-start(bf16[176,8,256]{2,0,1:T(8,128)(2,1)} %bitcast.70), calls=%async_computation.1 | async-start | bytes 1441792 | tf_op jit(solution)/shard_map/all_to_all | solution.py:267
  47.4 63.0 %all-gather.2.cloned.1.call-start = ((), (), s32[]{:S(2)}) async-start(), calls=%async_computation.5 | async-start | bytes 6488064 | tf_op jit(solution)/shard_map/all_gather | solution.py:283
  60.0 4.2 %copy-start.8 = (f32[1408]{0:T(1024)S(1)}, f32[1408]{0:T(1024)}, u32[]{:S(2)}) copy-start(f32[1408]{0:T(1024)} %param.11) | copy-start | bytes 16900
  64.2 1.5 copy-start.7
  66.9 45.5 %all-to-all-start.4 = ((s32[16,32,1]{1,2,0:T(1,128)}), s32[16,32,1]{1,2,0:T(1,128)S(1)}, u32[]{:S(2)}, u32[]{:S(2)}) async-start(s32[16,32,1]{1,2,0:T(1,128)} %bitcast.18), calls=%async_computation.4 | async-start | bytes 16384 | tf_op jit(solution)/shard_map/all_to_all | solution.py:262
  88.1 22.3 %copy-start.4 = (bf16[176,1,1408]{2,1,0:T(2,128)(2,1)S(1)}, bf16[176,1,1408]{2,1,0:T(2,128)(2,1)}, u32[]{:S(2)}) copy-start(bf16[176,1,1408]{2,1,0:T(2,128)(2,1)} %get-tuple-element.23) | copy-start | bytes 1486852
  112.4 3.7 %copy-start.3 = (bf16[176,1,1408]{2,1,0:T(2,128)(2,1)S(1)}, bf16[176,1,1408]{2,1,0:T(2,128)(2,1)}, u32[]{:S(2)}) copy-start(bf16[176,1,1408]{2,1,0:T(2,128)(2,1)} %get-tuple-element.24) | copy-start | bytes 1486852
  112.4 16.1 %all-to-all-start.2 = ((bf16[8,176,256]{2,1,0:T(8,128)(2,1)}), bf16[8,176,256]{2,1,0:T(8,128)(2,1)S(1)}, u32[]{:S(2)}, u32[]{:S(2)}) async-start(bf16[8,176,256]{2,1,0:T(8,128)(2,1)} %bitcast.8), calls=%async_computation.2 | async-start | bytes 1441792 | tf_op jit(solution)/shard_map/all_to_all | solution.py:272
  116.1 2.1 %copy-start.2 = (bf16[176,1,1408]{2,1,0:T(2,128)(2,1)S(1)}, bf16[176,1,1408]{2,1,0:T(2,128)(2,1)}, u32[]{:S(2)}) copy-start(bf16[176,1,1408]{2,1,0:T(2,128)(2,1)} %get-tuple-element.25) | copy-start | bytes 1486852
  118.2 2.1 %copy-start.1 = (bf16[176,1,1408]{2,1,0:T(2,128)(2,1)S(1)}, bf16[176,1,1408]{2,1,0:T(2,128)(2,1)}, u32[]{:S(2)}) copy-start(bf16[176,1,1408]{2,1,0:T(2,128)(2,1)} %get-tuple-element.22) | copy-start | bytes 1486852
  128.5 15.5 %all-to-all-start.3 = ((bf16[16,32,176]{2,1,0:T(8,128)(2,1)}), bf16[16,32,176]{2,1,0:T(8,128)(2,1)S(1)}, u32[]{:S(2)}, u32[]{:S(2)}) async-start(bf16[16,32,176]{2,1,0:T(8,128)(2,1)} %bitcast.16), calls=%async_computation.3 | async-start | bytes 524288 | tf_op jit(solution)/shard_map/all_to_all | solution.py:291
Sparse Core Ops, SparseCore 0:
  65.8 44.5 all-gather.1

commit v2 on v1

--- a/solution.py
+++ b/solution.py
@@ -233,18 +233,346 @@
     )(halo_lo, halo_n, qkv, left, right, start2, length2, m, l, acc)
 
 
+MESH = pl.DeviceIdType.MESH
+
+
+def tail_kernel(
+    rows,
+    cols,
+    attended_ref,
+    residual_ref,
+    out_weight_hbm,
+    merge_weight_hbm,
+    far_weight_hbm,
+    gain_ref,
+    dest_line_ref,
+    dest_column_ref,
+    layer_ref,
+    image_ref,
+    att,
+    weight,
+    weight_t,
+    merge_w,
+    layer_rows,
+    held,
+    far_rows,
+    merged,
+    pick,
+    sorted_rows,
+    got_rows,
+    load_sem,
+    spread_send,
+    spread_recv,
+    back_send,
+    back_recv,
+    near_send,
+    near_recv,
+    sib_send,
+    sib_recv,
+    far_send,
+    far_recv,
+    row_send,
+    row_recv,
+):
+    row = lax.axis_index("row")
+    me = lax.axis_index("col")
+    width, tokens = attended_ref.shape
+    full = weight.shape[0]
+    chunk = tokens // cols
+    part = chunk // 4
+    groups = tokens // 4
+    share = groups // rows
+    chips = cols // 2
+    core = me % 2
+    chip = me // 2
+    sibling = me + 1 - 2 * core
+    half = full // 2
+
+    barrier = pltpu.get_barrier_semaphore()
+    for k in range(1, cols):
+        pl.semaphore_signal(
+            barrier, inc=1, device_id={"col": (me + k) % cols}, device_id_type=MESH
+        )
+    for k in range(1, rows):
+        pl.semaphore_signal(
+            barrier, inc=1, device_id={"row": (row + k) % rows}, device_id_type=MESH
+        )
+    loads = [
+        pltpu.make_async_copy(out_weight_hbm, weight, load_sem.at[0]),
+        pltpu.make_async_copy(merge_weight_hbm, merge_w.at[0:width], load_sem.at[1]),
+    ]
+    pieces, _, piece = far_weight_hbm.shape
+    used = -(-merge_w.shape[1] // piece)
+    for r in range(used):
+        at = min(r * piece, merge_w.shape[1] - piece)
+        loads.append(
+            pltpu.make_async_copy(
+                far_weight_hbm.at[r],
+                merge_w.at[width : 2 * width, at : at + piece],
+                load_sem.at[2 + r],
+            )
+        )
+    for r, load in enumerate(loads):
+        if r != len(loads) - 1:
+            load.start()
+    pl.semaphore_wait(barrier, rows + cols - 2)
+
+    spread = []
+    for k in range(1, cols):
+        to = (me + k) % cols
+        copy = pltpu.make_async_remote_copy(
+            src_ref=attended_ref.at[:, pl.ds(pl.multiple_of(to * chunk, chunk), chunk)],
+            dst_ref=att.at[pl.ds(pl.multiple_of(me * width, 16), width)],
+            send_sem=spread_send.at[k],
+            recv_sem=spread_recv.at[k],
+            device_id={"col": to},
+            device_id_type=MESH,
+        )
+        copy.start()
+        spread.append(copy)
+    mine = pl.ds(pl.multiple_of(me * chunk, chunk), chunk)
+    att[pl.ds(pl.multiple_of(me * width, 16), width), :] = attended_ref[:, mine]
+
+    line = dest_line_ref[...]
+    owner_line = line // groups
+    owner_column = dest_column_ref[...] // groups
+    down = lax.broadcasted_iota(jnp.int32, (groups, groups), 0)
+    across = lax.broadcasted_iota(jnp.int32, (groups, groups), 1)
+    earlier = (owner_column == owner_line) & (down < across)
+    rank = jnp.sum(earlier.astype(jnp.int32), axis=0, keepdims=True)
+    spot = owner_line * share + rank
+    pick[...] = jnp.where(down == spot, 1.0, 0.0).astype(jnp.bfloat16)
+    slot = line % groups
+    extra = merged.shape[0] - width
+    which = lax.broadcasted_iota(jnp.int32, (extra, groups), 0)
+    digits = jnp.where(which == 0, slot // 16, jnp.where(which == 1, slot % 16, 0))
+    merged[width:, :] = digits.astype(jnp.float32).astype(jnp.bfloat16)
+
+    loads[0].wait()
+
+    def turn(i, carry):
+        at = pl.multiple_of(i * 128, 128)
+        weight_t[pl.ds(at, 128), :] = jnp.transpose(weight[:, pl.ds(at, 128)])
+        return carry
+
+    lax.fori_loop(0, full // 128, turn, 0)
+    for load in loads[1:-1]:
+        load.wait()
+    loads[-1].start()
+
+    for copy in spread:
+        copy.wait()
+    strip = full // 4
+    for i in range(4):
+        at = i * strip
+        projected = jnp.dot(
+            weight_t[at : at + strip, :], att[...], preferred_element_type=jnp.float32
+        )
+        layer_rows[at : at + strip, :] = (
+            residual_ref[at : at + strip, :].astype(jnp.float32) + projected
+        ).astype(jnp.bfloat16)
+
+    values32 = layer_rows[...].astype(jnp.float32)
+    centre = jnp.sum(values32, axis=0, keepdims=True) * (1.0 / full)
+    spread_of = jnp.sum(jnp.square(values32 - centre), axis=0, keepdims=True) * (1.0 / full)
+    scale = lax.rsqrt(spread_of + 1e-06)
+    normed = ((values32 - centre) * scale * gain_ref[...]).astype(jnp.bfloat16)
+    here = lax.broadcasted_iota(jnp.int32, (chunk, chunk), 0)
+    there = lax.broadcasted_iota(jnp.int32, (chunk, chunk), 1)
+    order = jnp.where((here % 4) * part + here // 4 == there, 1.0, 0.0).astype(jnp.bfloat16)
+    held[core] = jnp.dot(normed, order, preferred_element_type=jnp.float32).astype(jnp.bfloat16)
+
+    goal = (chip + 1 + 2 * core) % chips
+    near = []
+    for h in range(2):
+        span = pl.ds(h * half, half)
+        copy = pltpu.make_async_remote_copy(
+            src_ref=held.at[core, span],
+            dst_ref=held.at[2 + core, span],
+            send_sem=near_send.at[h],
+            recv_sem=near_recv.at[core],
+            device_id={"col": goal * 2 + h},
+            device_id_type=MESH,
+        )
+        copy.start()
+        near.append(copy)
+    own = pltpu.make_async_remote_copy(
+        src_ref=held.at[core],
+        dst_ref=held.at[core],
+        send_sem=sib_send.at[0],
+        recv_sem=sib_recv.at[0],
+        device_id={"col": sibling},
+        device_id_type=MESH,
+    )
+    own.start()
+
+    back = []
+    for k in range(1, cols):
+        to = (me + k) % cols
+        copy = pltpu.make_async_remote_copy(
+            src_ref=layer_rows.at[pl.ds(pl.multiple_of(to * width, 16), width)],
+            dst_ref=layer_ref.at[:, mine],
+            send_sem=back_send.at[k],
+            recv_sem=back_recv.at[k],
+            device_id={"col": to},
+            device_id_type=MESH,
+        )
+        copy.start()
+        back.append(copy)
+    layer_ref[:, mine] = layer_rows[pl.ds(pl.multiple_of(me * width, 16), width), :]
+    loads[-1].wait()
+
+    passed = []
+    my_half = pl.ds(pl.multiple_of(core * half, 16), half)
+    for s in range(2):
+        arrive = pltpu.make_async_remote_copy(
+            src_ref=held.at[core, my_half],
+            dst_ref=held.at[2 + s, my_half],
+            send_sem=near_send.at[s],
+            recv_sem=near_recv.at[s],
+            device_id={"col": sibling},
+            device_id_type=MESH,
+        )
+        arrive.wait_recv()
+        copy = pltpu.make_async_remote_copy(
+            src_ref=held.at[2 + s, my_half],
+            dst_ref=held.at[2 + s, my_half],
+            send_sem=sib_send.at[1 + s],
+            recv_sem=sib_recv.at[1 + s],
+            device_id={"col": sibling},
+            device_id_type=MESH,
+        )
+        copy.start()
+        passed.append(copy)
+    for copy in near:
+        copy.wait_send()
+    own.wait()
+    for copy in passed:
+        copy.wait()
+
+    total = None
+    for j in range(4):
+        side = jnp.concatenate(
+            [held[s, :, j * part : (j + 1) * part] for s in range(4)], axis=1
+        )
+        term = jnp.dot(
+            merge_w[:, j * full : (j + 1) * full], side, preferred_element_type=jnp.float32
+        )
+        total = term if total is None else total + term
+    far_rows[...] = total[width:].astype(jnp.bfloat16)
+    across_y = pltpu.make_async_remote_copy(
+        src_ref=far_rows,
+        dst_ref=merged.at[0:width, chunk : 2 * chunk],
+        send_sem=far_send,
+        recv_sem=far_recv,
+        device_id={"col": (me + cols // 2) % cols},
+        device_id_type=MESH,
+    )
+    across_y.start()
+    merged[0:width, 0:chunk] = total[:width].astype(jnp.bfloat16)
+    across_y.wait()
+
+    sorted_rows[...] = lax.dot_general(
+        pick[...], merged[...], (((1,), (1,)), ((), ())), preferred_element_type=jnp.float32
+    ).astype(jnp.bfloat16)
+    moves = []
+    for k in range(1, rows):
+        to = (row + k) % rows
+        copy = pltpu.make_async_remote_copy(
+            src_ref=sorted_rows.at[pl.ds(pl.multiple_of(to * share, share), share)],
+            dst_ref=got_rows.at[pl.ds(pl.multiple_of(row * share, share), share)],
+            send_sem=row_send.at[k],
+            recv_sem=row_recv.at[k],
+            device_id={"row": to},
+            device_id_type=MESH,
+        )
+        copy.start()
+        moves.append(copy)
+    keep = pl.ds(pl.multiple_of(row * share, share), share)
+    got_rows[keep, :] = sorted_rows[keep, :]
+    for copy in moves:
+        copy.wait()
+    got = got_rows[...]
+    target = got[:, width : width + 1].astype(jnp.float32) * 16.0 + got[
+        :, width + 1 : width + 2
+    ].astype(jnp.float32)
+    put = jnp.where(target == across.astype(jnp.float32), 1.0, 0.0).astype(jnp.bfloat16)
+    image_ref[...] = lax.dot_general(
+        got, put, (((0,), (0,)), ((), ())), preferred_element_type=jnp.float32
+    )[:width].astype(jnp.bfloat16)
+    for copy in back:
+        copy.wait()
+
+
+def tail(attended, residual, out_weight, merge_weight, far_weight, gain, dest_slots, rows, cols):
+    width, tokens = attended.shape
+    full = out_weight.shape[0]
+    chunk = tokens // cols
+    groups = tokens // 4
+    bf16 = jnp.bfloat16
+    vmem = pl.BlockSpec(memory_space=pltpu.VMEM)
+    hbm = pl.BlockSpec(memory_space=pl.ANY)
+    dma = pltpu.SemaphoreType.DMA
+    return pl.pallas_call(
+        functools.partial(tail_kernel, rows, cols),
+        out_shape=(
+            jax.ShapeDtypeStruct((width, tokens), bf16),
+            jax.ShapeDtypeStruct((width, groups), bf16),
+        ),
+        in_specs=[vmem, vmem, hbm, hbm, hbm, vmem, vmem, vmem],
+        out_specs=(vmem, vmem),
+        scratch_shapes=[
+            pltpu.VMEM((full, chunk), bf16),
+            pltpu.VMEM((full, full), bf16),
+            pltpu.VMEM((full, full), bf16),
+            pltpu.VMEM((2 * width, merge_weight.shape[1]), bf16),
+            pltpu.VMEM((full, chunk), bf16),
+            pltpu.VMEM((4, full, chunk), bf16),
+            pltpu.VMEM((width, chunk), bf16),
+            pltpu.VMEM((width + 16, groups), bf16),
+            pltpu.VMEM((groups, groups), bf16),
+            pltpu.VMEM((groups, width + 16), bf16),
+            pltpu.VMEM((groups, width + 16), bf16),
+            dma((2 + rows,)),
+            dma((cols,)),
+            dma((cols,)),
+            dma((cols,)),
+            dma((cols,)),
+            dma((2,)),
+            dma((2,)),
+            dma((3,)),
+            dma((3,)),
+            dma,
+            dma,
+            dma((rows,)),
+            dma((rows,)),
+        ],
+        compiler_params=pltpu.CompilerParams(
+            collective_id=0, has_side_effects=True, vmem_limit_bytes=48 << 20
+        ),
+        cost_estimate=pl.CostEstimate(
+            flops=8 * full * full * chunk, bytes_accessed=16 << 20, transcendentals=0
+        ),
+    )(
+        attended,
+        residual,
+        out_weight,
+        merge_weight,
+        far_weight,
+        gain[:, None],
+        dest_slots[None, :],
+        dest_slots[:, None],
+    )
+
+
 def body(qkv, residual_in, out_weight, merge_weight, merge_gain, image_groups, dest_row):
-    width_here = qkv.shape[1]
     tok_rows = qkv.shape[2]
-    full_width = out_weight.shape[0]
-    reach = tok_rows // 2
     rows = lax.axis_size("row")
     cols = lax.axis_size("col")
     row_id = lax.axis_index("row")
+    col_id = lax.axis_index("col")
     all_tokens = tok_rows * rows
-    chunk = tok_rows // cols
-    group_rows = tok_rows // 4
-    share = group_rows // rows
+    reach = tok_rows // 2
 
     left = lax.ppermute(
         qkv[1:, :, tok_rows - reach :], "row", [(i, i + 1) for i in range(rows - 1)]
@@ -252,47 +580,34 @@
     right = lax.ppermute(qkv[1:, :, :reach], "row", [(i + 1, i) for i in range(rows - 1)])
     residual = lax.all_to_all(residual_in, "col", 1, 0, tiled=True)
 
-    owner = dest_row // group_rows
-    ids = jnp.arange(group_rows, dtype=jnp.int32)
-    earlier = (owner[None, :] == owner[:, None]) & (ids[None, :] < ids[:, None])
-    spot = owner * share + jnp.sum(earlier.astype(jnp.int32), axis=1)
-    slots = jnp.arange(group_rows, dtype=jnp.int32)
-    picked = spot[:, None] == slots[None, :]
-    sent_dest = jnp.sum(jnp.where(picked, (dest_row % group_rows)[:, None], 0), axis=0)
-    got_dest = lax.all_to_all(sent_dest, "row", 0, 0, tiled=True)
-    placed = (got_dest[:, None] == slots[None, :]).astype(jnp.bfloat16)
-    picked = picked.astype(jnp.bfloat16)
+    lanes = merge_weight.shape[1]
+    piece = -(-lanes // (128 * rows)) * 128
+    piece_at = jnp.minimum(row_id * piece, lanes - piece)
+    slice_here = lax.dynamic_slice_in_dim(merge_weight, piece_at, piece, 1)
+    slice_far = lax.ppermute(slice_here, "col", [(i, (i + cols // 2) % cols) for i in range(cols)])
+    far_weight = lax.all_gather(slice_far, "row", axis=0)
+
+    chips = cols // 2
+    chip = col_id // 2
+    before, after, across = (chip + chips - 1) % chips, (chip + 1) % chips, (chip + 2) % chips
+    met = jnp.stack(
+        [
+            2 * chip,
+            2 * chip + 1,
+            2 * before,
+            2 * after + 1,
+            2 * across,
+            2 * across + 1,
+            2 * after,
+            2 * before + 1,
+        ]
+    )
+    dest_slots = jnp.take(dest_row.reshape(cols, -1), met, axis=0).reshape(-1)
 
     attended = attention(qkv, left, right, image_groups, row_id, all_tokens)
-    attended = lax.all_to_all(attended, "col", 1, 0, tiled=True)
-    projected = lax.dot_general(
-        out_weight, attended, (((0,), (0,)), ((), ())), preferred_element_type=jnp.float32
-    )
-    layer_rows = (residual.astype(jnp.float32) + projected).astype(jnp.bfloat16)
-    layer_out = lax.all_to_all(layer_rows, "col", 0, 1, tiled=True)
-    values32 = layer_rows.astype(jnp.float32)
-    centre = jnp.mean(values32, axis=0, keepdims=True)
-    spread = jnp.mean(jnp.square(values32 - centre), axis=0, keepdims=True)
-    normed = ((values32 - centre) * lax.rsqrt(spread + 1e-06) * merge_gain[:, None]).astype(
-        jnp.bfloat16
-    )
-    t = jnp.arange(chunk, dtype=jnp.int32)
-    order = ((t % 4) * (chunk // 4) + t // 4)[:, None] == t[None, :]
-    by_part = jnp.dot(normed, order.astype(jnp.bfloat16)).astype(jnp.bfloat16)
-    by_part = by_part.reshape(full_width, 4, chunk // 4).transpose(1, 0, 2)
-    gathered = lax.all_gather(by_part, "col", axis=2, tiled=True)
-    parts = merge_weight.reshape(width_here, 4, full_width)
-    merged = sum(
-        jnp.dot(parts[:, j], gathered[j], preferred_element_type=jnp.float32) for j in range(4)
-    ).astype(jnp.bfloat16)
-    sorted_rows = lax.dot_general(
-        picked, merged, (((0,), (1,)), ((), ())), preferred_element_type=jnp.float32
-    ).astype(jnp.bfloat16)
-    got_rows = lax.all_to_all(sorted_rows, "row", 0, 0, tiled=True)
-    image_rows = lax.dot_general(
-        got_rows, placed, (((0,), (0,)), ((), ())), preferred_element_type=jnp.float32
-    ).astype(jnp.bfloat16)
-    return (layer_out, image_rows)
+    return tail(
+        attended, residual, out_weight, merge_weight, far_weight, merge_gain, dest_slots, rows, cols
+    )
 
 
 def solution(mesh):

time: 153 us -> 131 us (0.86)
  Pallas kernels: 20.2 us -> 72.1 us
  waiting for transfers between devices: 43.4 us -> 14.8 us
  starting transfers between devices: 38.5 us -> 13.2 us
  matrix products: 14.7 us -> 0 us
  local copies, waits for them, and re-layouts: 17.3 us -> 13.9 us
  other arithmetic: 3.37 us -> 0.72 us
    pallas_call x0 -> x1, Pallas kernels: none -> 46.3 us  [tail(): pl.pallas_call(functools.partial(tail_kernel, rows, cols), out_shape=(jax...]
    all_to_all x4 -> x0, starting transfers between devices: 28.8 us -> none  [the longest x1 13.3 us: body(): got_dest = lax.all_to_all(sent_dest, 'row', 0, 0, tiled=True)]
    all_to_all x4 -> x0, waiting for transfers between devices: 22.2 us -> none  [the longest x1 10.8 us: body(): attended = lax.all_to_all(attended, 'col', 1, 0, tiled=True)]
    dot_general x7 -> x0, matrix products: 14.7 us -> none  [the longest x3 6.12 us: body(): jnp.dot(parts[:, j], gathered[j], preferred_element_type=jnp.float32)]
    all_gather x1, waiting for transfers between devices: 21.1 us -> 11.2 us  [body(): far_weight = lax.all_gather(slice_far, 'row', axis=0)]
    unnamed x18 -> x22, local copies, waits for them, and re-layouts: 0.04 us -> 6.83 us
    pallas_call x1, Pallas kernels: 15 us -> 21.5 us  [attention(): pl.pallas_call(functools.partial(local_kernel, coef), out_shape=(stat, st...]
    slice x1 -> x0, local copies, waits for them, and re-layouts: 4.28 us -> none  [body(): parts[:, j]]
  transfers between devices with their start and end apart: 8 -> 5, of which waited for: 4 -> 2; matrix products, arithmetic and copies ran while one was open for 17% -> 5% of each run, Pallas kernels for 13% -> 20%
where the time goes in v2:
time: 131 us; the launch traced here: 129 us
  Pallas kernels  72.1 us (55%)
  waiting for transfers between devices  14.8 us (11%)
  between operations  14.2 us (11%)
  local copies, waits for them, and re-layouts  13.9 us (11%)
  starting transfers between devices  13.2 us (10%)
    pallas_call x1, Pallas kernels, tail(): pl.pallas_call(functools.partial(tail_kernel, rows, cols), out_shape=(jax...  46.3 us
    pallas_call x1, Pallas kernels, attention(): pl.pallas_call(functools.partial(local_kernel, coef), out_shape=(stat, st...  21.5 us
    all_gather x1, waiting for transfers between devices, body(): far_weight = lax.all_gather(slice_far, 'row', axis=0)  11.2 us
    unnamed x22, local copies, waits for them, and re-layouts  6.83 us
    all_to_all x1, starting transfers between devices, body(): residual = lax.all_to_all(residual_in, 'col', 1, 0, tiled=True)  4.47 us
    pallas_call x1, Pallas kernels, attention(): pl.pallas_call(functools.partial(halo_kernel, coef), out_shape=jax.ShapeD...  4.28 us
    ppermute x1, starting transfers between devices, body(): lax.ppermute(qkv[1:, :, tok_rows - reach:], 'row', [(i, i + 1) for i in r...  4.04 us
    ppermute x1, waiting for transfers between devices, body(): lax.ppermute(slice_here, 'col', [(i, (i + cols // 2) % cols) for i in ran...  3.58 us
  transfers between devices with their start and end apart: 5, of which 2 were waited for; matrix products, arithmetic and copies ran while one was open for 5% of the time, Pallas kernels for 20%

profile of v2, /device:TPU:0, one launch (start us, length us, event | category | flops | bytes accessed | tf_op | source)
XLA Modules:
  0.0 128.9 jit_solution(15147421480365245582)
XLA Ops:
  7.2 0.0 all-gather.3.cloned.1.call-start
  7.2 1.0 constant_dynamic-slice_fusion
  8.3 3.4 %collective-permute-start.2 = (bf16[176,384]{1,0:T(8,128)(2,1)S(1)}, bf16[176,384]{1,0:T(8,128)(2,1)S(1)}, u32[]{:S(2)}, u32[]{:S(2)}) collective-permute-start(bf16[176,384]{1,0:T(8,128)(2,1)S(1)} %constant_dynamic-slice_fusion), channel_id=1, source_target_pairs={{0,4},{1,5},{2,6},{3,7},{4,0},{5,1},{6,2},{7,3},{8,12},{9,13},{10,... | collective-permute-start | bytes 405512 | tf_op jit(solution)/shard_map/ppermute | solution.py:587
  11.6 3.6 %collective-permute-done.2 = bf16[176,384]{1,0:T(8,128)(2,1)S(1)} collective-permute-done((bf16[176,384]{1,0:T(8,128)(2,1)S(1)}, bf16[176,384]{1,0:T(8,128)(2,1)S(1)}, u32[]{:S(2)}, u32[]{:S(2)}) %collective-permute-start.2) | collective-permute-done | bytes 135200 | tf_op jit(solution)/shard_map/ppermute | solution.py:587
  15.2 0.0 copy-start.6
  15.2 0.7 copy-done.6
  15.9 0.0 all-gather.3.cloned.1.call-update
  15.9 0.0 copy-start.5
  15.9 2.6 %fusion.3 = (bf16[2,176,1024]{2,1,0:T(8,128)(2,1)}, bf16[2,176,1024]{2,1,0:T(8,128)(2,1)}) fusion(bf16[3,176,2048]{2,1,0:T(8,128)(2,1)} %qkv_ref.3), kind=kLoop, calls=%fused_computation.48 | loop fusion | bytes 2883584 | tf_op jit(solution)/shard_map/slice | solution.py:580
  18.5 0.0 copy-start.9
  18.5 0.0 copy-start.8
  18.5 0.0 copy-start.7
  18.5 4.0 %collective-permute-start = (bf16[2,176,1024]{2,1,0:T(8,128)(2,1)}, bf16[2,176,1024]{2,1,0:T(8,128)(2,1)S(1)}, u32[]{:S(2)}, u32[]{:S(2)}) collective-permute-start(bf16[2,176,1024]{2,1,0:T(8,128)(2,1)} %get-tuple-element.21), channel_id=1, source_target_pairs={{0,8},{8,16},{16,24},{24,32},{32,40},{40,48},{48,56},{56,64},{64,7... | collective-permute-start | bytes 2162696 | tf_op jit(solution)/shard_map/ppermute | solution.py:577
  22.6 1.3 %collective-permute-start.1 = (bf16[2,176,1024]{2,1,0:T(8,128)(2,1)}, bf16[2,176,1024]{2,1,0:T(8,128)(2,1)}, u32[]{:S(2)}, u32[]{:S(2)}) collective-permute-start(bf16[2,176,1024]{2,1,0:T(8,128)(2,1)} %get-tuple-element.20), channel_id=1, source_target_pairs={{8,0},{16,8},{24,16},{32,24},{40,32},{48,40},{56,48},{64,56},{72,6... | collective-permute-start | bytes 2162696 | tf_op jit(solution)/shard_map/ppermute | solution.py:580
  23.9 0.0 copy-done.5
  23.9 0.0 copy-start
  23.9 0.9 copy.21
  24.8 4.5 %all-to-all-start = ((bf16[176,8,256]{2,0,1:T(8,128)(2,1)}), bf16[176,8,256]{2,0,1:T(8,128)(2,1)}, u32[]{:S(2)}, u32[]{:S(2)}) async-start(bf16[176,8,256]{2,0,1:T(8,128)(2,1)} %bitcast.33), calls=%async_computation | async-start | bytes 1441792 | tf_op jit(solution)/shard_map/all_to_all | solution.py:581
  29.3 0.0 copy-done.9
  29.3 0.1 reshape.438
  29.4 0.0 copy-done.8
  29.4 0.1 copy.15
  29.5 0.1 reduce-window.7
  29.6 0.1 multiply_reduce_fusion
  29.7 0.2 select_reduce_fusion
  29.9 0.1 slice.12
  30.0 0.1 slice.13
  30.1 0.1 stack.62
  30.2 0.6 gather_fusion
  30.8 0.1 stack.53
  30.9 0.1 broadcast_select_fusion
  31.0 0.2 select_n.117.dest_column_ref
  31.2 0.1 select_n.115.dest_line_ref
  31.3 0.0 copy-done.7
  31.3 1.1 broadcast_in_dim.49.gain_ref
  32.4 0.1 pad_add_fusion.first_ref
  32.5 0.1 pad_add_fusion.1.n_ref
  32.6 0.0 copy-done
  32.6 21.5 %shard_map.86 = (f32[16,1,256]{2,1,0:T(1,128)S(1)}, f32[16,1,256]{2,1,0:T(1,128)S(1)}, f32[16,88,256]{2,1,0:T(8,128)S(1)}) custom-call(s32[8]{0:T(128)S(1)} %maximum_minimum_fusion.lo_ref, s32[8]{0:T(128)S(1)} %get-tuple-element.10.n_ref, bf16[3,176,2048]{2,1,0:T(8,128)(2,1)S(1)} %copy-done, s32[1,2048]{1,0:T(1,128)S(1)} %bitcast.31, s32[1,2048]{1,0:T(1,128)S(1)} %bitcast.29), custom_call_target="tpu_custom_call" | custom-call | flops 1730150400 | bytes 8388608 | tf_op jit(solution)/shard_map/pallas_call | solution.py:203
  54.1 0.0 collective-permute-done.left_ref
  54.1 0.0 collective-permute-done.1.right_ref
  54.1 4.3 %shard_map.87.attended_ref = bf16[176,2048]{1,0:T(8,128)(2,1)S(1)} custom-call(s32[16]{0:T(128)S(1)} %pad_add_fusion.first_ref, s32[16]{0:T(128)S(1)} %pad_add_fusion.1.n_ref, bf16[3,176,2048]{2,1,0:T(8,128)(2,1)S(1)} %copy-done, bf16[2,176,1024]{2,1,0:T(8,128)(2,1)S(1)} %collective-permute-done.left_ref, ...), custom_call_target="tpu_custom_call" | custom-call | flops 432537600 | bytes 8388608 | tf_op jit(solution)/shard_map/pallas_call | solution.py:217
  58.4 0.0 copy-start.1
  58.4 0.8 copy-done.1
  59.3 0.0 all-to-all-done
  59.3 11.2 %all-gather.3.cloned.1.call-done = bf16[2816,384]{1,0:T(8,128)(2,1)} async-done(((bf16[176,384]{1,0:T(8,128)(2,1)}), bf16[2816,384]{1,0:T(8,128)(2,1)}) %all-gather.3.cloned.1.call-update) | async-done | bytes 2162704 | tf_op jit(solution)/shard_map/all_gather | solution.py:588
  70.4 0.0 copy-start.2
  70.4 1.1 copy-done.2
  71.5 0.0 copy-start.3
  71.6 1.1 copy-done.3
  72.7 0.0 copy-start.4
  72.7 1.5 %copy-done.4 = bf16[176,5632]{1,0:T(8,128)(2,1)S(1)} copy-done((bf16[176,5632]{1,0:T(8,128)(2,1)S(1)}, bf16[176,5632]{1,0:T(8,128)(2,1)}, u32[]{:S(2)}) %copy-start.4) | copy-done | bytes 1982488
  74.2 46.3 %shard_map.88 = (bf16[176,2048]{1,0:T(8,128)(2,1)S(1)}, bf16[176,512]{1,0:T(8,128)(2,1)S(1)}) custom-call(bf16[176,2048]{1,0:T(8,128)(2,1)S(1)} %copy-done.2, bf16[1408,256]{1,0:T(8,128)(2,1)} %bitcast.4.residual_ref, bf16[1408,1408]{1,0:T(8,128)(2,1)} %out_weight_hbm.1, bf16[176,5632]{1,0:T(8,128)(2,1)S(1)} %copy-done.4, bf16[16,176,384]{2,1,0:T(8,128)(2,1)} %bitcast.36, ...), custom_call_target="tpu_custom_call" | custom-call | flops 4060086272 | bytes 16777216 | tf_op jit(solution)/shard_map/pallas_call | solution.py:516
  120.5 0.9 copy.24
  121.4 0.7 copy.25
  (9 shorter events, 0.1 us)
Async XLA Ops:
  7.2 63.3 %all-gather.3.cloned.1.call-start = ((), (), s32[]{:S(2)}) async-start(), calls=%async_computation.1 | async-start | bytes 2297856 | tf_op jit(solution)/shard_map/all_gather | solution.py:588
  8.3 6.9 %collective-permute-start.2 = (bf16[176,384]{1,0:T(8,128)(2,1)S(1)}, bf16[176,384]{1,0:T(8,128)(2,1)S(1)}, u32[]{:S(2)}, u32[]{:S(2)}) collective-permute-start(bf16[176,384]{1,0:T(8,128)(2,1)S(1)} %constant_dynamic-slice_fusion), channel_id=1, source_target_pairs={{0,4},{1,5},{2,6},{3,7},{4,0},{5,1},{6,2},{7,3},{8,12},{9,13},{10,... | collective-permute-start | bytes 405512 | tf_op jit(solution)/shard_map/ppermute | solution.py:587
  15.2 0.7 copy-start.6
  15.9 8.0 %copy-start.5 = (bf16[176,2048]{1,0:T(8,128)(2,1)S(1)}, bf16[176,2048]{1,0:T(8,128)(2,1)}, u32[]{:S(2)}) copy-start(bf16[176,2048]{1,0:T(8,128)(2,1)} %param.8) | copy-start | bytes 2162692
  18.5 10.8 %copy-start.9 = (s32[512]{0:T(512)S(1)}, s32[512]{0:T(512)}, u32[]{:S(2)}) copy-start(s32[512]{0:T(512)} %param.13) | copy-start | bytes 6148
  18.5 10.9 %copy-start.8 = (s32[64]{0:T(128)S(1)}, s32[64]{0:T(128)}, u32[]{:S(2)}) copy-start(s32[64]{0:T(128)} %param.12) | copy-start | bytes 772
  18.5 12.8 %copy-start.7 = (f32[1408]{0:T(1024)S(1)}, f32[1408]{0:T(1024)}, u32[]{:S(2)}) copy-start(f32[1408]{0:T(1024)} %param.11) | copy-start | bytes 16900
  18.5 35.6 %collective-permute-start = (bf16[2,176,1024]{2,1,0:T(8,128)(2,1)}, bf16[2,176,1024]{2,1,0:T(8,128)(2,1)S(1)}, u32[]{:S(2)}, u32[]{:S(2)}) collective-permute-start(bf16[2,176,1024]{2,1,0:T(8,128)(2,1)} %get-tuple-element.21), channel_id=1, source_target_pairs={{0,8},{8,16},{16,24},{24,32},{32,40},{40,48},{48,56},{56,64},{64,7... | collective-permute-start | bytes 2162696 | tf_op jit(solution)/shard_map/ppermute | solution.py:577
  22.6 31.6 %collective-permute-start.1 = (bf16[2,176,1024]{2,1,0:T(8,128)(2,1)}, bf16[2,176,1024]{2,1,0:T(8,128)(2,1)}, u32[]{:S(2)}, u32[]{:S(2)}) collective-permute-start(bf16[2,176,1024]{2,1,0:T(8,128)(2,1)} %get-tuple-element.20), channel_id=1, source_target_pairs={{8,0},{16,8},{24,16},{32,24},{40,32},{48,40},{56,48},{64,56},{72,6... | collective-permute-start | bytes 2162696 | tf_op jit(solution)/shard_map/ppermute | solution.py:580
  23.9 8.7 %copy-start = (bf16[3,176,2048]{2,1,0:T(8,128)(2,1)S(1)}, bf16[3,176,2048]{2,1,0:T(8,128)(2,1)}, u32[]{:S(2)}) copy-start(bf16[3,176,2048]{2,1,0:T(8,128)(2,1)} %qkv_ref.3) | copy-start | bytes 6488068
  24.8 34.5 %all-to-all-start = ((bf16[176,8,256]{2,0,1:T(8,128)(2,1)}), bf16[176,8,256]{2,0,1:T(8,128)(2,1)}, u32[]{:S(2)}, u32[]{:S(2)}) async-start(bf16[176,8,256]{2,0,1:T(8,128)(2,1)} %bitcast.33), calls=%async_computation | async-start | bytes 1441792 | tf_op jit(solution)/shard_map/all_to_all | solution.py:581
  58.4 0.9 copy-start.1
  70.4 1.1 copy-start.2
  71.5 1.1 copy-start.3
  72.7 1.6 %copy-start.4 = (bf16[176,5632]{1,0:T(8,128)(2,1)S(1)}, bf16[176,5632]{1,0:T(8,128)(2,1)}, u32[]{:S(2)}) copy-start(bf16[176,5632]{1,0:T(8,128)(2,1)} %merge_weight_hbm.1) | copy-start | bytes 5947396
Sparse Core Ops, SparseCore 0:
  16.0 54.3 all-gather.2

commit v3 on v2

v3 whole, which is shorter than its diff:
```python
import functools
import math

import jax
import jax.numpy as jnp
from jax import lax
from jax.experimental import pallas as pl
from jax.experimental.pallas import tpu as pltpu
from jax.sharding import PartitionSpec as P

HEAD_DIM = 88
QB = 256
KB = 256
NEAR = 2
NEG = -1e30
MESH = pl.DeviceIdType.MESH


def tile_step(kt, v0, v1, qcat, ok, coef, row, m_ref, l_ref, acc_ref):
    scores = lax.dot_general(
        kt, qcat, (((1,), (0,)), ((), ())), preferred_element_type=jnp.float32
    )
    width = qcat.shape[1] // 2
    for head in range(2):
        part = jnp.where(ok, scores[:, head * width : (head + 1) * width], NEG)
        old = m_ref[row + head]
        new = jnp.maximum(old, jnp.max(part, axis=0, keepdims=True))
        fade = jnp.exp2((old - new) * coef)
        expo = jnp.exp2(part * coef - new * coef)
        l_ref[row + head] = l_ref[row + head] * fade + jnp.sum(expo, axis=0, keepdims=True)
        m_ref[row + head] = new
        values = v1 if head else v0
        acc_ref[row + head] = acc_ref[row + head] * fade + lax.dot_general(
            values,
            expo.astype(jnp.bfloat16),
            (((1,), (0,)), ((), ())),
            preferred_element_type=jnp.float32,
        )


def split_heads(values):
    wide = values.astype(jnp.float32)
    return wide[:HEAD_DIM].astype(jnp.bfloat16), wide[HEAD_DIM:].astype(jnp.bfloat16)


def query_pair(block):
    feature = lax.broadcasted_iota(jnp.int32, block.shape, 0)
    zero = jnp.zeros_like(block)
    return jnp.concatenate(
        [jnp.where(feature < HEAD_DIM, block, zero), jnp.where(feature < HEAD_DIM, zero, block)],
        axis=1,
    )


def head_kernel(
    rows,
    cols,
    coef,
    qkv_hbm,
    residual_hbm,
    merge_weight_hbm,
    groups_line_ref,
    groups_column_ref,
    left_hbm,
    right_hbm,
    spread_hbm,
    far_hbm,
    m_ref,
    l_ref,
    acc_ref,
    kt,
    vt,
    bound_ref,
    qkv,
    load_sem,
    halo_send,
    halo_recv,
    res_send,
    res_recv,
    far_send,
    far_recv,
):
    row = lax.axis_index("row")
    me = lax.axis_index("col")
    _, width, tokens = qkv.shape
    reach = left_hbm.shape[2]
    blocks = tokens // QB
    chunk = tokens // cols
    full = spread_hbm.shape[0]
    barrier = pltpu.get_barrier_semaphore()
    after = (row + 1) % rows
    before = (row + rows - 1) % rows
    for other in (after, before):
        pl.semaphore_signal(barrier, inc=1, device_id={"row": other}, device_id_type=MESH)
    for k in range(1, cols):
        pl.semaphore_signal(
            barrier, inc=1, device_id={"col": (me + k) % cols}, device_id_type=MESH
        )
    loads = [
        pltpu.make_async_copy(qkv_hbm.at[i], qkv.at[i], load_sem.at[i]) for i in range(3)
    ]
    for load in loads:
        load.start()
    mine = pl.ds(pl.multiple_of(me * chunk, chunk), chunk)
    place = pl.ds(pl.multiple_of(me * width, 16), width)
    keep = pltpu.make_async_copy(residual_hbm.at[:, mine], spread_hbm.at[place], load_sem.at[3])
    keep.start()
    pl.semaphore_wait(barrier, cols + 1)

    sent = []
    for side, (other, target, at) in enumerate(
        ((after, left_hbm, tokens - reach), (before, right_hbm, 0))
    ):
        for i in range(2):
            sent.append(
                pltpu.make_async_remote_copy(
                    src_ref=qkv_hbm.at[1 + i, :, at : at + reach],
                    dst_ref=target.at[i],
                    send_sem=halo_send.at[2 * side + i],
                    recv_sem=halo_recv.at[2 * side + i],
                    device_id={"row": other},
                    device_id_type=MESH,
                )
            )
    for k in range(1, cols):
        to = (me + k) % cols
        sent.append(
            pltpu.make_async_remote_copy(
                src_ref=residual_hbm.at[:, pl.ds(pl.multiple_of(to * chunk, chunk), chunk)],
                dst_ref=spread_hbm.at[place],
                send_sem=res_send.at[k],
                recv_sem=res_recv.at[k],
                device_id={"col": to},
                device_id_type=MESH,
            )
        )
    part = row // (rows // 4)
    sent.append(
        pltpu.make_async_remote_copy(
            src_ref=merge_weight_hbm.at[:, pl.ds(pl.multiple_of(part * full, 128), full)],
            dst_ref=far_hbm,
            send_sem=far_send,
            recv_sem=far_recv,
            device_id={"col": (me + cols // 2) % cols},
            device_id_type=MESH,
        )
    )
    for copy in sent:
        copy.start()

    images = groups_line_ref.shape[1]
    first = lax.broadcasted_iota(jnp.int32, (images, images), 0)
    second = lax.broadcasted_iota(jnp.int32, (images, images), 1)
    size = groups_column_ref[...] * 4
    begin = (
        jnp.sum(
            jnp.where(second < first, groups_line_ref[...], 0), axis=1, keepdims=True
        )
        * 4
        - row * tokens
    )
    for load in loads:
        load.wait()

    def prepare(b, carry):
        at = pl.multiple_of(b * QB, QB)
        token = lax.broadcasted_iota(jnp.int32, (images, QB), 1) + at
        inside = (token >= begin) & (token < begin + size)
        bound_ref[0:1, pl.ds(at, QB)] = jnp.sum(jnp.where(inside, begin, 0), axis=0, keepdims=True)
        bound_ref[1:2, pl.ds(at, QB)] = jnp.sum(jnp.where(inside, size, 0), axis=0, keepdims=True)
        kt[pl.ds(at, QB), :] = jnp.transpose(qkv[1, :, pl.ds(at, QB)])
        v0, v1 = split_heads(qkv[2, :, pl.ds(at, QB)])
        vt[0, :, pl.ds(at, QB)] = v0
        vt[1, :, pl.ds(at, QB)] = v1
        return carry

    lax.fori_loop(0, blocks, prepare, 0)

    def per_block(b, carry):
        at = pl.multiple_of(b * QB, QB)
        qcat = query_pair(qkv[0, :, pl.ds(at, QB)])
        start = bound_ref[0:1, pl.ds(at, QB)]
        length = bound_ref[1:2, pl.ds(at, QB)]
        row_at = b * 2
        for head in range(2):
            m_ref[row_at + head] = jnp.full((1, QB), NEG, jnp.float32)
            l_ref[row_at + head] = jnp.zeros((1, QB), jnp.float32)
            acc_ref[row_at + head] = jnp.zeros((HEAD_DIM, QB), jnp.float32)

        def per_tile(t, inner):
            key = pl.multiple_of(t * KB, KB)
            spot = lax.broadcasted_iota(jnp.int32, (KB, QB), 0) + (key - start)
            ok = (spot >= 0) & (spot < length)
            tile_step(
                kt[pl.ds(key, KB), :],
                vt[0, :, pl.ds(key, KB)],
                vt[1, :, pl.ds(key, KB)],
                qcat,
                ok,
                coef,
                row_at,
                m_ref,
                l_ref,
                acc_ref,
            )
            return inner

        lax.fori_loop(
            jnp.maximum(b - NEAR, 0), jnp.minimum(b + NEAR + 1, blocks), per_tile, 0
        )
        return carry

    lax.fori_loop(0, blocks, per_block, 0)
    keep.wait()
    for copy in sent:
        copy.wait()


def far_kernel(
    coef,
    groups_ref,
    row_ref,
    q_ref,
    left_ref,
    right_ref,
    bound_ref,
    m_in,
    l_in,
    acc_in,
    kt_in,
    vt_in,
    out_ref,
    low_ref,
    high_ref,
    kt,
    vt,
    m_ref,
    l_ref,
    acc_ref,
    sem,
):
    reach = left_ref.shape[2]
    width, tokens = q_ref.shape
    blocks = tokens // QB
    base = row_ref[0] * tokens
    moves = [
        pltpu.make_async_copy(kt_in, kt.at[reach : reach + tokens], sem.at[0]),
        pltpu.make_async_copy(vt_in, vt.at[:, :, reach : reach + tokens], sem.at[1]),
    ]
    for move in moves:
        move.start()

    def find(b, state):
        image, begin = state
        token = base + b * QB

        def past(at):
            def more(s):
                return s[1] + groups_ref[s[0]] * 4 <= at

            def step(s):
                return s[0] + 1, s[1] + groups_ref[s[0]] * 4

            return more, step

        image, begin = lax.while_loop(*past(token), (image, begin))
        low_ref[b] = begin - base
        image, begin = lax.while_loop(*past(token + QB - 1), (image, begin))
        high_ref[b] = begin + groups_ref[image] * 4 - base
        return image, begin

    lax.fori_loop(0, blocks, find, (jnp.int32(0), jnp.int32(0)))
    for i in range(reach // KB):
        for needed, source, at in (
            (low_ref[0] < (i + 1) * KB - reach, left_ref, 0),
            (high_ref[blocks - 1] > tokens + i * KB, right_ref, reach + tokens),
        ):

            @pl.when(needed)
            def _():
                span = slice(i * KB, (i + 1) * KB)
                to = slice(at + i * KB, at + (i + 1) * KB)
                kt[to, :] = jnp.transpose(source[0, :, span])
                v0, v1 = split_heads(source[1, :, span])
                vt[0, :, to] = v0
                vt[1, :, to] = v1

    for move in moves:
        move.wait()

    def per_block(b, carry):
        at = pl.multiple_of(b * QB, QB)
        row_at = b * 2
        near_low = jnp.maximum(b - NEAR, 0) * QB
        near_high = jnp.minimum(b + NEAR + 1, blocks) * QB
        below = jnp.maximum((near_low - low_ref[b] + KB - 1) // KB, 0)
        above = jnp.maximum((high_ref[b] - near_high + KB - 1) // KB, 0)
        for head in range(2):
            m_ref[head] = m_in[row_at + head]
            l_ref[head] = l_in[row_at + head]
            acc_ref[head] = acc_in[row_at + head]

        @pl.when(below + above > 0)
        def _():
            qcat = query_pair(q_ref[:, pl.ds(at, QB)])
            start = bound_ref[0:1, pl.ds(at, QB)]
            length = bound_ref[1:2, pl.ds(at, QB)]

            def per_tile(t, inner):
                key = jnp.where(
                    t < below, near_low - (t + 1) * KB, near_high + (t - below) * KB
                )
                spot = lax.broadcasted_iota(jnp.int32, (KB, QB), 0) + (key - start)
                ok = (spot >= 0) & (spot < length)
                slot = pl.multiple_of(key + reach, KB)
                tile_step(
                    kt[pl.ds(slot, KB), :],
                    vt[0, :, pl.ds(slot, KB)],
                    vt[1, :, pl.ds(slot, KB)],
                    qcat,
                    ok,
                    coef,
                    0,
                    m_ref,
                    l_ref,
                    acc_ref,
                )
                return inner

            lax.fori_loop(0, below + above, per_tile, 0)

        both = [acc_ref[head] / l_ref[head] for head in range(2)]
        out_ref[:, pl.ds(at, QB)] = jnp.concatenate(both, axis=0).astype(jnp.bfloat16)
        return carry

    lax.fori_loop(0, blocks, per_block, 0)


def attention(qkv, residual, merge_weight, image_groups, row_id, full, rows, cols):
    _, width, tokens = qkv.shape
    reach = tokens // 2
    blocks = tokens // QB
    chunk = tokens // cols
    bf16, f32 = jnp.bfloat16, jnp.float32
    coef = math.log2(math.e) / math.sqrt(HEAD_DIM)
    smem = pl.BlockSpec(memory_space=pltpu.SMEM)
    vmem = pl.BlockSpec(memory_space=pltpu.VMEM)
    hbm = pl.BlockSpec(memory_space=pl.ANY)
    dma = pltpu.SemaphoreType.DMA
    halo = jax.ShapeDtypeStruct((2, width, reach), bf16)
    stat = jax.ShapeDtypeStruct((2 * blocks, 1, QB), f32)
    left, right, spread, far, m, l, acc, kt, vt, bound = pl.pallas_call(
        functools.partial(head_kernel, rows, cols, coef),
        out_shape=(
            halo,
            halo,
            jax.ShapeDtypeStruct((full, chunk), bf16),
            jax.ShapeDtypeStruct((width, full), bf16),
            stat,
            stat,
            jax.ShapeDtypeStruct((2 * blocks, HEAD_DIM, QB), f32),
            jax.ShapeDtypeStruct((tokens, width), bf16),
            jax.ShapeDtypeStruct((2, HEAD_DIM, tokens), bf16),
            jax.ShapeDtypeStruct((8, tokens), jnp.int32),
        ),
        in_specs=[hbm, hbm, hbm, vmem, vmem],
        out_specs=(hbm, hbm, hbm, hbm, vmem, vmem, vmem, vmem, vmem, vmem),
        scratch_shapes=[
            pltpu.VMEM((3, width, tokens), bf16),
            dma((4,)),
            dma((4,)),
            dma((4,)),
            dma((cols,)),
            dma((cols,)),
            dma,
            dma,
        ],
        compiler_params=pltpu.CompilerParams(
            collective_id=1, has_side_effects=True, vmem_limit_bytes=56 << 20
        ),
    )(qkv, residual, merge_weight, image_groups[None, :], image_groups[:, None])
    attended = pl.pallas_call(
        functools.partial(far_kernel, coef),
        out_shape=jax.ShapeDtypeStruct((width, tokens), bf16),
        in_specs=[smem, smem] + [vmem] * 7 + [hbm] * 2,
        out_specs=vmem,
        scratch_shapes=[
            pltpu.SMEM((blocks,), jnp.int32),
            pltpu.SMEM((blocks,), jnp.int32),
            pltpu.VMEM((2 * reach + tokens, width), bf16),
            pltpu.VMEM((2, HEAD_DIM, 2 * reach + tokens), bf16),
            pltpu.VMEM((2, 1, QB), f32),
            pltpu.VMEM((2, 1, QB), f32),
            pltpu.VMEM((2, HEAD_DIM, QB), f32),
            dma((2,)),
        ],
        compiler_params=pltpu.CompilerParams(vmem_limit_bytes=56 << 20),
    )(image_groups, row_id[None], qkv[0], left, right, bound, m, l, acc, kt, vt)
    return attended, spread, far


def tail_kernel(
    rows,
    cols,
    attended_ref,
    residual_ref,
    out_weight_hbm,
    merge_weight_hbm,
    far_weight_hbm,
    gain_ref,
    dest_line_ref,
    dest_column_ref,
    layer_ref,
    image_ref,
    att,
    weight,
    weight_t,
    merge_w,
    layer_rows,
    held,
    far_rows,
    merged,
    pick,
    sorted_rows,
    got_rows,
    load_sem,
    spread_send,
    spread_recv,
    back_send,
    back_recv,
    near_send,
    near_recv,
    sib_send,
    sib_recv,
    far_send,
    far_recv,
    row_send,
    row_recv,
    far_w_send,
    far_w_recv,
    gain_column,
):
    row = lax.axis_index("row")
    me = lax.axis_index("col")
    width, tokens = attended_ref.shape
    full = weight.shape[0]
    chunk = tokens // cols
    part = chunk // 4
    groups = tokens // 4
    share = groups // rows
    chips = cols // 2
    core = me % 2
    chip = me // 2
    sibling = me + 1 - 2 * core
    half = full // 2

    barrier = pltpu.get_barrier_semaphore()
    for k in range(1, cols):
        pl.semaphore_signal(
            barrier, inc=1, device_id={"col": (me + k) % cols}, device_id_type=MESH
        )
    for k in range(1, rows):
        pl.semaphore_signal(
            barrier, inc=1, device_id={"row": (row + k) % rows}, device_id_type=MESH
        )
    loads = [
        pltpu.make_async_copy(out_weight_hbm, weight, load_sem.at[0]),
        pltpu.make_async_copy(merge_weight_hbm, merge_w.at[0:width], load_sem.at[1]),
    ]
    line_up = rows // 4
    part_at = row // line_up
    far_at = pl.ds(pl.multiple_of(part_at * full, 128), full)
    far_place = merge_w.at[width : 2 * width, far_at]
    loads.append(pltpu.make_async_copy(far_weight_hbm, far_place, load_sem.at[2]))
    for load in loads:
        load.start()
    pl.semaphore_wait(barrier, rows + cols - 2)

    spread = []
    for k in range(1, cols):
        to = (me + k) % cols
        copy = pltpu.make_async_remote_copy(
            src_ref=attended_ref.at[:, pl.ds(pl.multiple_of(to * chunk, chunk), chunk)],
            dst_ref=att.at[pl.ds(pl.multiple_of(me * width, 16), width)],
            send_sem=spread_send.at[k],
            recv_sem=spread_recv.at[k],
            device_id={"col": to},
            device_id_type=MESH,
        )
        copy.start()
        spread.append(copy)
    gather = []
    for k in range(1, 4):
        copy = pltpu.make_async_remote_copy(
            src_ref=far_weight_hbm,
            dst_ref=far_place,
            send_sem=far_w_send.at[k],
            recv_sem=far_w_recv.at[k],
            device_id={"row": (row + k * line_up) % rows},
            device_id_type=MESH,
        )
        copy.start()
        gather.append(copy)
    mine = pl.ds(pl.multiple_of(me * chunk, chunk), chunk)
    att[pl.ds(pl.multiple_of(me * width, 16), width), :] = attended_ref[:, mine]

    line = dest_line_ref[...]
    owner_line = line // groups
    owner_column = dest_column_ref[...] // groups
    down = lax.broadcasted_iota(jnp.int32, (groups, groups), 0)
    across = lax.broadcasted_iota(jnp.int32, (groups, groups), 1)
    earlier = (owner_column == owner_line) & (down < across)
    rank = jnp.sum(earlier.astype(jnp.int32), axis=0, keepdims=True)
    spot = owner_line * share + rank
    pick[...] = jnp.where(down == spot, 1.0, 0.0).astype(jnp.bfloat16)
    slot = line % groups
    extra = merged.shape[0] - width
    which = lax.broadcasted_iota(jnp.int32, (extra, groups), 0)
    digits = jnp.where(which == 0, slot // 16, jnp.where(which == 1, slot % 16, 0))
    merged[width:, :] = digits.astype(jnp.float32).astype(jnp.bfloat16)

    loads[0].wait()

    def turn(i, carry):
        at = pl.multiple_of(i * 128, 128)
        weight_t[pl.ds(at, 128), :] = jnp.transpose(weight[:, pl.ds(at, 128)])
        return carry

    lax.fori_loop(0, full // 128, turn, 0)
    gain_wide = jnp.broadcast_to(gain_ref[...], (8, full))
    gain_column[...] = jnp.transpose(gain_wide)
    for load in loads[1:]:
        load.wait()

    for copy in spread:
        copy.wait()
    strip = full // 4
    for i in range(4):
        at = i * strip
        projected = jnp.dot(
            weight_t[at : at + strip, :], att[...], preferred_element_type=jnp.float32
        )
        layer_rows[at : at + strip, :] = (
            residual_ref[at : at + strip, :].astype(jnp.float32) + projected
        ).astype(jnp.bfloat16)

    values32 = layer_rows[...].astype(jnp.float32)
    centre = jnp.sum(values32, axis=0, keepdims=True) * (1.0 / full)
    spread_of = jnp.sum(jnp.square(values32 - centre), axis=0, keepdims=True) * (1.0 / full)
    scale = lax.rsqrt(spread_of + 1e-06)
    normed = ((values32 - centre) * scale * gain_column[:, 0:1]).astype(jnp.bfloat16)
    here = lax.broadcasted_iota(jnp.int32, (chunk, chunk), 0)
    there = lax.broadcasted_iota(jnp.int32, (chunk, chunk), 1)
    order = jnp.where((here % 4) * part + here // 4 == there, 1.0, 0.0).astype(jnp.bfloat16)
    held[core] = jnp.dot(normed, order, preferred_element_type=jnp.float32).astype(jnp.bfloat16)

    goal = (chip + 1 + 2 * core) % chips
    near = []
    for h in range(2):
        span = pl.ds(h * half, half)
        copy = pltpu.make_async_remote_copy(
            src_ref=held.at[core, span],
            dst_ref=held.at[2 + core, span],
            send_sem=near_send.at[h],
            recv_sem=near_recv.at[core],
            device_id={"col": goal * 2 + h},
            device_id_type=MESH,
        )
        copy.start()
        near.append(copy)
    own = pltpu.make_async_remote_copy(
        src_ref=held.at[core],
        dst_ref=held.at[core],
        send_sem=sib_send.at[0],
        recv_sem=sib_recv.at[0],
        device_id={"col": sibling},
        device_id_type=MESH,
    )
    own.start()

    passed = []
    my_half = pl.ds(pl.multiple_of(core * half, 16), half)
    for s in range(2):
        arrive = pltpu.make_async_remote_copy(
            src_ref=held.at[core, my_half],
            dst_ref=held.at[2 + s, my_half],
            send_sem=near_send.at[s],
            recv_sem=near_recv.at[s],
            device_id={"col": sibling},
            device_id_type=MESH,
        )
        arrive.wait_recv()
        copy = pltpu.make_async_remote_copy(
            src_ref=held.at[2 + s, my_half],
            dst_ref=held.at[2 + s, my_half],
            send_sem=sib_send.at[1 + s],
            recv_sem=sib_recv.at[1 + s],
            device_id={"col": sibling},
            device_id_type=MESH,
        )
        copy.start()
        passed.append(copy)
    for copy in near:
        copy.wait_send()
    own.wait()
    for copy in passed:
        copy.wait()

    back = []
    for k in range(1, cols):
        to = (me + k) % cols
        copy = pltpu.make_async_remote_copy(
            src_ref=layer_rows.at[pl.ds(pl.multiple_of(to * width, 16), width)],
            dst_ref=layer_ref.at[:, mine],
            send_sem=back_send.at[k],
            recv_sem=back_recv.at[k],
            device_id={"col": to},
            device_id_type=MESH,
        )
        copy.start()
        back.append(copy)
    layer_ref[:, mine] = layer_rows[pl.ds(pl.multiple_of(me * width, 16), width), :]
    for copy in gather:
        copy.wait()

    total = None
    for j in range(4):
        side = jnp.concatenate(
            [held[s, :, j * part : (j + 1) * part] for s in range(4)], axis=1
        )
        term = jnp.dot(
            merge_w[:, j * full : (j + 1) * full], side, preferred_element_type=jnp.float32
        )
        total = term if total is None else total + term
    far_rows[...] = total[width:].astype(jnp.bfloat16)
    across_y = pltpu.make_async_remote_copy(
        src_ref=far_rows,
        dst_ref=merged.at[0:width, chunk : 2 * chunk],
        send_sem=far_send,
        recv_sem=far_recv,
        device_id={"col": (me + cols // 2) % cols},
        device_id_type=MESH,
    )
    across_y.start()
    merged[0:width, 0:chunk] = total[:width].astype(jnp.bfloat16)
    across_y.wait()

    sorted_rows[...] = lax.dot_general(
        pick[...], merged[...], (((1,), (1,)), ((), ())), preferred_element_type=jnp.float32
    ).astype(jnp.bfloat16)
    moves = []
    for k in range(1, rows):
        to = (row + k) % rows
        copy = pltpu.make_async_remote_copy(
            src_ref=sorted_rows.at[pl.ds(pl.multiple_of(to * share, share), share)],
            dst_ref=got_rows.at[pl.ds(pl.multiple_of(row * share, share), share)],
            send_sem=row_send.at[k],
            recv_sem=row_recv.at[k],
            device_id={"row": to},
            device_id_type=MESH,
        )
        copy.start()
        moves.append(copy)
    keep = pl.ds(pl.multiple_of(row * share, share), share)
    got_rows[keep, :] = sorted_rows[keep, :]
    for copy in moves:
        copy.wait()
    got = got_rows[...]
    target = got[:, width : width + 1].astype(jnp.float32) * 16.0 + got[
        :, width + 1 : width + 2
    ].astype(jnp.float32)
    put = jnp.where(target == across.astype(jnp.float32), 1.0, 0.0).astype(jnp.bfloat16)
    image_ref[...] = lax.dot_general(
        got, put, (((0,), (0,)), ((), ())), preferred_element_type=jnp.float32
    )[:width].astype(jnp.bfloat16)
    for copy in back:
        copy.wait()


def tail(attended, residual, out_weight, merge_weight, far_weight, gain, dest_slots, rows, cols):
    width, tokens = attended.shape
    full = out_weight.shape[0]
    chunk = tokens // cols
    groups = tokens // 4
    bf16 = jnp.bfloat16
    vmem = pl.BlockSpec(memory_space=pltpu.VMEM)
    hbm = pl.BlockSpec(memory_space=pl.ANY)
    dma = pltpu.SemaphoreType.DMA
    return pl.pallas_call(
        functools.partial(tail_kernel, rows, cols),
        out_shape=(
            jax.ShapeDtypeStruct((width, tokens), bf16),
            jax.ShapeDtypeStruct((width, groups), bf16),
        ),
        in_specs=[vmem, vmem, hbm, hbm, hbm, vmem, vmem, vmem],
        out_specs=(vmem, vmem),
        scratch_shapes=[
            pltpu.VMEM((full, chunk), bf16),
            pltpu.VMEM((full, full), bf16),
            pltpu.VMEM((full, full), bf16),
            pltpu.VMEM((2 * width, merge_weight.shape[1]), bf16),
            pltpu.VMEM((full, chunk), bf16),
            pltpu.VMEM((4, full, chunk), bf16),
            pltpu.VMEM((width, chunk), bf16),
            pltpu.VMEM((width + 16, groups), bf16),
            pltpu.VMEM((groups, groups), bf16),
            pltpu.VMEM((groups, width + 16), bf16),
            pltpu.VMEM((groups, width + 16), bf16),
            dma((3,)),
            dma((cols,)),
            dma((cols,)),
            dma((cols,)),
            dma((cols,)),
            dma((2,)),
            dma((2,)),
            dma((3,)),
            dma((3,)),
            dma,
            dma,
            dma((rows,)),
            dma((rows,)),
            dma((4,)),
            dma((4,)),
            pltpu.VMEM((full, 8), jnp.float32),
        ],
        compiler_params=pltpu.CompilerParams(
            collective_id=0, has_side_effects=True, vmem_limit_bytes=60 << 20
        ),
        cost_estimate=pl.CostEstimate(
            flops=8 * full * full * chunk, bytes_accessed=16 << 20, transcendentals=0
        ),
    )(
        attended,
        residual,
        out_weight,
        merge_weight,
        far_weight,
        gain[None, :],
        dest_slots[None, :],
        dest_slots[:, None],
    )


def body(qkv, residual_in, out_weight, merge_weight, merge_gain, image_groups, dest_row):
    rows = lax.axis_size("row")
    cols = lax.axis_size("col")
    row_id = lax.axis_index("row")
    col_id = lax.axis_index("col")

    chips = cols // 2
    chip = col_id // 2
    before, after, across = (chip + chips - 1) % chips, (chip + 1) % chips, (chip + 2) % chips
    met = jnp.stack(
        [
            2 * chip,
            2 * chip + 1,
            2 * before,
            2 * after + 1,
            2 * across,
            2 * across + 1,
            2 * after,
            2 * before + 1,
        ]
    )
    dest_slots = jnp.take(dest_row.reshape(cols, -1), met, axis=0).reshape(-1)

    attended, residual, far_weight = attention(
        qkv, residual_in, merge_weight, image_groups, row_id, out_weight.shape[0], rows, cols
    )
    return tail(
        attended, residual, out_weight, merge_weight, far_weight, merge_gain, dest_slots, rows, cols
    )


def solution(mesh):
    return jax.shard_map(
        body,
        mesh=mesh,
        in_specs=(P(None, "col", "row"), P("col", "row"), P(), P("col", None), P(), P(), P("row")),
        out_specs=(P("col", "row"), P("col", "row")),
        check_vma=False,
    )
```

time: 131 us -> 102 us (0.78); the launches traced: 129 us -> 102 us
  Pallas kernels: 72.1 us -> 90.9 us
  waiting for transfers between devices: 14.8 us -> 0 us
  between operations: 14.2 us -> 0.69 us
  starting transfers between devices: 13.2 us -> 0 us
  local copies, waits for them, and re-layouts: 13.9 us -> 10 us
    pallas_call x2, Pallas kernels: 25.8 us -> 42.1 us  [the longest x1 31.3 us: attention(): pl.pallas_call(functools.partial(head_kernel, rows, cols, coef), out_shap...]
    all_gather x1 -> x0, waiting for transfers between devices: 11.2 us -> none  [body(): far_weight = lax.all_gather(slice_far, 'row', axis=0)]
    ppermute x3 -> x0, starting transfers between devices: 8.69 us -> none  [the longest x1 4.04 us: body(): lax.ppermute(qkv[1:, :, tok_rows - reach:], 'row', [(i, i + 1) for i in r...]
    all_to_all x1 -> x0, starting transfers between devices: 4.47 us -> none  [body(): residual = lax.all_to_all(residual_in, 'col', 1, 0, tiled=True)]
    ppermute x3 -> x0, waiting for transfers between devices: 3.59 us -> none  [the longest x1 3.58 us: body(): lax.ppermute(slice_here, 'col', [(i, (i + cols // 2) % cols) for i in ran...]
    unnamed x22 -> x6, local copies, waits for them, and re-layouts: 6.83 us -> 3.66 us
    slice x3 -> x0, local copies, waits for them, and re-layouts: 2.79 us -> none  [the longest x1 2.61 us: body(): qkv[1:, :, :reach]]
    pallas_call x1, Pallas kernels: 46.3 us -> 48.8 us  [tail(): pl.pallas_call(functools.partial(tail_kernel, rows, cols), out_shape=(jax...]
  transfers between devices with their start and end apart: 5 -> 0, of which waited for: 2 -> 0; matrix products, arithmetic and copies ran while one was open for 5% -> 0% of each run, Pallas kernels for 20% -> 0%
where the time goes in v3:
time: 102 us
  Pallas kernels  90.9 us (89%)
  local copies, waits for them, and re-layouts  10 us (10%)
    pallas_call x1, Pallas kernels, tail(): pl.pallas_call(functools.partial(tail_kernel, rows, cols), out_shape=(jax...  48.8 us
    pallas_call x1, Pallas kernels, attention(): pl.pallas_call(functools.partial(head_kernel, rows, cols, coef), out_shap...  31.3 us
    pallas_call x1, Pallas kernels, attention(): pl.pallas_call(functools.partial(far_kernel, coef), out_shape=jax.ShapeDt...  10.7 us
    unnamed x6, local copies, waits for them, and re-layouts  3.66 us
    squeeze x1, local copies, waits for them, and re-layouts, attention(): qkv[0]  2.04 us

profile of v3, /device:TPU:0, one launch (start us, length us, event | category | flops | bytes accessed | tf_op | source)
XLA Modules:
  0.0 101.7 jit_solution(8953638062183244537)
XLA Ops:
  0.6 2.0 %slice_bitcast_fusion.q_ref = bf16[176,2048]{1,0:T(8,128)(2,1)} fusion(bf16[3,176,2048]{2,1,0:T(8,128)(2,1)} %qkv_hbm.1), kind=kLoop, calls=%fused_computation.1 | loop fusion | bytes 1441792 | tf_op jit(solution)/shard_map/squeeze | solution.py:398
  2.7 1.4 %copy.10.groups_column_ref = s32[64,1]{1,0:T(8,128)} copy(s32[64,1]{0,1:T(1,128)} %bitcast.23) | data formatting | bytes 512 | tf_op jit(solution)/shard_map/broadcast_in_dim | solution.py:381
  4.0 31.3 %shard_map.86 = (bf16[2,176,1024]{2,1,0:T(8,128)(2,1)}, bf16[2,176,1024]{2,1,0:T(8,128)(2,1)}, bf16[1408,256]{1,0:T(8,128)(2,1)}, bf16[176,1408]{1,0:T(8,128)(2,...) custom-call(bf16[3,176,2048]{2,1,0:T(8,128)(2,1)} %qkv_hbm.1, ...), custom_call_target="tpu_custom_call" | custom-call | tf_op jit(solution)/shard_map/pallas_call | solution.py:352
  35.4 0.0 copy-start
  35.4 0.0 copy-start.1
  35.4 10.7 %shard_map.87.attended_ref = bf16[176,2048]{1,0:T(8,128)(2,1)} custom-call(s32[64]{0:T(128)} %groups_ref.1, s32[1]{0:T(128)} %bitcast.row_ref, bf16[176,2048]{1,0:T(8,128)(2,1)} %slice_bitcast_fusion.q_ref, bf16[2,176,1024]{2,1,0:T(8,128)(2,1)} %get-tuple-element.12.left_ref, bf16[2,176,1024]{2,1,0:T(8,128)(2,1)} %get-tuple-element.13.right_ref, ...), custom_call_target="tpu_custom_call" | custom-call | tf_op jit(solution)/shard_map/pallas_call | solution.py:382
  46.1 0.0 copy-done
  46.1 0.6 broadcast_in_dim.25.gain_ref
  46.7 0.0 copy-done.1
  46.7 0.1 reshape.398
  46.8 0.1 stack.62
  46.9 0.6 gather_fusion
  47.5 0.1 stack.53
  47.6 0.1 broadcast_select_fusion
  47.7 0.6 select_n.66.dest_line_ref
  48.3 0.9 select_n.68.dest_column_ref
  49.2 48.8 %shard_map.88 = (bf16[176,2048]{1,0:T(8,128)(2,1)}, bf16[176,512]{1,0:T(8,128)(2,1)}) custom-call(bf16[176,2048]{1,0:T(8,128)(2,1)} %shard_map.87.attended_ref, bf16[1408,256]{1,0:T(8,128)(2,1)} %get-tuple-element.20.residual_ref, bf16[1408,1408]{1,0:T(8,128)(2,1)} %out_weight_hbm.1, bf16[176,5632]{1,0:T(8,128)(2,1)} %merge_weight_hbm.3, ...), custom_call_target="tpu_custom_call" | custom-call | flops 4060086272 | bytes 16777216 | tf_op jit(solution)/shard_map/pallas_call | solution.py:689
  98.0 2.0 %copy.14 = bf16[176,2048]{1,0:T(8,128)(2,1)} copy(bf16[176,2048]{1,0:T(8,128)(2,1)} %get-tuple-element.24) | data formatting | bytes 1441792
  100.1 1.6 %copy.15 = bf16[176,512]{1,0:T(8,128)(2,1)} copy(bf16[176,512]{1,0:T(8,128)(2,1)} %get-tuple-element.25) | data formatting | bytes 360448
  (3 shorter events, 0.0 us)
Async XLA Ops:
  35.4 10.8 %copy-start = (f32[1408]{0:T(1024)S(1)}, f32[1408]{0:T(1024)}, u32[]{:S(2)}) copy-start(f32[1408]{0:T(1024)} %param.11) | copy-start | bytes 16900
  35.4 11.4 %copy-start.1 = (s32[512]{0:T(512)S(1)}, s32[512]{0:T(512)}, u32[]{:S(2)}) copy-start(s32[512]{0:T(512)} %param.13) | copy-start | bytes 6148

commit v4 on v3

--- a/solution.py
+++ b/solution.py
@@ -60,7 +60,6 @@
     residual_hbm,
     merge_weight_hbm,
     groups_line_ref,
-    groups_column_ref,
     left_hbm,
     right_hbm,
     spread_hbm,
@@ -151,7 +150,9 @@
     images = groups_line_ref.shape[1]
     first = lax.broadcasted_iota(jnp.int32, (images, images), 0)
     second = lax.broadcasted_iota(jnp.int32, (images, images), 1)
-    size = groups_column_ref[...] * 4
+    size = (
+        jnp.sum(jnp.where(second == first, groups_line_ref[...], 0), axis=1, keepdims=True) * 4
+    )
     begin = (
         jnp.sum(
             jnp.where(second < first, groups_line_ref[...], 0), axis=1, keepdims=True
@@ -220,7 +221,7 @@
     coef,
     groups_ref,
     row_ref,
-    q_ref,
+    qkv_hbm,
     left_ref,
     right_ref,
     bound_ref,
@@ -237,6 +238,7 @@
     m_ref,
     l_ref,
     acc_ref,
+    q_ref,
     sem,
 ):
     reach = left_ref.shape[2]
@@ -246,6 +248,7 @@
     moves = [
         pltpu.make_async_copy(kt_in, kt.at[reach : reach + tokens], sem.at[0]),
         pltpu.make_async_copy(vt_in, vt.at[:, :, reach : reach + tokens], sem.at[1]),
+        pltpu.make_async_copy(qkv_hbm.at[0], q_ref, sem.at[2]),
     ]
     for move in moves:
         move.start()
@@ -363,7 +366,7 @@
             jax.ShapeDtypeStruct((2, HEAD_DIM, tokens), bf16),
             jax.ShapeDtypeStruct((8, tokens), jnp.int32),
         ),
-        in_specs=[hbm, hbm, hbm, vmem, vmem],
+        in_specs=[hbm, hbm, hbm, vmem],
         out_specs=(hbm, hbm, hbm, hbm, vmem, vmem, vmem, vmem, vmem, vmem),
         scratch_shapes=[
             pltpu.VMEM((3, width, tokens), bf16),
@@ -378,11 +381,11 @@
         compiler_params=pltpu.CompilerParams(
             collective_id=1, has_side_effects=True, vmem_limit_bytes=56 << 20
         ),
-    )(qkv, residual, merge_weight, image_groups[None, :], image_groups[:, None])
+    )(qkv, residual, merge_weight, image_groups[None, :])
     attended = pl.pallas_call(
         functools.partial(far_kernel, coef),
         out_shape=jax.ShapeDtypeStruct((width, tokens), bf16),
-        in_specs=[smem, smem] + [vmem] * 7 + [hbm] * 2,
+        in_specs=[smem, smem, hbm] + [vmem] * 6 + [hbm] * 2,
         out_specs=vmem,
         scratch_shapes=[
             pltpu.SMEM((blocks,), jnp.int32),
@@ -392,10 +395,11 @@
             pltpu.VMEM((2, 1, QB), f32),
             pltpu.VMEM((2, 1, QB), f32),
             pltpu.VMEM((2, HEAD_DIM, QB), f32),
-            dma((2,)),
+            pltpu.VMEM((width, tokens), bf16),
+            dma((3,)),
         ],
         compiler_params=pltpu.CompilerParams(vmem_limit_bytes=56 << 20),
-    )(image_groups, row_id[None], qkv[0], left, right, bound, m, l, acc, kt, vt)
+    )(image_groups, row_id[None], qkv, left, right, bound, m, l, acc, kt, vt)
     return attended, spread, far
 
 
@@ -408,10 +412,9 @@
     merge_weight_hbm,
     far_weight_hbm,
     gain_ref,
-    dest_line_ref,
-    dest_column_ref,
+    dest_ref,
     layer_ref,
-    image_ref,
+    got_rows,
     att,
     weight,
     weight_t,
@@ -422,7 +425,6 @@
     merged,
     pick,
     sorted_rows,
-    got_rows,
     load_sem,
     spread_send,
     spread_recv,
@@ -504,9 +506,23 @@
     mine = pl.ds(pl.multiple_of(me * chunk, chunk), chunk)
     att[pl.ds(pl.multiple_of(me * width, 16), width), :] = attended_ref[:, mine]
 
-    line = dest_line_ref[...]
+    before, after, across_chip = (chip + 3) % chips, (chip + 1) % chips, (chip + 2) % chips
+    tile = 2 * part
+    lane = lax.broadcasted_iota(jnp.int32, (1, tile), 1)
+    of_chip = [dest_ref[pl.ds(c, 1), :] for c in (chip, before, across_chip, after)]
+    line = jnp.concatenate(
+        [
+            of_chip[0],
+            jnp.where(lane < part, of_chip[1], of_chip[3]),
+            of_chip[2],
+            jnp.where(lane < part, of_chip[3], of_chip[1]),
+        ],
+        axis=1,
+    )
     owner_line = line // groups
-    owner_column = dest_column_ref[...] // groups
+    owner_column = jnp.transpose(
+        jnp.broadcast_to(owner_line.astype(jnp.float32), (8, groups))
+    )[:, 0:1].astype(jnp.int32)
     down = lax.broadcasted_iota(jnp.int32, (groups, groups), 0)
     across = lax.broadcasted_iota(jnp.int32, (groups, groups), 1)
     earlier = (owner_column == owner_line) & (down < across)
@@ -527,8 +543,10 @@
         return carry
 
     lax.fori_loop(0, full // 128, turn, 0)
-    gain_wide = jnp.broadcast_to(gain_ref[...], (8, full))
-    gain_column[...] = jnp.transpose(gain_wide)
+    for i in range(full // 128):
+        gain_column[i * 128 : (i + 1) * 128, :] = jnp.transpose(
+            jnp.broadcast_to(gain_ref[i : i + 1, :], (8, 128))
+        )
     for load in loads[1:]:
         load.wait()
 
@@ -606,6 +624,29 @@
     for copy in passed:
         copy.wait()
 
+    for copy in gather:
+        copy.wait()
+
+    total = None
+    for j in range(4):
+        side = jnp.concatenate(
+            [held[s, :, j * part : (j + 1) * part] for s in range(4)], axis=1
+        )
+        term = jnp.dot(
+            merge_w[:, j * full : (j + 1) * full], side, preferred_element_type=jnp.float32
+        )
+        total = term if total is None else total + term
+    far_rows[...] = total[width:].astype(jnp.bfloat16)
+    across_y = pltpu.make_async_remote_copy(
+        src_ref=far_rows,
+        dst_ref=merged.at[0:width, chunk : 2 * chunk],
+        send_sem=far_send,
+        recv_sem=far_recv,
+        device_id={"col": (me + cols // 2) % cols},
+        device_id_type=MESH,
+    )
+    across_y.start()
+    merged[0:width, 0:chunk] = total[:width].astype(jnp.bfloat16)
     back = []
     for k in range(1, cols):
         to = (me + k) % cols
@@ -620,29 +661,6 @@
         copy.start()
         back.append(copy)
     layer_ref[:, mine] = layer_rows[pl.ds(pl.multiple_of(me * width, 16), width), :]
-    for copy in gather:
-        copy.wait()
-
-    total = None
-    for j in range(4):
-        side = jnp.concatenate(
-            [held[s, :, j * part : (j + 1) * part] for s in range(4)], axis=1
-        )
-        term = jnp.dot(
-            merge_w[:, j * full : (j + 1) * full], side, preferred_element_type=jnp.float32
-        )
-        total = term if total is None else total + term
-    far_rows[...] = total[width:].astype(jnp.bfloat16)
-    across_y = pltpu.make_async_remote_copy(
-        src_ref=far_rows,
-        dst_ref=merged.at[0:width, chunk : 2 * chunk],
-        send_sem=far_send,
-        recv_sem=far_recv,
-        device_id={"col": (me + cols // 2) % cols},
-        device_id_type=MESH,
-    )
-    across_y.start()
-    merged[0:width, 0:chunk] = total[:width].astype(jnp.bfloat16)
     across_y.wait()
 
     sorted_rows[...] = lax.dot_general(
@@ -665,19 +683,27 @@
     got_rows[keep, :] = sorted_rows[keep, :]
     for copy in moves:
         copy.wait()
-    got = got_rows[...]
+    for copy in back:
+        copy.wait()
+
+
+def place_kernel(layer_hbm, got_ref, layer_out, image_ref, sem):
+    copy = pltpu.make_async_copy(layer_hbm, layer_out, sem)
+    copy.start()
+    width, groups = image_ref.shape
+    got = got_ref[...]
     target = got[:, width : width + 1].astype(jnp.float32) * 16.0 + got[
         :, width + 1 : width + 2
     ].astype(jnp.float32)
-    put = jnp.where(target == across.astype(jnp.float32), 1.0, 0.0).astype(jnp.bfloat16)
+    slot = lax.broadcasted_iota(jnp.int32, (groups, groups), 1).astype(jnp.float32)
+    put = jnp.where(target == slot, 1.0, 0.0).astype(jnp.bfloat16)
     image_ref[...] = lax.dot_general(
         got, put, (((0,), (0,)), ((), ())), preferred_element_type=jnp.float32
     )[:width].astype(jnp.bfloat16)
-    for copy in back:
-        copy.wait()
-
-
-def tail(attended, residual, out_weight, merge_weight, far_weight, gain, dest_slots, rows, cols):
+    copy.wait()
+
+
+def tail(attended, residual, out_weight, merge_weight, far_weight, gain, dest_row, rows, cols):
     width, tokens = attended.shape
     full = out_weight.shape[0]
     chunk = tokens // cols
@@ -686,13 +712,13 @@
     vmem = pl.BlockSpec(memory_space=pltpu.VMEM)
     hbm = pl.BlockSpec(memory_space=pl.ANY)
     dma = pltpu.SemaphoreType.DMA
-    return pl.pallas_call(
+    layer, got = pl.pallas_call(
         functools.partial(tail_kernel, rows, cols),
         out_shape=(
             jax.ShapeDtypeStruct((width, tokens), bf16),
-            jax.ShapeDtypeStruct((width, groups), bf16),
+            jax.ShapeDtypeStruct((groups, width + 16), bf16),
         ),
-        in_specs=[vmem, vmem, hbm, hbm, hbm, vmem, vmem, vmem],
+        in_specs=[vmem, vmem, hbm, hbm, hbm, vmem, vmem],
         out_specs=(vmem, vmem),
         scratch_shapes=[
             pltpu.VMEM((full, chunk), bf16),
@@ -704,7 +730,6 @@
             pltpu.VMEM((width, chunk), bf16),
             pltpu.VMEM((width + 16, groups), bf16),
             pltpu.VMEM((groups, groups), bf16),
-            pltpu.VMEM((groups, width + 16), bf16),
             pltpu.VMEM((groups, width + 16), bf16),
             dma((3,)),
             dma((cols,)),
@@ -735,40 +760,31 @@
         out_weight,
         merge_weight,
         far_weight,
-        gain[None, :],
-        dest_slots[None, :],
-        dest_slots[:, None],
-    )
+        gain.reshape(-1, 128),
+        dest_row.reshape(cols // 2, -1),
+    )
+    return pl.pallas_call(
+        place_kernel,
+        out_shape=(
+            jax.ShapeDtypeStruct((width, tokens), bf16),
+            jax.ShapeDtypeStruct((width, groups), bf16),
+        ),
+        in_specs=[hbm, vmem],
+        out_specs=(hbm, vmem),
+        scratch_shapes=[dma],
+        compiler_params=pltpu.CompilerParams(vmem_limit_bytes=60 << 20),
+    )(layer, got)
 
 
 def body(qkv, residual_in, out_weight, merge_weight, merge_gain, image_groups, dest_row):
     rows = lax.axis_size("row")
     cols = lax.axis_size("col")
     row_id = lax.axis_index("row")
-    col_id = lax.axis_index("col")
-
-    chips = cols // 2
-    chip = col_id // 2
-    before, after, across = (chip + chips - 1) % chips, (chip + 1) % chips, (chip + 2) % chips
-    met = jnp.stack(
-        [
-            2 * chip,
-            2 * chip + 1,
-            2 * before,
-            2 * after + 1,
-            2 * across,
-            2 * across + 1,
-            2 * after,
-            2 * before + 1,
-        ]
-    )
-    dest_slots = jnp.take(dest_row.reshape(cols, -1), met, axis=0).reshape(-1)
-
     attended, residual, far_weight = attention(
         qkv, residual_in, merge_weight, image_groups, row_id, out_weight.shape[0], rows, cols
     )
     return tail(
-        attended, residual, out_weight, merge_weight, far_weight, merge_gain, dest_slots, rows, cols
+        attended, residual, out_weight, merge_weight, far_weight, merge_gain, dest_row, rows, cols
     )
 
 

time: 102 us -> 113 us (1.11); the launches traced: 102 us -> 110 us
  Pallas kernels: 90.9 us -> 110 us
  local copies, waits for them, and re-layouts: 10 us -> 0 us
    pallas_call x0 -> x1, Pallas kernels: none -> 24.6 us  [tail(): pl.pallas_call(place_kernel, out_shape=(jax.ShapeDtypeStruct((width, toke...]
    pallas_call x1, Pallas kernels: 48.8 us -> 45.1 us  [tail(): pl.pallas_call(functools.partial(tail_kernel, rows, cols), out_shape=(jax...]
    unnamed x6 -> x0, local copies, waits for them, and re-layouts: 3.66 us -> none
    squeeze x1 -> x0, local copies, waits for them, and re-layouts: 2.04 us -> none  [attention(): qkv[0]]
    pallas_call x1, Pallas kernels: 10.7 us -> 8.72 us  [attention(): pl.pallas_call(functools.partial(far_kernel, coef), out_shape=jax.ShapeDt...]
    broadcast_in_dim x2 -> x0, local copies, waits for them, and re-layouts: 1.96 us -> none  [the longest x1 1.36 us: attention(): image_groups[:, None]]
    select_n x2 -> x0, local copies, waits for them, and re-layouts: 1.55 us -> none  [body(): dest_slots = jnp.take(dest_row.reshape(cols, -1), met, axis=0).reshape(-1)]
where the time goes in v4:
time: 113 us; the launch traced here: 110 us
  Pallas kernels  110 us (97%)
    pallas_call x1, Pallas kernels, tail(): pl.pallas_call(functools.partial(tail_kernel, rows, cols), out_shape=(jax...  45.1 us
    pallas_call x1, Pallas kernels, attention(): pl.pallas_call(functools.partial(head_kernel, rows, cols, coef), out_shap...  31.3 us
    pallas_call x1, Pallas kernels, tail(): pl.pallas_call(place_kernel, out_shape=(jax.ShapeDtypeStruct((width, toke...  24.6 us
    pallas_call x1, Pallas kernels, attention(): pl.pallas_call(functools.partial(far_kernel, coef), out_shape=jax.ShapeDt...  8.72 us

profile of v4, /device:TPU:0, one launch (start us, length us, event | category | flops | bytes accessed | tf_op | source)
XLA Modules:
  0.0 110.3 jit_solution(10421026011258805798)
XLA Ops:
  0.6 31.3 %shard_map.86 = (bf16[2,176,1024]{2,1,0:T(8,128)(2,1)}, bf16[2,176,1024]{2,1,0:T(8,128)(2,1)}, bf16[1408,256]{1,0:T(8,128)(2,1)}, bf16[176,1408]{1,0:T(8,128)(2,...) custom-call(bf16[3,176,2048]{2,1,0:T(8,128)(2,1)} %qkv_hbm.3, ...), custom_call_target="tpu_custom_call" | custom-call | tf_op jit(solution)/shard_map/pallas_call | solution.py:355
  31.9 8.7 %shard_map.87.attended_ref = bf16[176,2048]{1,0:T(8,128)(2,1)} custom-call(s32[64]{0:T(128)} %groups_ref.1, s32[1]{0:T(128)} %bitcast.row_ref, bf16[3,176,2048]{2,1,0:T(8,128)(2,1)} %qkv_hbm.3, bf16[2,176,1024]{2,1,0:T(8,128)(2,1)} %get-tuple-element.14.left_ref, bf16[2,176,1024]{2,1,0:T(8,128)(2,1)} %get-tuple-element.15.right_ref, ...), custom_call_target="tpu_custom_call" | custom-call | tf_op jit(solution)/shard_map/pallas_call | solution.py:385
  40.6 45.1 %shard_map.88 = (bf16[176,2048]{1,0:T(8,128)(2,1)}, bf16[512,192]{1,0:T(8,128)(2,1)}) custom-call(bf16[176,2048]{1,0:T(8,128)(2,1)} %shard_map.87.attended_ref, bf16[1408,256]{1,0:T(8,128)(2,1)} %get-tuple-element.22.residual_ref, bf16[1408,1408]{1,0:T(8,128)(2,1)} %out_weight_hbm.1, bf16[176,5632]{1,0:T(8,128)(2,1)} %merge_weight_hbm.3, ...), custom_call_target="tpu_custom_call" | custom-call | flops 4060086272 | bytes 16777216 | tf_op jit(solution)/shard_map/pallas_call | solution.py:715
  85.8 24.6 %shard_map.89 = (bf16[176,2048]{1,0:T(8,128)(2,1)}, bf16[176,512]{1,0:T(8,128)(2,1)}) custom-call(bf16[176,2048]{1,0:T(8,128)(2,1)} %get-tuple-element.24.layer_hbm, bf16[512,192]{1,0:T(8,128)(2,1)} %get-tuple-element.25.got_ref), custom_call_target="tpu_custom_call" | custom-call | tf_op jit(solution)/shard_map/pallas_call | solution.py:766

commit v5 on v4

v5 whole, which is shorter than its diff:
```python
import functools
import math

import jax
import jax.numpy as jnp
from jax import lax
from jax.experimental import pallas as pl
from jax.experimental.pallas import tpu as pltpu
from jax.sharding import PartitionSpec as P

HEAD_DIM = 88
QB = 256
KB = 256
NEAR = 2
PIECES = 2
NEG = -1e30
MESH = pl.DeviceIdType.MESH


def tile_step(kt, v0, v1, qcat, ok, coef, row, m_ref, l_ref, acc_ref):
    scores = lax.dot_general(
        kt, qcat, (((1,), (0,)), ((), ())), preferred_element_type=jnp.float32
    )
    width = qcat.shape[1] // 2
    for head in range(2):
        part = jnp.where(ok, scores[:, head * width : (head + 1) * width], NEG)
        old = m_ref[row + head]
        new = jnp.maximum(old, jnp.max(part, axis=0, keepdims=True))
        fade = jnp.exp2((old - new) * coef)
        expo = jnp.exp2(part * coef - new * coef)
        l_ref[row + head] = l_ref[row + head] * fade + jnp.sum(expo, axis=0, keepdims=True)
        m_ref[row + head] = new
        values = v1 if head else v0
        acc_ref[row + head] = acc_ref[row + head] * fade + lax.dot_general(
            values,
            expo.astype(jnp.bfloat16),
            (((1,), (0,)), ((), ())),
            preferred_element_type=jnp.float32,
        )


def split_heads(values):
    wide = values.astype(jnp.float32)
    return wide[:HEAD_DIM].astype(jnp.bfloat16), wide[HEAD_DIM:].astype(jnp.bfloat16)


def query_pair(block):
    feature = lax.broadcasted_iota(jnp.int32, block.shape, 0)
    zero = jnp.zeros_like(block)
    return jnp.concatenate(
        [jnp.where(feature < HEAD_DIM, block, zero), jnp.where(feature < HEAD_DIM, zero, block)],
        axis=1,
    )


def head_kernel(
    rows,
    cols,
    coef,
    qkv,
    res,
    merge_weight_ref,
    groups_line_ref,
    left_hbm,
    right_hbm,
    spread_hbm,
    far_hbm,
    m_ref,
    l_ref,
    acc_ref,
    kt,
    vt,
    bound_ref,
    load_sem,
    halo_send,
    halo_recv,
    res_send,
    res_recv,
    far_send,
    far_recv,
):
    row = lax.axis_index("row")
    me = lax.axis_index("col")
    _, width, tokens = qkv.shape
    reach = left_hbm.shape[2]
    blocks = tokens // QB
    chunk = tokens // cols
    full = spread_hbm.shape[0]
    barrier = pltpu.get_barrier_semaphore()
    after = (row + 1) % rows
    before = (row + rows - 1) % rows
    for other in (after, before):
        pl.semaphore_signal(barrier, inc=1, device_id={"row": other}, device_id_type=MESH)
    for k in range(1, cols):
        pl.semaphore_signal(
            barrier, inc=1, device_id={"col": (me + k) % cols}, device_id_type=MESH
        )
    mine = pl.ds(pl.multiple_of(me * chunk, chunk), chunk)
    place = pl.ds(pl.multiple_of(me * width, 16), width)
    keep = pltpu.make_async_copy(res.at[:, mine], spread_hbm.at[place], load_sem)
    keep.start()
    pl.semaphore_wait(barrier, cols + 1)

    sent = []
    for side, (other, target, at) in enumerate(
        ((after, left_hbm, tokens - reach), (before, right_hbm, 0))
    ):
        for i in range(2):
            sent.append(
                pltpu.make_async_remote_copy(
                    src_ref=qkv.at[1 + i, :, at : at + reach],
                    dst_ref=target.at[i],
                    send_sem=halo_send.at[2 * side + i],
                    recv_sem=halo_recv.at[2 * side + i],
                    device_id={"row": other},
                    device_id_type=MESH,
                )
            )
    for k in range(1, cols):
        to = (me + k) % cols
        sent.append(
            pltpu.make_async_remote_copy(
                src_ref=res.at[:, pl.ds(pl.multiple_of(to * chunk, chunk), chunk)],
                dst_ref=spread_hbm.at[place],
                send_sem=res_send.at[k],
                recv_sem=res_recv.at[k],
                device_id={"col": to},
                device_id_type=MESH,
            )
        )
    part = row // (rows // 4)
    sent.append(
        pltpu.make_async_remote_copy(
            src_ref=merge_weight_ref.at[:, pl.ds(pl.multiple_of(part * full, 128), full)],
            dst_ref=far_hbm,
            send_sem=far_send,
            recv_sem=far_recv,
            device_id={"col": (me + cols // 2) % cols},
            device_id_type=MESH,
        )
    )
    for copy in sent:
        copy.start()

    images = groups_line_ref.shape[1]
    first = lax.broadcasted_iota(jnp.int32, (images, images), 0)
    second = lax.broadcasted_iota(jnp.int32, (images, images), 1)
    size = (
        jnp.sum(jnp.where(second == first, groups_line_ref[...], 0), axis=1, keepdims=True) * 4
    )
    begin = (
        jnp.sum(
            jnp.where(second < first, groups_line_ref[...], 0), axis=1, keepdims=True
        )
        * 4
        - row * tokens
    )

    def prepare(b, carry):
        at = pl.multiple_of(b * QB, QB)
        token = lax.broadcasted_iota(jnp.int32, (images, QB), 1) + at
        inside = (token >= begin) & (token < begin + size)
        bound_ref[0:1, pl.ds(at, QB)] = jnp.sum(jnp.where(inside, begin, 0), axis=0, keepdims=True)
        bound_ref[1:2, pl.ds(at, QB)] = jnp.sum(jnp.where(inside, size, 0), axis=0, keepdims=True)
        kt[pl.ds(at, QB), :] = jnp.transpose(qkv[1, :, pl.ds(at, QB)])
        v0, v1 = split_heads(qkv[2, :, pl.ds(at, QB)])
        vt[0, :, pl.ds(at, QB)] = v0
        vt[1, :, pl.ds(at, QB)] = v1
        return carry

    lax.fori_loop(0, blocks, prepare, 0)

    def per_block(b, carry):
        at = pl.multiple_of(b * QB, QB)
        qcat = query_pair(qkv[0, :, pl.ds(at, QB)])
        start = bound_ref[0:1, pl.ds(at, QB)]
        length = bound_ref[1:2, pl.ds(at, QB)]
        row_at = b * 2
        for head in range(2):
            m_ref[row_at + head] = jnp.full((1, QB), NEG, jnp.float32)
            l_ref[row_at + head] = jnp.zeros((1, QB), jnp.float32)
            acc_ref[row_at + head] = jnp.zeros((HEAD_DIM, QB), jnp.float32)

        def per_tile(t, inner):
            key = pl.multiple_of(t * KB, KB)
            spot = lax.broadcasted_iota(jnp.int32, (KB, QB), 0) + (key - start)
            ok = (spot >= 0) & (spot < length)
            tile_step(
                kt[pl.ds(key, KB), :],
                vt[0, :, pl.ds(key, KB)],
                vt[1, :, pl.ds(key, KB)],
                qcat,
                ok,
                coef,
                row_at,
                m_ref,
                l_ref,
                acc_ref,
            )
            return inner

        lax.fori_loop(
            jnp.maximum(b - NEAR, 0), jnp.minimum(b + NEAR + 1, blocks), per_tile, 0
        )
        return carry

    lax.fori_loop(0, blocks, per_block, 0)
    keep.wait()
    for copy in sent:
        copy.wait()


def far_kernel(
    coef,
    groups_ref,
    row_ref,
    qkv_ref,
    left_ref,
    right_ref,
    bound_ref,
    m_in,
    l_in,
    acc_in,
    kt_in,
    vt_in,
    out_ref,
    low_ref,
    high_ref,
    kt,
    vt,
    m_ref,
    l_ref,
    acc_ref,
):
    reach = left_ref.shape[2]
    tokens = qkv_ref.shape[2]
    blocks = tokens // QB
    base = row_ref[0] * tokens

    def find(b, state):
        token = base + b * QB

        def past(at, state):
            def more(s):
                return s[1] + groups_ref[s[0]] * 4 <= at

            def step(s):
                return s[0] + 1, s[1] + groups_ref[s[0]] * 4

            return lax.while_loop(more, step, state)

        state = past(token, state)
        low_ref[b] = state[1] - base
        state = past(token + QB - 1, state)
        high_ref[b] = state[1] + groups_ref[state[0]] * 4 - base
        return state

    lax.fori_loop(0, blocks, find, (jnp.int32(0), jnp.int32(0)))
    for i in range(reach // KB):
        for needed, source, at in (
            (low_ref[0] < (i + 1) * KB - reach, left_ref, 0),
            (high_ref[blocks - 1] > tokens + i * KB, right_ref, reach),
        ):

            @pl.when(needed)
            def _():
                span = slice(i * KB, (i + 1) * KB)
                to = slice(at + i * KB, at + (i + 1) * KB)
                kt[to, :] = jnp.transpose(source[0, :, span])
                v0, v1 = split_heads(source[1, :, span])
                vt[0, :, to] = v0
                vt[1, :, to] = v1

    def per_block(b, carry):
        at = pl.multiple_of(b * QB, QB)
        row_at = b * 2
        near_low = jnp.maximum(b - NEAR, 0) * QB
        near_high = jnp.minimum(b + NEAR + 1, blocks) * QB
        low, high = low_ref[b], high_ref[b]
        below = jnp.maximum((near_low - jnp.maximum(low, 0) + KB - 1) // KB, 0)
        above = jnp.maximum((jnp.minimum(high, tokens) - near_high + KB - 1) // KB, 0)
        before = jnp.maximum((KB - 1 - low) // KB, 0)
        after = jnp.maximum((high - tokens + KB - 1) // KB, 0)
        for head in range(2):
            m_ref[head] = m_in[row_at + head]
            l_ref[head] = l_in[row_at + head]
            acc_ref[head] = acc_in[row_at + head]

        @pl.when(below + above + before + after > 0)
        def _():
            qcat = query_pair(qkv_ref[0, :, pl.ds(at, QB)])
            start = bound_ref[0:1, pl.ds(at, QB)]
            length = bound_ref[1:2, pl.ds(at, QB)]

            def tile(key, slot, k_from, v_from):
                slot = pl.multiple_of(slot, KB)
                spot = lax.broadcasted_iota(jnp.int32, (KB, QB), 0) + (key - start)
                ok = (spot >= 0) & (spot < length)
                tile_step(
                    k_from[pl.ds(slot, KB), :],
                    v_from[0, :, pl.ds(slot, KB)],
                    v_from[1, :, pl.ds(slot, KB)],
                    qcat,
                    ok,
                    coef,
                    0,
                    m_ref,
                    l_ref,
                    acc_ref,
                )

            def own_tile(t, inner):
                key = jnp.where(
                    t < below, near_low - (t + 1) * KB, near_high + (t - below) * KB
                )
                tile(key, key, kt_in, vt_in)
                return inner

            def halo_tile(t, inner):
                key = jnp.where(t < before, -(t + 1) * KB, tokens + (t - before) * KB)
                slot = jnp.where(t < before, reach - (t + 1) * KB, reach + (t - before) * KB)
                tile(key, slot, kt, vt)
                return inner

            lax.fori_loop(0, below + above, own_tile, 0)
            lax.fori_loop(0, before + after, halo_tile, 0)

        both = [acc_ref[head] * (1.0 / l_ref[head]) for head in range(2)]
        out_ref[:, pl.ds(at, QB)] = jnp.concatenate(both, axis=0).astype(jnp.bfloat16)
        return carry

    lax.fori_loop(0, blocks, per_block, 0)


def attention(qkv, residual, merge_weight, image_groups, row_id, full, rows, cols):
    _, width, tokens = qkv.shape
    reach = tokens // 2
    blocks = tokens // QB
    chunk = tokens // cols
    bf16, f32 = jnp.bfloat16, jnp.float32
    coef = math.log2(math.e) / math.sqrt(HEAD_DIM)
    smem = pl.BlockSpec(memory_space=pltpu.SMEM)
    vmem = pl.BlockSpec(memory_space=pltpu.VMEM)
    hbm = pl.BlockSpec(memory_space=pl.ANY)
    dma = pltpu.SemaphoreType.DMA
    halo = jax.ShapeDtypeStruct((2, width, reach), bf16)
    stat = jax.ShapeDtypeStruct((2 * blocks, 1, QB), f32)
    left, right, spread, far, m, l, acc, kt, vt, bound = pl.pallas_call(
        functools.partial(head_kernel, rows, cols, coef),
        out_shape=(
            halo,
            halo,
            jax.ShapeDtypeStruct((full, chunk), bf16),
            jax.ShapeDtypeStruct((width, full), bf16),
            stat,
            stat,
            jax.ShapeDtypeStruct((2 * blocks, HEAD_DIM, QB), f32),
            jax.ShapeDtypeStruct((tokens, width), bf16),
            jax.ShapeDtypeStruct((2, HEAD_DIM, tokens), bf16),
            jax.ShapeDtypeStruct((8, tokens), jnp.int32),
        ),
        in_specs=[vmem, vmem, vmem, vmem],
        out_specs=(hbm, hbm, hbm, hbm, vmem, vmem, vmem, vmem, vmem, vmem),
        scratch_shapes=[
            dma,
            dma((4,)),
            dma((4,)),
            dma((cols,)),
            dma((cols,)),
            dma,
            dma,
        ],
        compiler_params=pltpu.CompilerParams(
            collective_id=1, has_side_effects=True, vmem_limit_bytes=20 << 20
        ),
    )(qkv, residual, merge_weight, image_groups[None, :])
    attended = pl.pallas_call(
        functools.partial(far_kernel, coef),
        out_shape=jax.ShapeDtypeStruct((width, tokens), bf16),
        in_specs=[smem, smem] + [vmem] * 9,
        out_specs=vmem,
        scratch_shapes=[
            pltpu.SMEM((blocks,), jnp.int32),
            pltpu.SMEM((blocks,), jnp.int32),
            pltpu.VMEM((2 * reach, width), bf16),
            pltpu.VMEM((2, HEAD_DIM, 2 * reach), bf16),
            pltpu.VMEM((2, 1, QB), f32),
            pltpu.VMEM((2, 1, QB), f32),
            pltpu.VMEM((2, HEAD_DIM, QB), f32),
        ],
        compiler_params=pltpu.CompilerParams(vmem_limit_bytes=20 << 20),
    )(image_groups, row_id[None], qkv, left, right, bound, m, l, acc, kt, vt)
    return attended, spread, far


def tail_kernel(
    rows,
    cols,
    attended_ref,
    residual_ref,
    weight,
    merge_weight_ref,
    far_weight_ref,
    gain_ref,
    dest_ref,
    layer_ref,
    got_rows,
    att,
    weight_t,
    merge_w,
    layer_rows,
    held,
    far_rows,
    merged,
    pick,
    sorted_rows,
    gain_column,
    load_sem,
    spread_send,
    spread_recv,
    back_send,
    back_recv,
    near_send,
    near_recv,
    own_send,
    own_recv,
    pass_send,
    pass_recv,
    far_send,
    far_recv,
    row_send,
    row_recv,
    far_w_send,
    far_w_recv,
):
    row = lax.axis_index("row")
    me = lax.axis_index("col")
    width, tokens = attended_ref.shape
    full = weight.shape[0]
    chunk = tokens // cols
    piece = chunk // PIECES
    part = piece // 4
    groups = tokens // 4
    share = groups // rows
    chips = cols // 2
    core = me % 2
    chip = me // 2
    sibling = me + 1 - 2 * core
    half = full // 2
    line_up = rows // 4

    barrier = pltpu.get_barrier_semaphore()
    for k in range(1, cols):
        pl.semaphore_signal(
            barrier, inc=1, device_id={"col": (me + k) % cols}, device_id_type=MESH
        )
    for k in range(1, rows):
        pl.semaphore_signal(
            barrier, inc=1, device_id={"row": (row + k) % rows}, device_id_type=MESH
        )
    far_at = pl.ds(pl.multiple_of(row // line_up * full, 128), full)
    far_place = merge_w.at[width : 2 * width, far_at]
    loads = [
        pltpu.make_async_copy(merge_weight_ref, merge_w.at[0:width], load_sem.at[0]),
        pltpu.make_async_copy(far_weight_ref, far_place, load_sem.at[1]),
    ]
    for load in loads:
        load.start()
    my_rows = pl.ds(pl.multiple_of(me * width, 16), width)
    pl.semaphore_wait(barrier, rows + cols - 2)

    def lanes(owner, p):
        return pl.ds(pl.multiple_of(owner * chunk + p * piece, 128), piece)

    spread = []
    for p in range(PIECES):
        for k in range(1, cols):
            to = (me + k) % cols
            copy = pltpu.make_async_remote_copy(
                src_ref=attended_ref.at[:, lanes(to, p)],
                dst_ref=att.at[p, my_rows],
                send_sem=spread_send.at[p, k],
                recv_sem=spread_recv.at[p, k],
                device_id={"col": to},
                device_id_type=MESH,
            )
            copy.start()
            spread.append(copy)
    gather = []
    for k in range(1, 4):
        copy = pltpu.make_async_remote_copy(
            src_ref=far_weight_ref,
            dst_ref=far_place,
            send_sem=far_w_send.at[k],
            recv_sem=far_w_recv.at[k],
            device_id={"row": (row + k * line_up) % rows},
            device_id_type=MESH,
        )
        copy.start()
        gather.append(copy)
    for p in range(PIECES):
        att[p, my_rows, :] = attended_ref[:, lanes(me, p)]

    def turn(i, carry):
        at = pl.multiple_of(i * 128, 128)
        weight_t[pl.ds(at, 128), :] = jnp.transpose(weight[:, pl.ds(at, 128)])
        return carry

    lax.fori_loop(0, full // 128, turn, 0)
    for i in range(full // 128):
        gain_column[i * 128 : (i + 1) * 128, :] = jnp.transpose(
            jnp.broadcast_to(gain_ref[i : i + 1, :], (8, 128))
        )

    before, after, across_chip = (chip + 3) % chips, (chip + 1) % chips, (chip + 2) % chips
    of = [dest_ref[pl.ds(c, 1), :] for c in (chip, before, across_chip, after)]
    span = chunk // 4
    line = jnp.concatenate(
        [
            of[c][:, k * span + p * part : k * span + (p + 1) * part]
            for order in (((0, 0), (0, 1), (1, 0), (3, 1)), ((2, 0), (2, 1), (3, 0), (1, 1)))
            for p in range(PIECES)
            for c, k in order
        ],
        axis=1,
    )
    owner_line = line // groups
    owner_column = jnp.transpose(
        jnp.broadcast_to(owner_line.astype(jnp.float32), (8, groups))
    )[:, 0:1].astype(jnp.int32)
    down = lax.broadcasted_iota(jnp.int32, (groups, groups), 0)
    across = lax.broadcasted_iota(jnp.int32, (groups, groups), 1)
    earlier = (owner_column == owner_line) & (down < across)
    rank = jnp.sum(earlier.astype(jnp.int32), axis=0, keepdims=True)
    pick[...] = jnp.where(down == owner_line * share + rank, 1.0, 0.0).astype(jnp.bfloat16)
    slot = line % groups
    which = lax.broadcasted_iota(jnp.int32, (merged.shape[0] - width, groups), 0)
    digits = jnp.where(which == 0, slot // 16, jnp.where(which == 1, slot % 16, 0))
    merged[width:, :] = digits.astype(jnp.float32).astype(jnp.bfloat16)

    here = lax.broadcasted_iota(jnp.int32, (piece, piece), 0)
    there = lax.broadcasted_iota(jnp.int32, (piece, piece), 1)
    order = jnp.where((here % 4) * part + here // 4 == there, 1.0, 0.0).astype(jnp.bfloat16)
    goal = (chip + 1 + 2 * core) % chips
    near, own, back = [], [], []
    for p in range(PIECES):
        for copy in spread[p * (cols - 1) : (p + 1) * (cols - 1)]:
            copy.wait()
        at = slice(p * piece, (p + 1) * piece)
        projected = jnp.dot(weight_t[...], att[p], preferred_element_type=jnp.float32)
        rounded = (residual_ref[:, at].astype(jnp.float32) + projected).astype(jnp.bfloat16)
        layer_rows[p] = rounded
        values32 = rounded.astype(jnp.float32)
        centre = jnp.sum(values32, axis=0, keepdims=True) * (1.0 / full)
        spread_of = jnp.sum(jnp.square(values32 - centre), axis=0, keepdims=True) * (1.0 / full)
        scale = lax.rsqrt(spread_of + 1e-06)
        normed = ((values32 - centre) * scale * gain_column[:, 0:1]).astype(jnp.bfloat16)
        held[p, core] = jnp.dot(normed, order, preferred_element_type=jnp.float32).astype(
            jnp.bfloat16
        )
        for h in range(2):
            rows_of = pl.ds(h * half, half)
            copy = pltpu.make_async_remote_copy(
                src_ref=held.at[p, core, rows_of],
                dst_ref=held.at[p, 2 + core, rows_of],
                send_sem=near_send.at[p, h],
                recv_sem=near_recv.at[p, core],
                device_id={"col": goal * 2 + h},
                device_id_type=MESH,
            )
            copy.start()
            near.append(copy)
        copy = pltpu.make_async_remote_copy(
            src_ref=held.at[p, core],
            dst_ref=held.at[p, core],
            send_sem=own_send.at[p],
            recv_sem=own_recv.at[p],
            device_id={"col": sibling},
            device_id_type=MESH,
        )
        copy.start()
        own.append(copy)
        layer_ref[:, lanes(me, p)] = layer_rows[p, my_rows, :]

    passed = []
    my_half = pl.ds(pl.multiple_of(core * half, 16), half)
    for p in range(PIECES):
        for s in range(2):
            arrive = pltpu.make_async_remote_copy(
                src_ref=held.at[p, core, my_half],
                dst_ref=held.at[p, 2 + s, my_half],
                send_sem=near_send.at[p, s],
                recv_sem=near_recv.at[p, s],
                device_id={"col": sibling},
                device_id_type=MESH,
            )
            arrive.wait_recv()
            copy = pltpu.make_async_remote_copy(
                src_ref=held.at[p, 2 + s, my_half],
                dst_ref=held.at[p, 2 + s, my_half],
                send_sem=pass_send.at[p, s],
                recv_sem=pass_recv.at[p, s],
                device_id={"col": sibling},
                device_id_type=MESH,
            )
            copy.start()
            passed.append(copy)
    for copy in near:
        copy.wait_send()

    def send_back(p):
        for k in range(1, cols):
            to = (me + k) % cols
            copy = pltpu.make_async_remote_copy(
                src_ref=layer_rows.at[p, pl.ds(pl.multiple_of(to * width, 16), width)],
                dst_ref=layer_ref.at[:, lanes(me, p)],
                send_sem=back_send.at[p, k],
                recv_sem=back_recv.at[p, k],
                device_id={"col": to},
                device_id_type=MESH,
            )
            copy.start()
            back.append(copy)

    for p in range(PIECES - 1):
        send_back(p)
    for load in loads:
        load.wait()
    for copy in gather:
        copy.wait()
    for copy in own + passed:
        copy.wait()

    total = None
    for j in range(4):
        side = jnp.concatenate(
            [
                held[p, s, :, j * part : (j + 1) * part]
                for p in range(PIECES)
                for s in range(4)
            ],
            axis=1,
        )
        term = jnp.dot(
            merge_w[:, j * full : (j + 1) * full], side, preferred_element_type=jnp.float32
        )
        total = term if total is None else total + term
    far_rows[...] = total[width:].astype(jnp.bfloat16)
    across_y = pltpu.make_async_remote_copy(
        src_ref=far_rows,
        dst_ref=merged.at[0:width, chunk : 2 * chunk],
        send_sem=far_send,
        recv_sem=far_recv,
        device_id={"col": (me + cols // 2) % cols},
        device_id_type=MESH,
    )
    across_y.start()
    send_back(PIECES - 1)
    merged[0:width, 0:chunk] = total[:width].astype(jnp.bfloat16)
    across_y.wait()

    sorted_rows[...] = lax.dot_general(
        pick[...], merged[...], (((1,), (1,)), ((), ())), preferred_element_type=jnp.float32
    ).astype(jnp.bfloat16)
    moves = []
    for k in range(1, rows):
        to = (row + k) % rows
        copy = pltpu.make_async_remote_copy(
            src_ref=sorted_rows.at[pl.ds(pl.multiple_of(to * share, share), share)],
            dst_ref=got_rows.at[pl.ds(pl.multiple_of(row * share, share), share)],
            send_sem=row_send.at[k],
            recv_sem=row_recv.at[k],
            device_id={"row": to},
            device_id_type=MESH,
        )
        copy.start()
        moves.append(copy)
    keep = pl.ds(pl.multiple_of(row * share, share), share)
    got_rows[keep, :] = sorted_rows[keep, :]
    for copy in moves + back:
        copy.wait()


def place_kernel(layer_ref, got_ref, layer_out, image_ref, sem):
    copy = pltpu.make_async_copy(layer_ref, layer_out, sem)
    copy.start()
    width, groups = image_ref.shape
    got = got_ref[...]
    target = got[:, width : width + 1].astype(jnp.float32) * 16.0 + got[
        :, width + 1 : width + 2
    ].astype(jnp.float32)
    slot = lax.broadcasted_iota(jnp.int32, (groups, groups), 1).astype(jnp.float32)
    put = jnp.where(target == slot, 1.0, 0.0).astype(jnp.bfloat16)
    image_ref[...] = lax.dot_general(
        got, put, (((0,), (0,)), ((), ())), preferred_element_type=jnp.float32
    )[:width].astype(jnp.bfloat16)
    copy.wait()


def tail(attended, residual, out_weight, merge_weight, far_weight, gain, dest_row, rows, cols):
    width, tokens = attended.shape
    full = out_weight.shape[0]
    chunk = tokens // cols
    piece = chunk // PIECES
    groups = tokens // 4
    bf16 = jnp.bfloat16
    vmem = pl.BlockSpec(memory_space=pltpu.VMEM)
    hbm = pl.BlockSpec(memory_space=pl.ANY)
    dma = pltpu.SemaphoreType.DMA
    layer, got = pl.pallas_call(
        functools.partial(tail_kernel, rows, cols),
        out_shape=(
            jax.ShapeDtypeStruct((width, tokens), bf16),
            jax.ShapeDtypeStruct((groups, width + 16), bf16),
        ),
        in_specs=[vmem] * 7,
        out_specs=(vmem, vmem),
        scratch_shapes=[
            pltpu.VMEM((PIECES, full, piece), bf16),
            pltpu.VMEM((full, full), bf16),
            pltpu.VMEM((2 * width, merge_weight.shape[1]), bf16),
            pltpu.VMEM((PIECES, full, piece), bf16),
            pltpu.VMEM((PIECES, 4, full, piece), bf16),
            pltpu.VMEM((width, chunk), bf16),
            pltpu.VMEM((width + 16, groups), bf16),
            pltpu.VMEM((groups, groups), bf16),
            pltpu.VMEM((groups, width + 16), bf16),
            pltpu.VMEM((full, 8), jnp.float32),
            dma((2,)),
            dma((PIECES, cols)),
            dma((PIECES, cols)),
            dma((PIECES, cols)),
            dma((PIECES, cols)),
            dma((PIECES, 2)),
            dma((PIECES, 2)),
            dma((PIECES,)),
            dma((PIECES,)),
            dma((PIECES, 2)),
            dma((PIECES, 2)),
            dma,
            dma,
            dma((rows,)),
            dma((rows,)),
            dma((4,)),
            dma((4,)),
        ],
        compiler_params=pltpu.CompilerParams(
            collective_id=0, has_side_effects=True, vmem_limit_bytes=40 << 20
        ),
    )(
        attended,
        residual,
        out_weight,
        merge_weight,
        far_weight,
        gain.reshape(-1, 128),
        dest_row.reshape(cols // 2, -1),
    )
    return pl.pallas_call(
        place_kernel,
        out_shape=(
            jax.ShapeDtypeStruct((width, tokens), bf16),
            jax.ShapeDtypeStruct((width, groups), bf16),
        ),
        in_specs=[vmem, vmem],
        out_specs=(hbm, vmem),
        scratch_shapes=[dma],
        compiler_params=pltpu.CompilerParams(vmem_limit_bytes=16 << 20),
    )(layer, got)


def body(qkv, residual_in, out_weight, merge_weight, merge_gain, image_groups, dest_row):
    rows = lax.axis_size("row")
    cols = lax.axis_size("col")
    row_id = lax.axis_index("row")
    attended, residual, far_weight = attention(
        qkv, residual_in, merge_weight, image_groups, row_id, out_weight.shape[0], rows, cols
    )
    return tail(
        attended, residual, out_weight, merge_weight, far_weight, merge_gain, dest_row, rows, cols
    )


def solution(mesh):
    return jax.shard_map(
        body,
        mesh=mesh,
        in_specs=(P(None, "col", "row"), P("col", "row"), P(), P("col", None), P(), P(), P("row")),
        out_specs=(P("col", "row"), P("col", "row")),
        check_vma=False,
    )
```

time: 113 us -> 84.6 us (0.75); the launches traced: 110 us -> 84.4 us
  Pallas kernels: 110 us -> 78.7 us
  local copies, waits for them, and re-layouts: 0 us -> 4.94 us
    pallas_call x1, Pallas kernels: 24.6 us -> 1.54 us  [tail(): pl.pallas_call(place_kernel, out_shape=(jax.ShapeDtypeStruct((width, toke...]
    unnamed x0 -> x16, local copies, waits for them, and re-layouts: none -> 4.94 us
    pallas_call x1, Pallas kernels: 8.72 us -> 4.36 us  [attention(): pl.pallas_call(functools.partial(far_kernel, coef), out_shape=jax.ShapeDt...]
    pallas_call x1, Pallas kernels: 31.3 us -> 28.5 us  [attention(): pl.pallas_call(functools.partial(head_kernel, rows, cols, coef), out_shap...]
where the time goes in v5:
time: 84.6 us; the launch traced here: 84.4 us
  Pallas kernels  78.7 us (93%)
  local copies, waits for them, and re-layouts  4.94 us (6%)
    pallas_call x1, Pallas kernels, tail(): pl.pallas_call(functools.partial(tail_kernel, rows, cols), out_shape=(jax...  44.3 us
    pallas_call x1, Pallas kernels, attention(): pl.pallas_call(functools.partial(head_kernel, rows, cols, coef), out_shap...  28.5 us
    unnamed x16, local copies, waits for them, and re-layouts  4.94 us
    pallas_call x1, Pallas kernels, attention(): pl.pallas_call(functools.partial(far_kernel, coef), out_shape=jax.ShapeDt...  4.36 us

profile of v5, /device:TPU:0, one launch (start us, length us, event | category | flops | bytes accessed | tf_op | source)
XLA Modules:
  0.0 84.4 jit_solution(3268830977179229713)
XLA Ops:
  0.6 0.0 copy-start
  0.6 1.6 %copy-done = bf16[3,176,2048]{2,1,0:T(8,128)(2,1)S(1)} copy-done((bf16[3,176,2048]{2,1,0:T(8,128)(2,1)S(1)}, bf16[3,176,2048]{2,1,0:T(8,128)(2,1)}, u32[]{:S(2)}) %copy-start) | copy-done | bytes 2162712
  2.2 0.0 copy-start.1
  2.2 1.5 %copy-done.1 = bf16[176,5632]{1,0:T(8,128)(2,1)S(1)} copy-done((bf16[176,5632]{1,0:T(8,128)(2,1)S(1)}, bf16[176,5632]{1,0:T(8,128)(2,1)}, u32[]{:S(2)}) %copy-start.1) | copy-done | bytes 1982488
  3.8 0.0 copy-start.4
  3.8 1.1 %copy-done.4 = bf16[176,2048]{1,0:T(8,128)(2,1)S(1)} copy-done((bf16[176,2048]{1,0:T(8,128)(2,1)S(1)}, bf16[176,2048]{1,0:T(8,128)(2,1)}, u32[]{:S(2)}) %copy-start.4) | copy-done | bytes 720920
  4.9 0.0 copy-start.7
  4.9 0.7 copy-done.7
  5.6 28.5 %shard_map.86 = (bf16[2,176,1024]{2,1,0:T(8,128)(2,1)S(1)}, bf16[2,176,1024]{2,1,0:T(8,128)(2,1)S(1)}, bf16[1408,256]{1,0:T(8,128)(2,1)S(1)}, bf16[176,1408]{1,0...) custom-call(bf16[3,176,2048]{2,1,0:T(8,128)(2,1)S(1)} %copy-done, ...), custom_call_target="tpu_custom_call" | custom-call | tf_op jit(solution)/shard_map/pallas_call | solution.py:348
  34.1 0.0 copy-start.2
  34.1 0.0 copy-start.3
  34.1 0.0 copy-start.5
  34.1 0.0 copy-start.6
  34.1 4.4 %shard_map.87.attended_ref = bf16[176,2048]{1,0:T(8,128)(2,1)S(1)} custom-call(s32[64]{0:T(128)S(1)} %copy-done.7, s32[1]{0:T(128)} %bitcast.row_ref, bf16[3,176,2048]{2,1,0:T(8,128)(2,1)S(1)} %copy-done, bf16[2,176,1024]{2,1,0:T(8,128)(2,1)S(1)} %get-tuple-element.14.left_ref, bf16[2,176,1024]{2,1,0:T(8,128)(2,1)S(1)} %get-tuple-element.15.right_ref, ...), custom_call_target="tpu_custom_call" | custom-call | tf_op jit(solution)/shard_map/pallas_call | solution.py:377
  38.5 0.0 copy-done.2
  38.5 0.0 copy-done.3
  38.5 0.0 copy-done.5
  38.5 0.0 copy-done.6
  38.5 44.3 %shard_map.88 = (bf16[176,2048]{1,0:T(8,128)(2,1)S(1)}, bf16[512,192]{1,0:T(8,128)(2,1)S(1)}) custom-call(bf16[176,2048]{1,0:T(8,128)(2,1)S(1)} %shard_map.87.attended_ref, bf16[1408,256]{1,0:T(8,128)(2,1)S(1)} %get-tuple-element.22.residual_ref, bf16[1408,1408]{1,0:T(8,128)(2,1)S(1)} %copy-done.3, bf16[176,5632]{1,0:T(8,128)(2,1)S(1)} %copy-done.2, ...), custom_call_target="tpu_custom_call" | custom-call | tf_op jit(solution)/shard_map/pallas_call | solution.py:710
  82.8 1.5 %shard_map.89 = (bf16[176,2048]{1,0:T(8,128)(2,1)}, bf16[176,512]{1,0:T(8,128)(2,1)}) custom-call(bf16[176,2048]{1,0:T(8,128)(2,1)S(1)} %get-tuple-element.24.layer_ref, bf16[512,192]{1,0:T(8,128)(2,1)S(1)} %get-tuple-element.25.got_ref), custom_call_target="tpu_custom_call" | custom-call | tf_op jit(solution)/shard_map/pallas_call | solution.py:759
Async XLA Ops:
  0.6 1.6 %copy-start = (bf16[3,176,2048]{2,1,0:T(8,128)(2,1)S(1)}, bf16[3,176,2048]{2,1,0:T(8,128)(2,1)}, u32[]{:S(2)}) copy-start(bf16[3,176,2048]{2,1,0:T(8,128)(2,1)} %qkv_ref.1) | copy-start | bytes 6488068
  2.2 1.6 %copy-start.1 = (bf16[176,5632]{1,0:T(8,128)(2,1)S(1)}, bf16[176,5632]{1,0:T(8,128)(2,1)}, u32[]{:S(2)}) copy-start(bf16[176,5632]{1,0:T(8,128)(2,1)} %merge_weight_ref.3) | copy-start | bytes 5947396
  3.8 1.1 %copy-start.4 = (bf16[176,2048]{1,0:T(8,128)(2,1)S(1)}, bf16[176,2048]{1,0:T(8,128)(2,1)}, u32[]{:S(2)}) copy-start(bf16[176,2048]{1,0:T(8,128)(2,1)} %res.1) | copy-start | bytes 2162692
  4.9 0.7 copy-start.7
  34.1 4.4 %copy-start.2 = (bf16[176,5632]{1,0:T(8,128)(2,1)S(1)}, bf16[176,5632]{1,0:T(8,128)(2,1)}, u32[]{:S(2)}) copy-start(bf16[176,5632]{1,0:T(8,128)(2,1)} %merge_weight_ref.3) | copy-start | bytes 5947396
  34.1 4.4 %copy-start.3 = (bf16[1408,1408]{1,0:T(8,128)(2,1)S(1)}, bf16[1408,1408]{1,0:T(8,128)(2,1)}, u32[]{:S(2)}) copy-start(bf16[1408,1408]{1,0:T(8,128)(2,1)} %weight.1) | copy-start | bytes 11894788
  34.1 4.4 %copy-start.5 = (f32[1408]{0:T(1024)S(1)}, f32[1408]{0:T(1024)}, u32[]{:S(2)}) copy-start(f32[1408]{0:T(1024)} %param.11) | copy-start | bytes 16900
  34.1 4.4 %copy-start.6 = (s32[512]{0:T(512)S(1)}, s32[512]{0:T(512)}, u32[]{:S(2)}) copy-start(s32[512]{0:T(512)} %param.13) | copy-start | bytes 6148

commit v6 on v5

--- a/solution.py
+++ b/solution.py
@@ -11,7 +11,6 @@
 HEAD_DIM = 88
 QB = 256
 KB = 256
-NEAR = 2
 PIECES = 2
 NEG = -1e30
 MESH = pl.DeviceIdType.MESH
@@ -57,10 +56,10 @@
     rows,
     cols,
     coef,
-    qkv,
-    res,
-    merge_weight_ref,
-    groups_line_ref,
+    qkv_hbm,
+    res_hbm,
+    merge_weight_hbm,
+    groups_hbm,
     left_hbm,
     right_hbm,
     spread_hbm,
@@ -68,9 +67,8 @@
     m_ref,
     l_ref,
     acc_ref,
-    kt,
-    vt,
     bound_ref,
+    q_ref,
     load_sem,
     halo_send,
     halo_recv,
@@ -78,10 +76,17 @@
     res_recv,
     far_send,
     far_recv,
+    held_scores,
+    kt,
+    vt,
+    kv,
+    res,
+    far,
+    groups_line_ref,
 ):
     row = lax.axis_index("row")
     me = lax.axis_index("col")
-    _, width, tokens = qkv.shape
+    width, tokens = q_ref.shape
     reach = left_hbm.shape[2]
     blocks = tokens // QB
     chunk = tokens // cols
@@ -97,7 +102,20 @@
         )
     mine = pl.ds(pl.multiple_of(me * chunk, chunk), chunk)
     place = pl.ds(pl.multiple_of(me * width, 16), width)
-    keep = pltpu.make_async_copy(res.at[:, mine], spread_hbm.at[place], load_sem)
+    part = row // (rows // 4)
+    piece = merge_weight_hbm.at[:, pl.ds(pl.multiple_of(part * full, 128), full)]
+    loads = [
+        pltpu.make_async_copy(qkv_hbm.at[i], target, load_sem.at[i])
+        for i, target in ((1, kv.at[0]), (2, kv.at[1]), (0, q_ref))
+    ]
+    loads.append(pltpu.make_async_copy(res_hbm, res, load_sem.at[3]))
+    loads.append(pltpu.make_async_copy(piece, far, load_sem.at[4]))
+    loads.append(pltpu.make_async_copy(groups_hbm, groups_line_ref, load_sem.at[6]))
+    for load in loads:
+        load.start()
+    for load in loads:
+        load.wait()
+    keep = pltpu.make_async_copy(res.at[:, mine], spread_hbm.at[place], load_sem.at[5])
     keep.start()
     pl.semaphore_wait(barrier, cols + 1)
 
@@ -108,7 +126,7 @@
         for i in range(2):
             sent.append(
                 pltpu.make_async_remote_copy(
-                    src_ref=qkv.at[1 + i, :, at : at + reach],
+                    src_ref=kv.at[i, :, at : at + reach],
                     dst_ref=target.at[i],
                     send_sem=halo_send.at[2 * side + i],
                     recv_sem=halo_recv.at[2 * side + i],
@@ -128,10 +146,9 @@
                 device_id_type=MESH,
             )
         )
-    part = row // (rows // 4)
     sent.append(
         pltpu.make_async_remote_copy(
-            src_ref=merge_weight_ref.at[:, pl.ds(pl.multiple_of(part * full, 128), full)],
+            src_ref=far,
             dst_ref=far_hbm,
             send_sem=far_send,
             recv_sem=far_recv,
@@ -162,8 +179,8 @@
         inside = (token >= begin) & (token < begin + size)
         bound_ref[0:1, pl.ds(at, QB)] = jnp.sum(jnp.where(inside, begin, 0), axis=0, keepdims=True)
         bound_ref[1:2, pl.ds(at, QB)] = jnp.sum(jnp.where(inside, size, 0), axis=0, keepdims=True)
-        kt[pl.ds(at, QB), :] = jnp.transpose(qkv[1, :, pl.ds(at, QB)])
-        v0, v1 = split_heads(qkv[2, :, pl.ds(at, QB)])
+        kt[pl.ds(at, QB), :] = jnp.transpose(kv[0, :, pl.ds(at, QB)])
+        v0, v1 = split_heads(kv[1, :, pl.ds(at, QB)])
         vt[0, :, pl.ds(at, QB)] = v0
         vt[1, :, pl.ds(at, QB)] = v1
         return carry
@@ -172,36 +189,34 @@
 
     def per_block(b, carry):
         at = pl.multiple_of(b * QB, QB)
-        qcat = query_pair(qkv[0, :, pl.ds(at, QB)])
+        qcat = query_pair(q_ref[:, pl.ds(at, QB)])
         start = bound_ref[0:1, pl.ds(at, QB)]
         length = bound_ref[1:2, pl.ds(at, QB)]
-        row_at = b * 2
+        spot = lax.broadcasted_iota(jnp.int32, (KB, QB), 0) - start
+        tops = [jnp.full((1, QB), NEG, jnp.float32) for _ in range(2)]
+        for t in range(blocks):
+            key = t * KB
+            scores = jnp.dot(kt[key : key + KB, :], qcat, preferred_element_type=jnp.float32)
+            ok = (spot >= -key) & (spot < length - key)
+            for head in range(2):
+                part = jnp.where(ok, scores[:, head * QB : (head + 1) * QB], NEG)
+                held_scores[head, t] = part
+                tops[head] = jnp.maximum(tops[head], jnp.max(part, axis=0, keepdims=True))
         for head in range(2):
-            m_ref[row_at + head] = jnp.full((1, QB), NEG, jnp.float32)
-            l_ref[row_at + head] = jnp.zeros((1, QB), jnp.float32)
-            acc_ref[row_at + head] = jnp.zeros((HEAD_DIM, QB), jnp.float32)
-
-        def per_tile(t, inner):
-            key = pl.multiple_of(t * KB, KB)
-            spot = lax.broadcasted_iota(jnp.int32, (KB, QB), 0) + (key - start)
-            ok = (spot >= 0) & (spot < length)
-            tile_step(
-                kt[pl.ds(key, KB), :],
-                vt[0, :, pl.ds(key, KB)],
-                vt[1, :, pl.ds(key, KB)],
-                qcat,
-                ok,
-                coef,
-                row_at,
-                m_ref,
-                l_ref,
-                acc_ref,
-            )
-            return inner
-
-        lax.fori_loop(
-            jnp.maximum(b - NEAR, 0), jnp.minimum(b + NEAR + 1, blocks), per_tile, 0
-        )
+            peak = tops[head] * coef
+            total = jnp.zeros((1, QB), jnp.float32)
+            sums = jnp.zeros((HEAD_DIM, QB), jnp.float32)
+            for t in range(blocks):
+                expo = jnp.exp2(held_scores[head, t] * coef - peak)
+                total = total + jnp.sum(expo, axis=0, keepdims=True)
+                sums = sums + jnp.dot(
+                    vt[head, :, t * KB : (t + 1) * KB],
+                    expo.astype(jnp.bfloat16),
+                    preferred_element_type=jnp.float32,
+                )
+            m_ref[b * 2 + head] = tops[head]
+            l_ref[b * 2 + head] = total
+            acc_ref[b * 2 + head] = sums
         return carry
 
     lax.fori_loop(0, blocks, per_block, 0)
@@ -214,15 +229,13 @@
     coef,
     groups_ref,
     row_ref,
-    qkv_ref,
+    q_ref,
     left_ref,
     right_ref,
     bound_ref,
     m_in,
     l_in,
     acc_in,
-    kt_in,
-    vt_in,
     out_ref,
     low_ref,
     high_ref,
@@ -233,7 +246,7 @@
     acc_ref,
 ):
     reach = left_ref.shape[2]
-    tokens = qkv_ref.shape[2]
+    tokens = q_ref.shape[1]
     blocks = tokens // QB
     base = row_ref[0] * tokens
 
@@ -274,32 +287,29 @@
     def per_block(b, carry):
         at = pl.multiple_of(b * QB, QB)
         row_at = b * 2
-        near_low = jnp.maximum(b - NEAR, 0) * QB
-        near_high = jnp.minimum(b + NEAR + 1, blocks) * QB
-        low, high = low_ref[b], high_ref[b]
-        below = jnp.maximum((near_low - jnp.maximum(low, 0) + KB - 1) // KB, 0)
-        above = jnp.maximum((jnp.minimum(high, tokens) - near_high + KB - 1) // KB, 0)
-        before = jnp.maximum((KB - 1 - low) // KB, 0)
-        after = jnp.maximum((high - tokens + KB - 1) // KB, 0)
+        before = jnp.maximum((KB - 1 - low_ref[b]) // KB, 0)
+        after = jnp.maximum((high_ref[b] - tokens + KB - 1) // KB, 0)
         for head in range(2):
             m_ref[head] = m_in[row_at + head]
             l_ref[head] = l_in[row_at + head]
             acc_ref[head] = acc_in[row_at + head]
 
-        @pl.when(below + above + before + after > 0)
+        @pl.when(before + after > 0)
         def _():
-            qcat = query_pair(qkv_ref[0, :, pl.ds(at, QB)])
+            qcat = query_pair(q_ref[:, pl.ds(at, QB)])
             start = bound_ref[0:1, pl.ds(at, QB)]
             length = bound_ref[1:2, pl.ds(at, QB)]
 
-            def tile(key, slot, k_from, v_from):
+            def halo_tile(t, inner):
+                key = jnp.where(t < before, -(t + 1) * KB, tokens + (t - before) * KB)
+                slot = jnp.where(t < before, reach - (t + 1) * KB, reach + (t - before) * KB)
                 slot = pl.multiple_of(slot, KB)
                 spot = lax.broadcasted_iota(jnp.int32, (KB, QB), 0) + (key - start)
                 ok = (spot >= 0) & (spot < length)
                 tile_step(
-                    k_from[pl.ds(slot, KB), :],
-                    v_from[0, :, pl.ds(slot, KB)],
-                    v_from[1, :, pl.ds(slot, KB)],
+                    kt[pl.ds(slot, KB), :],
+                    vt[0, :, pl.ds(slot, KB)],
+                    vt[1, :, pl.ds(slot, KB)],
                     qcat,
                     ok,
                     coef,
@@ -308,21 +318,8 @@
                     l_ref,
                     acc_ref,
                 )
-
-            def own_tile(t, inner):
-                key = jnp.where(
-                    t < below, near_low - (t + 1) * KB, near_high + (t - below) * KB
-                )
-                tile(key, key, kt_in, vt_in)
                 return inner
 
-            def halo_tile(t, inner):
-                key = jnp.where(t < before, -(t + 1) * KB, tokens + (t - before) * KB)
-                slot = jnp.where(t < before, reach - (t + 1) * KB, reach + (t - before) * KB)
-                tile(key, slot, kt, vt)
-                return inner
-
-            lax.fori_loop(0, below + above, own_tile, 0)
             lax.fori_loop(0, before + after, halo_tile, 0)
 
         both = [acc_ref[head] * (1.0 / l_ref[head]) for head in range(2)]
@@ -345,7 +342,7 @@
     dma = pltpu.SemaphoreType.DMA
     halo = jax.ShapeDtypeStruct((2, width, reach), bf16)
     stat = jax.ShapeDtypeStruct((2 * blocks, 1, QB), f32)
-    left, right, spread, far, m, l, acc, kt, vt, bound = pl.pallas_call(
+    left, right, spread, far, m, l, acc, bound, q = pl.pallas_call(
         functools.partial(head_kernel, rows, cols, coef),
         out_shape=(
             halo,
@@ -355,29 +352,35 @@
             stat,
             stat,
             jax.ShapeDtypeStruct((2 * blocks, HEAD_DIM, QB), f32),
-            jax.ShapeDtypeStruct((tokens, width), bf16),
-            jax.ShapeDtypeStruct((2, HEAD_DIM, tokens), bf16),
             jax.ShapeDtypeStruct((8, tokens), jnp.int32),
+            jax.ShapeDtypeStruct((width, tokens), bf16),
         ),
-        in_specs=[vmem, vmem, vmem, vmem],
-        out_specs=(hbm, hbm, hbm, hbm, vmem, vmem, vmem, vmem, vmem, vmem),
+        in_specs=[hbm, hbm, hbm, hbm],
+        out_specs=(hbm, hbm, hbm, hbm, vmem, vmem, vmem, vmem, vmem),
         scratch_shapes=[
-            dma,
+            dma((7,)),
             dma((4,)),
             dma((4,)),
             dma((cols,)),
             dma((cols,)),
             dma,
             dma,
+            pltpu.VMEM((2, blocks, KB, QB), f32),
+            pltpu.VMEM((tokens, width), bf16),
+            pltpu.VMEM((2, HEAD_DIM, tokens), bf16),
+            pltpu.VMEM((2, width, tokens), bf16),
+            pltpu.VMEM((width, tokens), bf16),
+            pltpu.VMEM((width, full), bf16),
+            pltpu.VMEM((1, image_groups.shape[0]), jnp.int32),
         ],
         compiler_params=pltpu.CompilerParams(
-            collective_id=1, has_side_effects=True, vmem_limit_bytes=20 << 20
+            collective_id=1, has_side_effects=True, vmem_limit_bytes=50331648
         ),
     )(qkv, residual, merge_weight, image_groups[None, :])
     attended = pl.pallas_call(
         functools.partial(far_kernel, coef),
         out_shape=jax.ShapeDtypeStruct((width, tokens), bf16),
-        in_specs=[smem, smem] + [vmem] * 9,
+        in_specs=[smem, smem] + [vmem] * 7,
         out_specs=vmem,
         scratch_shapes=[
             pltpu.SMEM((blocks,), jnp.int32),
@@ -389,7 +392,7 @@
             pltpu.VMEM((2, HEAD_DIM, QB), f32),
         ],
         compiler_params=pltpu.CompilerParams(vmem_limit_bytes=20 << 20),
-    )(image_groups, row_id[None], qkv, left, right, bound, m, l, acc, kt, vt)
+    )(image_groups, row_id[None], q, left, right, bound, m, l, acc)
     return attended, spread, far
 
 

time: 84.6 us -> 79.4 us (0.939)
  local copies, waits for them, and re-layouts: 4.94 us -> 2.16 us
  Pallas kernels: 78.7 us -> 76.4 us
    pallas_call x1, Pallas kernels: 4.36 us -> 1.12 us  [attention(): pl.pallas_call(functools.partial(far_kernel, coef), out_shape=jax.ShapeDt...]
    unnamed x16 -> x12, local copies, waits for them, and re-layouts: 4.94 us -> 2.16 us
    pallas_call x1, Pallas kernels: 44.3 us -> 45.1 us  [tail(): pl.pallas_call(functools.partial(tail_kernel, rows, cols), out_shape=(jax...]
where the time goes in v6:
time: 79.4 us; the launch traced here: 79.2 us
  Pallas kernels  76.4 us (96%)
  local copies, waits for them, and re-layouts  2.16 us (3%)
    pallas_call x1, Pallas kernels, tail(): pl.pallas_call(functools.partial(tail_kernel, rows, cols), out_shape=(jax...  45.1 us
    pallas_call x1, Pallas kernels, attention(): pl.pallas_call(functools.partial(head_kernel, rows, cols, coef), out_shap...  28.6 us
    unnamed x12, local copies, waits for them, and re-layouts  2.16 us

profile of v6, /device:TPU:0, one launch (start us, length us, event | category | flops | bytes accessed | tf_op | source)
XLA Modules:
  0.0 79.2 jit_solution(17016318209864471336)
XLA Ops:
  0.6 0.0 copy-start.2
  0.6 1.1 %copy-done.2 = bf16[176,2048]{1,0:T(8,128)(2,1)S(1)} copy-done((bf16[176,2048]{1,0:T(8,128)(2,1)S(1)}, bf16[176,2048]{1,0:T(8,128)(2,1)}, u32[]{:S(2)}) %copy-start.2) | copy-done | bytes 720920
  1.7 0.0 copy-start.5
  1.7 0.7 copy-done.5
  2.4 0.0 copy-start.1
  2.4 28.6 %shard_map.86 = (bf16[2,176,1024]{2,1,0:T(8,128)(2,1)S(1)}, bf16[2,176,1024]{2,1,0:T(8,128)(2,1)S(1)}, bf16[1408,256]{1,0:T(8,128)(2,1)S(1)}, bf16[176,1408]{1,0...) custom-call(bf16[3,176,2048]{2,1,0:T(8,128)(2,1)} %qkv_hbm.1, ...), custom_call_target="tpu_custom_call" | custom-call | tf_op jit(solution)/shard_map/pallas_call | solution.py:345
  31.0 0.0 copy-start
  31.0 0.0 copy-start.3
  31.0 0.0 copy-start.4
  31.0 1.1 %shard_map.87.attended_ref = bf16[176,2048]{1,0:T(8,128)(2,1)S(1)} custom-call(s32[64]{0:T(128)S(1)} %copy-done.5, s32[1]{0:T(128)} %bitcast.row_ref, bf16[176,2048]{1,0:T(8,128)(2,1)S(1)} %get-tuple-element.13.q_ref, bf16[2,176,1024]{2,1,0:T(8,128)(2,1)S(1)} %get-tuple-element.14.left_ref, bf16[2,176,1024]{2,1,0:T(8,128)(2,1)S(1)} %get-tuple-element.15.right_ref, ...), custom_call_target="tpu_custom_call" | custom-call | tf_op jit(solution)/shard_map/pallas_call | solution.py:380
  32.1 0.0 copy-done.1
  32.1 0.4 copy-done
  32.5 0.0 copy-done.3
  32.5 0.0 copy-done.4
  32.5 45.1 %shard_map.88 = (bf16[176,2048]{1,0:T(8,128)(2,1)S(1)}, bf16[512,192]{1,0:T(8,128)(2,1)S(1)}) custom-call(bf16[176,2048]{1,0:T(8,128)(2,1)S(1)} %shard_map.87.attended_ref, bf16[1408,256]{1,0:T(8,128)(2,1)S(1)} %get-tuple-element.20.residual_ref, bf16[1408,1408]{1,0:T(8,128)(2,1)S(1)} %copy-done.1, bf16[176,5632]{1,0:T(8,128)(2,1)S(1)} %copy-done, ...), custom_call_target="tpu_custom_call" | custom-call | tf_op jit(solution)/shard_map/pallas_call | solution.py:713
  77.7 1.5 %shard_map.89 = (bf16[176,2048]{1,0:T(8,128)(2,1)}, bf16[176,512]{1,0:T(8,128)(2,1)}) custom-call(bf16[176,2048]{1,0:T(8,128)(2,1)S(1)} %get-tuple-element.22.layer_ref, bf16[512,192]{1,0:T(8,128)(2,1)S(1)} %get-tuple-element.23.got_ref), custom_call_target="tpu_custom_call" | custom-call | tf_op jit(solution)/shard_map/pallas_call | solution.py:762
Async XLA Ops:
  0.6 1.1 %copy-start.2 = (bf16[176,2048]{1,0:T(8,128)(2,1)S(1)}, bf16[176,2048]{1,0:T(8,128)(2,1)}, u32[]{:S(2)}) copy-start(bf16[176,2048]{1,0:T(8,128)(2,1)} %res_hbm.1) | copy-start | bytes 2162692
  1.7 0.7 copy-start.5
  2.4 29.7 %copy-start.1 = (bf16[1408,1408]{1,0:T(8,128)(2,1)S(1)}, bf16[1408,1408]{1,0:T(8,128)(2,1)}, u32[]{:S(2)}) copy-start(bf16[1408,1408]{1,0:T(8,128)(2,1)} %weight.1) | copy-start | bytes 11894788
  31.0 1.6 %copy-start = (bf16[176,5632]{1,0:T(8,128)(2,1)S(1)}, bf16[176,5632]{1,0:T(8,128)(2,1)}, u32[]{:S(2)}) copy-start(bf16[176,5632]{1,0:T(8,128)(2,1)} %merge_weight_ref.1) | copy-start | bytes 5947396
  31.0 1.5 %copy-start.3 = (f32[1408]{0:T(1024)S(1)}, f32[1408]{0:T(1024)}, u32[]{:S(2)}) copy-start(f32[1408]{0:T(1024)} %param.11) | copy-start | bytes 16900
  31.0 1.5 %copy-start.4 = (s32[512]{0:T(512)S(1)}, s32[512]{0:T(512)}, u32[]{:S(2)}) copy-start(s32[512]{0:T(512)} %param.13) | copy-start | bytes 6148

commit v7 on v6

v7 whole, which is shorter than its diff:
```python
import functools
import math

import jax
import jax.numpy as jnp
from jax import lax
from jax.experimental import pallas as pl
from jax.experimental.pallas import tpu as pltpu
from jax.sharding import PartitionSpec as P

HEAD_DIM = 88
QB = 256
KB = 256
HB = 512
PIECES = 2
NEG = -1e30
MESH = pl.DeviceIdType.MESH


def halo_step(keys, values, qcat, ok, coef, m_ref, l_ref, acc_ref):
    width = qcat.shape[1] // 2
    scores = jnp.dot(keys, qcat, preferred_element_type=jnp.float32)
    for head in range(2):
        part = jnp.where(ok, scores[:, head * width : (head + 1) * width], NEG)
        old = m_ref[head]
        new = jnp.maximum(old, jnp.max(part, axis=0, keepdims=True))
        fade = jnp.exp2((old - new) * coef)
        expo = jnp.exp2(part * coef - new * coef)
        l_ref[head] = l_ref[head] * fade + jnp.sum(expo, axis=0, keepdims=True)
        m_ref[head] = new
        acc_ref[head] = acc_ref[head] * fade + jnp.dot(
            values[head], expo.astype(jnp.bfloat16), preferred_element_type=jnp.float32
        )


def split_heads(values):
    wide = values.astype(jnp.float32)
    return wide[:HEAD_DIM].astype(jnp.bfloat16), wide[HEAD_DIM:].astype(jnp.bfloat16)


def query_pair(block):
    feature = lax.broadcasted_iota(jnp.int32, block.shape, 0)
    zero = jnp.zeros_like(block)
    return jnp.concatenate(
        [jnp.where(feature < HEAD_DIM, block, zero), jnp.where(feature < HEAD_DIM, zero, block)],
        axis=1,
    )


def layer_kernel(
    rows,
    cols,
    coef,
    qkv_hbm,
    residual_hbm,
    out_weight_hbm,
    merge_weight_hbm,
    gain_hbm,
    groups_hbm,
    dest_hbm,
    layer_ref,
    got_rows,
    q_ref,
    kv,
    kt,
    vt,
    left,
    right,
    halo_kt,
    halo_vt,
    bound_ref,
    held_scores,
    m_ref,
    l_ref,
    acc_ref,
    attended,
    res,
    residual,
    att,
    weight,
    weight_t,
    merge_w,
    layer_rows,
    held,
    far_rows,
    merged,
    pick,
    sorted_rows,
    gain_column,
    gain_ref,
    groups_line_ref,
    dest_ref,
    load_sem,
    halo_send,
    halo_recv,
    res_send,
    res_recv,
    shift_send,
    shift_recv,
    gather_send,
    gather_recv,
    spread_send,
    spread_recv,
    back_send,
    back_recv,
    near_send,
    near_recv,
    own_send,
    own_recv,
    pass_send,
    pass_recv,
    far_send,
    far_recv,
    row_send,
    row_recv,
):
    row = lax.axis_index("row")
    me = lax.axis_index("col")
    width, tokens = q_ref.shape
    full = weight.shape[0]
    reach = left.shape[2]
    blocks = tokens // QB
    chunk = tokens // cols
    piece = chunk // PIECES
    part = piece // 4
    groups = tokens // 4
    share = groups // rows
    chips = cols // 2
    core = me % 2
    chip = me // 2
    sibling = me + 1 - 2 * core
    half = full // 2
    line_up = rows // 4
    x_at, z_at = row // line_up, row % line_up

    barrier = pltpu.get_barrier_semaphore()
    for k in range(1, cols):
        pl.semaphore_signal(
            barrier, inc=1, device_id={"col": (me + k) % cols}, device_id_type=MESH
        )
    for k in range(1, rows):
        pl.semaphore_signal(
            barrier, inc=1, device_id={"row": (row + k) % rows}, device_id_type=MESH
        )
    loads = [
        pltpu.make_async_copy(source, target, load_sem.at[i])
        for i, (source, target) in enumerate(
            (
                (qkv_hbm.at[1], kv.at[0]),
                (qkv_hbm.at[2], kv.at[1]),
                (merge_weight_hbm, merge_w.at[0:width]),
                (residual_hbm, res),
                (groups_hbm, groups_line_ref),
                (qkv_hbm.at[0], q_ref),
                (gain_hbm, gain_ref),
                (dest_hbm, dest_ref),
                (out_weight_hbm, weight),
            )
        )
    ]
    for load in loads:
        load.start()
    for load in loads[:4]:
        load.wait()
    pl.semaphore_wait(barrier, rows + cols - 2)

    after_row, before_row = (row + 1) % rows, (row + rows - 1) % rows
    mine = pl.ds(pl.multiple_of(me * chunk, chunk), chunk)
    my_rows = pl.ds(pl.multiple_of(me * width, 16), width)
    halo = []
    for side, (other, target, at) in enumerate(
        ((after_row, left, tokens - reach), (before_row, right, 0))
    ):
        for i in range(2):
            halo.append(
                pltpu.make_async_remote_copy(
                    src_ref=kv.at[i, :, at : at + reach],
                    dst_ref=target.at[i],
                    send_sem=halo_send.at[2 * side + i],
                    recv_sem=halo_recv.at[2 * side + i],
                    device_id={"row": other},
                    device_id_type=MESH,
                )
            )
    cut = width // 32 * 16 + 16
    spans = ((0, cut, x_at), (cut, width, z_at))
    shift, gather = [], []
    for s, (top, end, at) in enumerate(spans):
        across = pl.ds(pl.multiple_of(at * full, 128), full)
        place = merge_w.at[width + top : width + end, across]
        shift.append(
            pltpu.make_async_remote_copy(
                src_ref=merge_w.at[top:end, across],
                dst_ref=place,
                send_sem=shift_send.at[s],
                recv_sem=shift_recv.at[s],
                device_id={"col": (me + cols // 2) % cols},
                device_id_type=MESH,
            )
        )
        for k in range(1, 4):
            other = x_at * line_up + (z_at + k) % line_up if s else (row + k * line_up) % rows
            gather.append(
                pltpu.make_async_remote_copy(
                    src_ref=place,
                    dst_ref=place,
                    send_sem=gather_send.at[s, k],
                    recv_sem=gather_recv.at[s, k],
                    device_id={"row": other},
                    device_id_type=MESH,
                )
            )
    resident = []
    for k in range(1, cols):
        to = (me + k) % cols
        resident.append(
            pltpu.make_async_remote_copy(
                src_ref=res.at[:, pl.ds(pl.multiple_of(to * chunk, chunk), chunk)],
                dst_ref=residual.at[my_rows],
                send_sem=res_send.at[k],
                recv_sem=res_recv.at[k],
                device_id={"col": to},
                device_id_type=MESH,
            )
        )
    for copy in halo + shift + resident:
        copy.start()
    residual[my_rows, :] = res[:, mine]
    for load in loads[4:]:
        load.wait()

    images = groups_line_ref.shape[1]
    first = lax.broadcasted_iota(jnp.int32, (images, images), 0)
    second = lax.broadcasted_iota(jnp.int32, (images, images), 1)
    sizes = groups_line_ref[...]
    size = jnp.sum(jnp.where(second == first, sizes, 0), axis=1, keepdims=True) * 4
    begin = (
        jnp.sum(jnp.where(second < first, sizes, 0), axis=1, keepdims=True) * 4 - row * tokens
    )

    def prepare(b, carry):
        at = pl.multiple_of(b * QB, QB)
        token = lax.broadcasted_iota(jnp.int32, (images, QB), 1) + at
        inside = (token >= begin) & (token < begin + size)
        bound_ref[0:1, pl.ds(at, QB)] = jnp.sum(jnp.where(inside, begin, 0), axis=0, keepdims=True)
        bound_ref[1:2, pl.ds(at, QB)] = jnp.sum(jnp.where(inside, size, 0), axis=0, keepdims=True)
        kt[pl.ds(at, QB), :] = jnp.transpose(kv[0, :, pl.ds(at, QB)])
        v0, v1 = split_heads(kv[1, :, pl.ds(at, QB)])
        vt[0, :, pl.ds(at, QB)] = v0
        vt[1, :, pl.ds(at, QB)] = v1
        return carry

    lax.fori_loop(0, blocks, prepare, 0)

    def local_block(b, carry):
        at = pl.multiple_of(b * QB, QB)
        qcat = query_pair(q_ref[:, pl.ds(at, QB)])
        start = bound_ref[0:1, pl.ds(at, QB)]
        length = bound_ref[1:2, pl.ds(at, QB)]
        spot = lax.broadcasted_iota(jnp.int32, (KB, QB), 0) - start
        tops = [jnp.full((1, QB), NEG, jnp.float32) for _ in range(2)]
        for t in range(blocks):
            key = t * KB
            scores = jnp.dot(kt[key : key + KB, :], qcat, preferred_element_type=jnp.float32)
            ok = (spot >= -key) & (spot < length - key)
            for head in range(2):
                masked = jnp.where(ok, scores[:, head * QB : (head + 1) * QB], NEG)
                held_scores[head, t] = masked
                tops[head] = jnp.maximum(tops[head], jnp.max(masked, axis=0, keepdims=True))
        for head in range(2):
            peak = tops[head] * coef
            total = jnp.zeros((1, QB), jnp.float32)
            sums = jnp.zeros((HEAD_DIM, QB), jnp.float32)
            for t in range(blocks):
                expo = jnp.exp2(held_scores[head, t] * coef - peak)
                total = total + jnp.sum(expo, axis=0, keepdims=True)
                sums = sums + jnp.dot(
                    vt[head, :, t * KB : (t + 1) * KB],
                    expo.astype(jnp.bfloat16),
                    preferred_element_type=jnp.float32,
                )
            m_ref[b * 2 + head] = tops[head]
            l_ref[b * 2 + head] = total
            acc_ref[b * 2 + head] = sums
        return carry

    lax.fori_loop(0, blocks, local_block, 0)

    def turn(i, carry):
        at = pl.multiple_of(i * 128, 128)
        weight_t[pl.ds(at, 128), :] = jnp.transpose(weight[:, pl.ds(at, 128)])
        return carry

    lax.fori_loop(0, full // 128, turn, 0)
    for i in range(full // 128):
        gain_column[i * 128 : (i + 1) * 128, :] = jnp.transpose(
            jnp.broadcast_to(gain_ref[i : i + 1, :], (8, 128))
        )

    before, after, across_chip = (chip + 3) % chips, (chip + 1) % chips, (chip + 2) % chips
    of = [dest_ref[pl.ds(c, 1), :] for c in (chip, before, across_chip, after)]
    span = chunk // 4
    line = jnp.concatenate(
        [
            of[c][:, k * span + p * part : k * span + (p + 1) * part]
            for order in (((0, 0), (0, 1), (1, 0), (3, 1)), ((2, 0), (2, 1), (3, 0), (1, 1)))
            for p in range(PIECES)
            for c, k in order
        ],
        axis=1,
    )
    owner_line = line // groups
    owner_column = jnp.transpose(
        jnp.broadcast_to(owner_line.astype(jnp.float32), (8, groups))
    )[:, 0:1].astype(jnp.int32)
    down = lax.broadcasted_iota(jnp.int32, (groups, groups), 0)
    across = lax.broadcasted_iota(jnp.int32, (groups, groups), 1)
    earlier = (owner_column == owner_line) & (down < across)
    rank = jnp.sum(earlier.astype(jnp.int32), axis=0, keepdims=True)
    pick[...] = jnp.where(down == owner_line * share + rank, 1.0, 0.0).astype(jnp.bfloat16)
    slot = line % groups
    which = lax.broadcasted_iota(jnp.int32, (merged.shape[0] - width, groups), 0)
    digits = jnp.where(which == 0, slot // 16, jnp.where(which == 1, slot % 16, 0))
    merged[width:, :] = digits.astype(jnp.float32).astype(jnp.bfloat16)

    for copy in shift:
        copy.wait_recv()
    for copy in gather:
        copy.start()
    for copy in halo:
        copy.wait_recv()

    def prepare_halo(i, carry):
        at = pl.multiple_of(i * QB, QB)
        for source, base in ((left, 0), (right, reach)):
            to = pl.ds(pl.multiple_of(base + at, QB), QB)
            halo_kt[to, :] = jnp.transpose(source[0, :, pl.ds(at, QB)])
            v0, v1 = split_heads(source[1, :, pl.ds(at, QB)])
            halo_vt[0, :, to] = v0
            halo_vt[1, :, to] = v1
        return carry

    lax.fori_loop(0, reach // QB, prepare_halo, 0)

    def spread_copy(k):
        to = (me + k) % cols
        return pltpu.make_async_remote_copy(
            src_ref=attended.at[to],
            dst_ref=att.at[my_rows],
            send_sem=spread_send.at[k],
            recv_sem=spread_recv.at[k],
            device_id={"col": to},
            device_id_type=MESH,
        )

    def halo_block(b):
        at = pl.multiple_of(b * QB, QB)
        qcat = query_pair(q_ref[:, pl.ds(at, QB)])
        start = bound_ref[0:1, pl.ds(at, QB)]
        length = bound_ref[1:2, pl.ds(at, QB)]
        high = b // (blocks // 2)
        tiles = high * (b - blocks // 2 + 1) + (1 - high) * (blocks // 2 - b)

        def pair(t, inner):
            slot = high * (reach + t * HB) + (1 - high) * (reach - (t + 1) * HB)
            slot = pl.multiple_of(slot, HB)
            key = slot - reach + high * tokens
            spot = lax.broadcasted_iota(jnp.int32, (HB, QB), 0) + (key - start)
            ok = (spot >= 0) & (spot < length)
            halo_step(
                halo_kt[pl.ds(slot, HB), :],
                [halo_vt[head, :, pl.ds(slot, HB)] for head in range(2)],
                qcat,
                ok,
                coef,
                m_ref.at[pl.ds(b * 2, 2)],
                l_ref.at[pl.ds(b * 2, 2)],
                acc_ref.at[pl.ds(b * 2, 2)],
            )
            return inner

        lax.fori_loop(0, (tiles * KB + HB - 1) // HB, pair, 0)
        both = [acc_ref[b * 2 + head] * (1.0 / l_ref[b * 2 + head]) for head in range(2)]
        attended[b] = jnp.concatenate(both, axis=0).astype(jnp.bfloat16)

    def block_of(i, carry):
        halo_block((me + 1 + i) % cols)
        spread_copy(1 + i).start()
        return carry

    lax.fori_loop(0, cols - 1, block_of, 0)
    halo_block(me)
    att[my_rows, :] = attended[me]
    for copy in resident:
        copy.wait()
    for k in range(1, cols):
        spread_copy(k).wait_recv()

    def lanes(owner, p):
        return pl.ds(pl.multiple_of(owner * chunk + p * piece, 128), piece)

    here = lax.broadcasted_iota(jnp.int32, (piece, piece), 0)
    there = lax.broadcasted_iota(jnp.int32, (piece, piece), 1)
    order = jnp.where((here % 4) * part + here // 4 == there, 1.0, 0.0).astype(jnp.bfloat16)
    goal = (chip + 1 + 2 * core) % chips
    near, own, back = [], [], []
    for p in range(PIECES):
        at = slice(p * piece, (p + 1) * piece)
        projected = jnp.dot(weight_t[...], att[:, at], preferred_element_type=jnp.float32)
        rounded = (residual[:, at].astype(jnp.float32) + projected).astype(jnp.bfloat16)
        layer_rows[p] = rounded
        values32 = rounded.astype(jnp.float32)
        centre = jnp.sum(values32, axis=0, keepdims=True) * (1.0 / full)
        spread_of = jnp.sum(jnp.square(values32 - centre), axis=0, keepdims=True) * (1.0 / full)
        scale = lax.rsqrt(spread_of + 1e-06)
        normed = ((values32 - centre) * scale * gain_column[:, 0:1]).astype(jnp.bfloat16)
        held[p, core] = jnp.dot(normed, order, preferred_element_type=jnp.float32).astype(
            jnp.bfloat16
        )
        for h in range(2):
            rows_of = pl.ds(h * half, half)
            copy = pltpu.make_async_remote_copy(
                src_ref=held.at[p, core, rows_of],
                dst_ref=held.at[p, 2 + core, rows_of],
                send_sem=near_send.at[p, h],
                recv_sem=near_recv.at[p, core],
                device_id={"col": goal * 2 + h},
                device_id_type=MESH,
            )
            copy.start()
            near.append(copy)
        copy = pltpu.make_async_remote_copy(
            src_ref=held.at[p, core],
            dst_ref=held.at[p, core],
            send_sem=own_send.at[p],
            recv_sem=own_recv.at[p],
            device_id={"col": sibling},
            device_id_type=MESH,
        )
        copy.start()
        own.append(copy)
        layer_ref[:, lanes(me, p)] = layer_rows[p, my_rows, :]

    for k in range(1, cols):
        spread_copy(k).wait_send()
    passed = []
    my_half = pl.ds(pl.multiple_of(core * half, 16), half)
    for p in range(PIECES):
        for s in range(2):
            arrive = pltpu.make_async_remote_copy(
                src_ref=held.at[p, core, my_half],
                dst_ref=held.at[p, 2 + s, my_half],
                send_sem=near_send.at[p, s],
                recv_sem=near_recv.at[p, s],
                device_id={"col": sibling},
                device_id_type=MESH,
            )
            arrive.wait_recv()
            copy = pltpu.make_async_remote_copy(
                src_ref=held.at[p, 2 + s, my_half],
                dst_ref=held.at[p, 2 + s, my_half],
                send_sem=pass_send.at[p, s],
                recv_sem=pass_recv.at[p, s],
                device_id={"col": sibling},
                device_id_type=MESH,
            )
            copy.start()
            passed.append(copy)
    for copy in near:
        copy.wait_send()

    def send_back(p):
        for k in range(1, cols):
            to = (me + k) % cols
            copy = pltpu.make_async_remote_copy(
                src_ref=layer_rows.at[p, pl.ds(pl.multiple_of(to * width, 16), width)],
                dst_ref=layer_ref.at[:, lanes(me, p)],
                send_sem=back_send.at[p, k],
                recv_sem=back_recv.at[p, k],
                device_id={"col": to},
                device_id_type=MESH,
            )
            copy.start()
            back.append(copy)

    for p in range(PIECES - 1):
        send_back(p)
    for copy in gather:
        copy.wait()
    for copy in own + passed:
        copy.wait()

    total = None
    for j in range(4):
        side = jnp.concatenate(
            [
                held[p, s, :, j * part : (j + 1) * part]
                for p in range(PIECES)
                for s in range(4)
            ],
            axis=1,
        )
        term = jnp.dot(
            merge_w[:, j * full : (j + 1) * full], side, preferred_element_type=jnp.float32
        )
        total = term if total is None else total + term
    far_rows[...] = total[width:].astype(jnp.bfloat16)
    across_y = pltpu.make_async_remote_copy(
        src_ref=far_rows,
        dst_ref=merged.at[0:width, chunk : 2 * chunk],
        send_sem=far_send,
        recv_sem=far_recv,
        device_id={"col": (me + cols // 2) % cols},
        device_id_type=MESH,
    )
    across_y.start()
    send_back(PIECES - 1)
    merged[0:width, 0:chunk] = total[:width].astype(jnp.bfloat16)
    across_y.wait()

    sorted_rows[...] = lax.dot_general(
        pick[...], merged[...], (((1,), (1,)), ((), ())), preferred_element_type=jnp.float32
    ).astype(jnp.bfloat16)
    moves = []
    for k in range(1, rows):
        to = (row + k) % rows
        copy = pltpu.make_async_remote_copy(
            src_ref=sorted_rows.at[pl.ds(pl.multiple_of(to * share, share), share)],
            dst_ref=got_rows.at[pl.ds(pl.multiple_of(row * share, share), share)],
            send_sem=row_send.at[k],
            recv_sem=row_recv.at[k],
            device_id={"row": to},
            device_id_type=MESH,
        )
        copy.start()
        moves.append(copy)
    keep = pl.ds(pl.multiple_of(row * share, share), share)
    got_rows[keep, :] = sorted_rows[keep, :]
    for copy in moves + back:
        copy.wait()
    for copy in halo + shift:
        copy.wait_send()


def place_kernel(layer_ref, got_ref, layer_out, image_ref, sem):
    copy = pltpu.make_async_copy(layer_ref, layer_out, sem)
    copy.start()
    width, groups = image_ref.shape
    got = got_ref[...]
    target = got[:, width : width + 1].astype(jnp.float32) * 16.0 + got[
        :, width + 1 : width + 2
    ].astype(jnp.float32)
    slot = lax.broadcasted_iota(jnp.int32, (groups, groups), 1).astype(jnp.float32)
    put = jnp.where(target == slot, 1.0, 0.0).astype(jnp.bfloat16)
    image_ref[...] = lax.dot_general(
        got, put, (((0,), (0,)), ((), ())), preferred_element_type=jnp.float32
    )[:width].astype(jnp.bfloat16)
    copy.wait()


def body(qkv, residual_in, out_weight, merge_weight, merge_gain, image_groups, dest_row):
    rows = lax.axis_size("row")
    cols = lax.axis_size("col")
    _, width, tokens = qkv.shape
    full = out_weight.shape[0]
    reach = tokens // 2
    blocks = tokens // QB
    chunk = tokens // cols
    piece = chunk // PIECES
    groups = tokens // 4
    bf16, f32, i32 = jnp.bfloat16, jnp.float32, jnp.int32
    coef = math.log2(math.e) / math.sqrt(HEAD_DIM)
    vmem = pl.BlockSpec(memory_space=pltpu.VMEM)
    hbm = pl.BlockSpec(memory_space=pl.ANY)
    dma = pltpu.SemaphoreType.DMA
    gain = merge_gain.reshape(-1, 128)
    dest = dest_row.reshape(cols // 2, -1)
    sizes = image_groups[None, :]
    layer, got = pl.pallas_call(
        functools.partial(layer_kernel, rows, cols, coef),
        out_shape=(
            jax.ShapeDtypeStruct((width, tokens), bf16),
            jax.ShapeDtypeStruct((groups, width + 16), bf16),
        ),
        in_specs=[hbm] * 7,
        out_specs=(vmem, vmem),
        scratch_shapes=[
            pltpu.VMEM((width, tokens), bf16),
            pltpu.VMEM((2, width, tokens), bf16),
            pltpu.VMEM((tokens, width), bf16),
            pltpu.VMEM((2, HEAD_DIM, tokens), bf16),
            pltpu.VMEM((2, width, reach), bf16),
            pltpu.VMEM((2, width, reach), bf16),
            pltpu.VMEM((2 * reach, width), bf16),
            pltpu.VMEM((2, HEAD_DIM, 2 * reach), bf16),
            pltpu.VMEM((8, tokens), i32),
            pltpu.VMEM((2, blocks, KB, QB), f32),
            pltpu.VMEM((2 * blocks, 1, QB), f32),
            pltpu.VMEM((2 * blocks, 1, QB), f32),
            pltpu.VMEM((2 * blocks, HEAD_DIM, QB), f32),
            pltpu.VMEM((blocks, width, QB), bf16),
            pltpu.VMEM((width, tokens), bf16),
            pltpu.VMEM((full, chunk), bf16),
            pltpu.VMEM((full, chunk), bf16),
            pltpu.VMEM((full, full), bf16),
            pltpu.VMEM((full, full), bf16),
            pltpu.VMEM((2 * width, merge_weight.shape[1]), bf16),
            pltpu.VMEM((PIECES, full, piece), bf16),
            pltpu.VMEM((PIECES, 4, full, piece), bf16),
            pltpu.VMEM((width, chunk), bf16),
            pltpu.VMEM((width + 16, groups), bf16),
            pltpu.VMEM((groups, groups), bf16),
            pltpu.VMEM((groups, width + 16), bf16),
            pltpu.VMEM((full, 8), f32),
            pltpu.VMEM(gain.shape, f32),
            pltpu.VMEM(sizes.shape, i32),
            pltpu.VMEM(dest.shape, i32),
            dma((9,)),
            dma((4,)),
            dma((4,)),
            dma((cols,)),
            dma((cols,)),
            dma((2,)),
            dma((2,)),
            dma((2, 4)),
            dma((2, 4)),
            dma((cols,)),
            dma((cols,)),
            dma((PIECES, cols)),
            dma((PIECES, cols)),
            dma((PIECES, 2)),
            dma((PIECES, 2)),
            dma((PIECES,)),
            dma((PIECES,)),
            dma((PIECES, 2)),
            dma((PIECES, 2)),
            dma,
            dma,
            dma((rows,)),
            dma((rows,)),
        ],
        compiler_params=pltpu.CompilerParams(
            collective_id=0, has_side_effects=True, vmem_limit_bytes=int(60 * 2**20)
        ),
    )(qkv, residual_in, out_weight, merge_weight, gain, sizes, dest)
    return pl.pallas_call(
        place_kernel,
        out_shape=(
            jax.ShapeDtypeStruct((width, tokens), bf16),
            jax.ShapeDtypeStruct((width, groups), bf16),
        ),
        in_specs=[vmem, vmem],
        out_specs=(hbm, vmem),
        scratch_shapes=[dma],
        compiler_params=pltpu.CompilerParams(vmem_limit_bytes=16 << 20),
    )(layer, got)


def solution(mesh):
    return jax.shard_map(
        body,
        mesh=mesh,
        in_specs=(P(None, "col", "row"), P("col", "row"), P(), P("col", None), P(), P(), P("row")),
        out_specs=(P("col", "row"), P("col", "row")),
        check_vma=False,
    )
```

time: 79.4 us -> 75.5 us (0.951)
  Pallas kernels: 76.4 us -> 72.6 us
    pallas_call x4 -> x2, Pallas kernels: 76.4 us -> 72.6 us  [the longest x1 71.1 us: body(): pl.pallas_call(functools.partial(layer_kernel, rows, cols, coef), out_sha...]
    unnamed x12 -> x4, local copies, waits for them, and re-layouts: 2.16 us -> 2.05 us
where the time goes in v7:
time: 75.5 us; the launch traced here: 75.3 us
  Pallas kernels  72.6 us (96%)
  local copies, waits for them, and re-layouts  2.05 us (3%)
    pallas_call x1, Pallas kernels, body(): pl.pallas_call(functools.partial(layer_kernel, rows, cols, coef), out_sha...  71.1 us
    unnamed x4, local copies, waits for them, and re-layouts  2.05 us
    pallas_call x1, Pallas kernels, body(): pl.pallas_call(place_kernel, out_shape=(jax.ShapeDtypeStruct((width, toke...  1.54 us

profile of v7, /device:TPU:0, one launch (start us, length us, event | category | flops | bytes accessed | tf_op | source)
XLA Modules:
  0.0 75.3 jit_solution(5315594635801544862)
XLA Ops:
  0.6 71.1 %shard_map.86 = (bf16[176,2048]{1,0:T(8,128)(2,1)}, bf16[512,192]{1,0:T(8,128)(2,1)}) custom-call(bf16[3,176,2048]{2,1,0:T(8,128)(2,1)} %qkv_hbm.1, bf16[176,2048]{1,0:T(8,128)(2,1)} %residual_hbm.1, bf16[1408,1408]{1,0:T(8,128)(2,1)} %out_weight_hbm.1, bf16[176,5632]{1,0:T(8,128)(2,1)} %merge_weight_hbm.1, f32[11,128]{1,0:T(8,128)} %bitcast.3, ...), custom_call_target="tpu_custom_call" | custom-call | tf_op jit(solution)/shard_map/pallas_call | solution.py:579
  71.7 0.0 copy-start
  71.7 1.1 %copy-done = bf16[176,2048]{1,0:T(8,128)(2,1)S(1)} copy-done((bf16[176,2048]{1,0:T(8,128)(2,1)S(1)}, bf16[176,2048]{1,0:T(8,128)(2,1)}, u32[]{:S(2)}) %copy-start) | copy-done | bytes 720920
  72.8 0.0 copy-start.1
  72.8 0.9 %copy-done.1 = bf16[512,192]{1,0:T(8,128)(2,1)S(1)} copy-done((bf16[512,192]{1,0:T(8,128)(2,1)S(1)}, bf16[512,192]{1,0:T(8,128)(2,1)}, u32[]{:S(2)}) %copy-start.1) | copy-done | bytes 196632
  73.8 1.5 %shard_map.87 = (bf16[176,2048]{1,0:T(8,128)(2,1)}, bf16[176,512]{1,0:T(8,128)(2,1)}) custom-call(bf16[176,2048]{1,0:T(8,128)(2,1)S(1)} %copy-done, bf16[512,192]{1,0:T(8,128)(2,1)S(1)} %copy-done.1), custom_call_target="tpu_custom_call" | custom-call | tf_op jit(solution)/shard_map/pallas_call | solution.py:646
Async XLA Ops:
  71.7 1.1 %copy-start = (bf16[176,2048]{1,0:T(8,128)(2,1)S(1)}, bf16[176,2048]{1,0:T(8,128)(2,1)}, u32[]{:S(2)}) copy-start(bf16[176,2048]{1,0:T(8,128)(2,1)} %get-tuple-element.4.layer_ref) | copy-start | bytes 2162692
  72.8 0.9 %copy-start.1 = (bf16[512,192]{1,0:T(8,128)(2,1)S(1)}, bf16[512,192]{1,0:T(8,128)(2,1)}, u32[]{:S(2)}) copy-start(bf16[512,192]{1,0:T(8,128)(2,1)} %get-tuple-element.5.got_ref) | copy-start | bytes 589828

commit v8 on v7

--- a/solution.py
+++ b/solution.py
@@ -223,7 +223,7 @@
                 device_id_type=MESH,
             )
         )
-    for copy in halo + shift + resident:
+    for copy in halo + shift:
         copy.start()
     residual[my_rows, :] = res[:, mine]
     for load in loads[4:]:
@@ -284,7 +284,10 @@
             acc_ref[b * 2 + head] = sums
         return carry
 
-    lax.fori_loop(0, blocks, local_block, 0)
+    lax.fori_loop(0, blocks // 2, local_block, 0)
+    for copy in resident:
+        copy.start()
+    lax.fori_loop(blocks // 2, blocks, local_block, 0)
 
     def turn(i, carry):
         at = pl.multiple_of(i * 128, 128)
@@ -514,9 +517,9 @@
         device_id_type=MESH,
     )
     across_y.start()
-    send_back(PIECES - 1)
     merged[0:width, 0:chunk] = total[:width].astype(jnp.bfloat16)
     across_y.wait()
+    send_back(PIECES - 1)
 
     sorted_rows[...] = lax.dot_general(
         pick[...], merged[...], (((1,), (1,)), ((), ())), preferred_element_type=jnp.float32
@@ -542,9 +545,15 @@
         copy.wait_send()
 
 
-def place_kernel(layer_ref, got_ref, layer_out, image_ref, sem):
-    copy = pltpu.make_async_copy(layer_ref, layer_out, sem)
-    copy.start()
+def place_kernel(layer_hbm, got_hbm, layer_out, image_ref, layer, got_ref, sem):
+    load = pltpu.make_async_copy(got_hbm, got_ref, sem.at[0])
+    copies = [
+        pltpu.make_async_copy(layer_hbm, layer, sem.at[1]),
+        pltpu.make_async_copy(layer, layer_out, sem.at[2]),
+    ]
+    load.start()
+    copies[0].start()
+    load.wait()
     width, groups = image_ref.shape
     got = got_ref[...]
     target = got[:, width : width + 1].astype(jnp.float32) * 16.0 + got[
@@ -552,10 +561,12 @@
     ].astype(jnp.float32)
     slot = lax.broadcasted_iota(jnp.int32, (groups, groups), 1).astype(jnp.float32)
     put = jnp.where(target == slot, 1.0, 0.0).astype(jnp.bfloat16)
+    copies[0].wait()
+    copies[1].start()
     image_ref[...] = lax.dot_general(
         got, put, (((0,), (0,)), ((), ())), preferred_element_type=jnp.float32
     )[:width].astype(jnp.bfloat16)
-    copy.wait()
+    copies[1].wait()
 
 
 def body(qkv, residual_in, out_weight, merge_weight, merge_gain, image_groups, dest_row):
@@ -649,10 +660,14 @@
             jax.ShapeDtypeStruct((width, tokens), bf16),
             jax.ShapeDtypeStruct((width, groups), bf16),
         ),
-        in_specs=[vmem, vmem],
+        in_specs=[hbm, hbm],
         out_specs=(hbm, vmem),
-        scratch_shapes=[dma],
-        compiler_params=pltpu.CompilerParams(vmem_limit_bytes=16 << 20),
+        scratch_shapes=[
+            pltpu.VMEM((width, tokens), bf16),
+            pltpu.VMEM((groups, width + 16), bf16),
+            dma((3,)),
+        ],
+        compiler_params=pltpu.CompilerParams(vmem_limit_bytes=60 << 20),
     )(layer, got)
 
 

time: 75.5 us -> 74 us (0.980)
  local copies, waits for them, and re-layouts: 2.05 us -> 0 us
    unnamed x4 -> x0, local copies, waits for them, and re-layouts: 2.05 us -> none
    pallas_call x1, Pallas kernels: 1.54 us -> 2.85 us  [body(): pl.pallas_call(place_kernel, out_shape=(jax.ShapeDtypeStruct((width, toke...]
    pallas_call x1, Pallas kernels: 71.1 us -> 70.2 us  [body(): pl.pallas_call(functools.partial(layer_kernel, rows, cols, coef), out_sha...]
where the time goes in v8:
time: 74 us; the launch traced here: 73.9 us
  Pallas kernels  73.1 us (99%)
  between operations  0.8 us (1%)
    pallas_call x1, Pallas kernels, body(): pl.pallas_call(functools.partial(layer_kernel, rows, cols, coef), out_sha...  70.2 us
    pallas_call x1, Pallas kernels, body(): pl.pallas_call(place_kernel, out_shape=(jax.ShapeDtypeStruct((width, toke...  2.85 us

profile of v8, /device:TPU:0, one launch (start us, length us, event | category | flops | bytes accessed | tf_op | source)
XLA Modules:
  0.0 73.9 jit_solution(13975030639135308191)
XLA Ops:
  0.6 70.2 %shard_map.86 = (bf16[176,2048]{1,0:T(8,128)(2,1)}, bf16[512,192]{1,0:T(8,128)(2,1)}) custom-call(bf16[3,176,2048]{2,1,0:T(8,128)(2,1)} %qkv_hbm.1, bf16[176,2048]{1,0:T(8,128)(2,1)} %residual_hbm.1, bf16[1408,1408]{1,0:T(8,128)(2,1)} %out_weight_hbm.1, bf16[176,5632]{1,0:T(8,128)(2,1)} %merge_weight_hbm.1, f32[11,128]{1,0:T(8,128)} %bitcast.3, ...), custom_call_target="tpu_custom_call" | custom-call | tf_op jit(solution)/shard_map/pallas_call | solution.py:590
  70.9 2.9 %shard_map.87 = (bf16[176,2048]{1,0:T(8,128)(2,1)}, bf16[176,512]{1,0:T(8,128)(2,1)}) custom-call(bf16[176,2048]{1,0:T(8,128)(2,1)} %get-tuple-element.4.layer_hbm, bf16[512,192]{1,0:T(8,128)(2,1)} %get-tuple-element.5.got_hbm), custom_call_target="tpu_custom_call" | custom-call | tf_op jit(solution)/shard_map/pallas_call | solution.py:657

commit v9 on v8

--- a/solution.py
+++ b/solution.py
@@ -167,40 +167,54 @@
     after_row, before_row = (row + 1) % rows, (row + rows - 1) % rows
     mine = pl.ds(pl.multiple_of(me * chunk, chunk), chunk)
     my_rows = pl.ds(pl.multiple_of(me * width, 16), width)
-    halo = []
+    near_halo, far_halo = [], []
     for side, (other, target, at) in enumerate(
         ((after_row, left, tokens - reach), (before_row, right, 0))
     ):
         for i in range(2):
-            halo.append(
-                pltpu.make_async_remote_copy(
-                    src_ref=kv.at[i, :, at : at + reach],
-                    dst_ref=target.at[i],
-                    send_sem=halo_send.at[2 * side + i],
-                    recv_sem=halo_recv.at[2 * side + i],
+            for h in range(2):
+                to = (h if side else 1 - h) * HB
+                copy = pltpu.make_async_remote_copy(
+                    src_ref=kv.at[i, :, at + to : at + to + HB],
+                    dst_ref=target.at[i, :, to : to + HB],
+                    send_sem=halo_send.at[side, i, h],
+                    recv_sem=halo_recv.at[side, i, h],
                     device_id={"row": other},
                     device_id_type=MESH,
                 )
+                (far_halo if h else near_halo).append(copy)
+    strip = width // 64 * 16
+    top = 4 * strip
+    x_lanes = pl.ds(pl.multiple_of(x_at * full, 128), full)
+    z_lanes = pl.ds(pl.multiple_of(z_at * full, 128), full)
+    my_strip = pl.ds(pl.multiple_of(x_at * strip, 16), strip)
+    far_strip = pl.ds(pl.multiple_of(width + x_at * strip, 16), strip)
+    strip_place = merge_w.at[far_strip, z_lanes]
+    top_place = merge_w.at[width : width + top, z_lanes]
+    low_place = merge_w.at[width + top : 2 * width, x_lanes]
+    shift = [
+        pltpu.make_async_remote_copy(
+            src_ref=source,
+            dst_ref=place,
+            send_sem=shift_send.at[s],
+            recv_sem=shift_recv.at[s],
+            device_id={"col": (me + cols // 2) % cols},
+            device_id_type=MESH,
+        )
+        for s, (source, place) in enumerate(
+            ((merge_w.at[my_strip, z_lanes], strip_place), (merge_w.at[top:width, x_lanes], low_place))
+        )
+    ]
+    by_x, by_z = [], []
+    for k in range(1, 4):
+        for s, (place, other, group) in enumerate(
+            (
+                (strip_place, (row + k * line_up) % rows, by_x),
+                (low_place, (row + k * line_up) % rows, by_x),
+                (top_place, x_at * line_up + (z_at + k) % line_up, by_z),
             )
-    cut = width // 32 * 16 + 16
-    spans = ((0, cut, x_at), (cut, width, z_at))
-    shift, gather = [], []
-    for s, (top, end, at) in enumerate(spans):
-        across = pl.ds(pl.multiple_of(at * full, 128), full)
-        place = merge_w.at[width + top : width + end, across]
-        shift.append(
-            pltpu.make_async_remote_copy(
-                src_ref=merge_w.at[top:end, across],
-                dst_ref=place,
-                send_sem=shift_send.at[s],
-                recv_sem=shift_recv.at[s],
-                device_id={"col": (me + cols // 2) % cols},
-                device_id_type=MESH,
-            )
-        )
-        for k in range(1, 4):
-            other = x_at * line_up + (z_at + k) % line_up if s else (row + k * line_up) % rows
-            gather.append(
+        ):
+            group.append(
                 pltpu.make_async_remote_copy(
                     src_ref=place,
                     dst_ref=place,
@@ -223,7 +237,7 @@
                 device_id_type=MESH,
             )
         )
-    for copy in halo + shift:
+    for copy in near_halo + shift:
         copy.start()
     residual[my_rows, :] = res[:, mine]
     for load in loads[4:]:
@@ -284,10 +298,17 @@
             acc_ref[b * 2 + head] = sums
         return carry
 
-    lax.fori_loop(0, blocks // 2, local_block, 0)
-    for copy in resident:
+    lax.fori_loop(0, 2, local_block, 0)
+    for copy in shift:
+        copy.wait_recv()
+    for copy in by_x + resident:
         copy.start()
-    lax.fori_loop(blocks // 2, blocks, local_block, 0)
+    lax.fori_loop(2, 4, local_block, 0)
+    for copy in near_halo:
+        copy.wait_send()
+    for copy in far_halo:
+        copy.start()
+    lax.fori_loop(4, blocks, local_block, 0)
 
     def turn(i, carry):
         at = pl.multiple_of(i * 128, 128)
@@ -326,24 +347,15 @@
     digits = jnp.where(which == 0, slot // 16, jnp.where(which == 1, slot % 16, 0))
     merged[width:, :] = digits.astype(jnp.float32).astype(jnp.bfloat16)
 
-    for copy in shift:
-        copy.wait_recv()
-    for copy in gather:
-        copy.start()
-    for copy in halo:
-        copy.wait_recv()
-
-    def prepare_halo(i, carry):
-        at = pl.multiple_of(i * QB, QB)
+    def prepare_halo(at, to):
         for source, base in ((left, 0), (right, reach)):
-            to = pl.ds(pl.multiple_of(base + at, QB), QB)
-            halo_kt[to, :] = jnp.transpose(source[0, :, pl.ds(at, QB)])
-            v0, v1 = split_heads(source[1, :, pl.ds(at, QB)])
-            halo_vt[0, :, to] = v0
-            halo_vt[1, :, to] = v1
-        return carry
-
-    lax.fori_loop(0, reach // QB, prepare_halo, 0)
+            here = (reach - HB - at if base == 0 else at) + to
+            span = slice(here, here + QB)
+            slot = slice(base + here, base + here + QB)
+            halo_kt[slot, :] = jnp.transpose(source[0, :, span])
+            v0, v1 = split_heads(source[1, :, span])
+            halo_vt[0, :, slot] = v0
+            halo_vt[1, :, slot] = v1
 
     def spread_copy(k):
         to = (me + k) % cols
@@ -356,43 +368,73 @@
             device_id_type=MESH,
         )
 
-    def halo_block(b):
+    def halo_block(b, t):
         at = pl.multiple_of(b * QB, QB)
         qcat = query_pair(q_ref[:, pl.ds(at, QB)])
         start = bound_ref[0:1, pl.ds(at, QB)]
         length = bound_ref[1:2, pl.ds(at, QB)]
         high = b // (blocks // 2)
-        tiles = high * (b - blocks // 2 + 1) + (1 - high) * (blocks // 2 - b)
-
-        def pair(t, inner):
-            slot = high * (reach + t * HB) + (1 - high) * (reach - (t + 1) * HB)
-            slot = pl.multiple_of(slot, HB)
-            key = slot - reach + high * tokens
-            spot = lax.broadcasted_iota(jnp.int32, (HB, QB), 0) + (key - start)
-            ok = (spot >= 0) & (spot < length)
-            halo_step(
-                halo_kt[pl.ds(slot, HB), :],
-                [halo_vt[head, :, pl.ds(slot, HB)] for head in range(2)],
-                qcat,
-                ok,
-                coef,
-                m_ref.at[pl.ds(b * 2, 2)],
-                l_ref.at[pl.ds(b * 2, 2)],
-                acc_ref.at[pl.ds(b * 2, 2)],
-            )
-            return inner
-
-        lax.fori_loop(0, (tiles * KB + HB - 1) // HB, pair, 0)
+        slot = high * (reach + t * HB) + (1 - high) * (reach - (t + 1) * HB)
+        slot = pl.multiple_of(slot, HB)
+        key = slot - reach + high * tokens
+        spot = lax.broadcasted_iota(jnp.int32, (HB, QB), 0) + (key - start)
+        ok = (spot >= 0) & (spot < length)
+        halo_step(
+            halo_kt[pl.ds(slot, HB), :],
+            [halo_vt[head, :, pl.ds(slot, HB)] for head in range(2)],
+            qcat,
+            ok,
+            coef,
+            m_ref.at[pl.ds(b * 2, 2)],
+            l_ref.at[pl.ds(b * 2, 2)],
+            acc_ref.at[pl.ds(b * 2, 2)],
+        )
+
+    def finish(b, k):
         both = [acc_ref[b * 2 + head] * (1.0 / l_ref[b * 2 + head]) for head in range(2)]
         attended[b] = jnp.concatenate(both, axis=0).astype(jnp.bfloat16)
 
-    def block_of(i, carry):
-        halo_block((me + 1 + i) % cols)
-        spread_copy(1 + i).start()
+        @pl.when(k < cols)
+        def _():
+            spread_copy(k).start()
+
+    def is_middle(b):
+        return (b >= blocks // 4) & (b < blocks - blocks // 4)
+
+    def near_pass(i, carry):
+        b = (me + 1 + i) % cols
+        halo_block(b, 0)
+
+        @pl.when(is_middle(b))
+        def _():
+            finish(b, i + 1)
+
         return carry
 
-    lax.fori_loop(0, cols - 1, block_of, 0)
-    halo_block(me)
+    def far_pass(i, carry):
+        b = (me + 1 + i) % cols
+
+        @pl.when(jnp.logical_not(is_middle(b)))
+        def _():
+            halo_block(b, 1)
+            finish(b, i + 1)
+
+        return carry
+
+    for copy in near_halo:
+        copy.wait_recv()
+    for to in range(0, HB, QB):
+        prepare_halo(0, to)
+    lax.fori_loop(0, cols, near_pass, 0)
+    for copy in far_halo:
+        copy.wait_recv()
+    for copy in by_x:
+        copy.wait()
+    for copy in by_z:
+        copy.start()
+    for to in range(0, HB, QB):
+        prepare_halo(HB, to)
+    lax.fori_loop(0, cols, far_pass, 0)
     att[my_rows, :] = attended[me]
     for copy in resident:
         copy.wait()
@@ -488,7 +530,7 @@
 
     for p in range(PIECES - 1):
         send_back(p)
-    for copy in gather:
+    for copy in by_z:
         copy.wait()
     for copy in own + passed:
         copy.wait()
@@ -541,7 +583,7 @@
     got_rows[keep, :] = sorted_rows[keep, :]
     for copy in moves + back:
         copy.wait()
-    for copy in halo + shift:
+    for copy in far_halo + shift:
         copy.wait_send()
 
 
@@ -627,14 +669,14 @@
             pltpu.VMEM(sizes.shape, i32),
             pltpu.VMEM(dest.shape, i32),
             dma((9,)),
-            dma((4,)),
-            dma((4,)),
+            dma((2, 2, 2)),
+            dma((2, 2, 2)),
             dma((cols,)),
             dma((cols,)),
             dma((2,)),
             dma((2,)),
-            dma((2, 4)),
-            dma((2, 4)),
+            dma((3, 4)),
+            dma((3, 4)),
             dma((cols,)),
             dma((cols,)),
             dma((PIECES, cols)),

time: 74 us -> 80.1 us (1.082); the launches traced: 73.9 us -> 78.7 us
  Pallas kernels: 73.1 us -> 77.9 us
    pallas_call x1, Pallas kernels: 70.2 us -> 75.1 us  [body(): pl.pallas_call(functools.partial(layer_kernel, rows, cols, coef), out_sha...]
where the time goes in v9:
time: 80.1 us; the launch traced here: 78.7 us
  Pallas kernels  77.9 us (97%)
    pallas_call x1, Pallas kernels, body(): pl.pallas_call(functools.partial(layer_kernel, rows, cols, coef), out_sha...  75.1 us
    pallas_call x1, Pallas kernels, body(): pl.pallas_call(place_kernel, out_shape=(jax.ShapeDtypeStruct((width, toke...  2.85 us

profile of v9, /device:TPU:0, one launch (start us, length us, event | category | flops | bytes accessed | tf_op | source)
XLA Modules:
  0.0 78.7 jit_solution(9943423230519640511)
XLA Ops:
  0.6 75.1 %shard_map.86 = (bf16[176,2048]{1,0:T(8,128)(2,1)}, bf16[512,192]{1,0:T(8,128)(2,1)}) custom-call(bf16[3,176,2048]{2,1,0:T(8,128)(2,1)} %qkv_hbm.1, bf16[176,2048]{1,0:T(8,128)(2,1)} %residual_hbm.1, bf16[1408,1408]{1,0:T(8,128)(2,1)} %out_weight_hbm.1, bf16[176,5632]{1,0:T(8,128)(2,1)} %merge_weight_hbm.1, f32[11,128]{1,0:T(8,128)} %bitcast.3, ...), custom_call_target="tpu_custom_call" | custom-call | tf_op jit(solution)/shard_map/pallas_call | solution.py:632
  75.7 2.9 %shard_map.87 = (bf16[176,2048]{1,0:T(8,128)(2,1)}, bf16[176,512]{1,0:T(8,128)(2,1)}) custom-call(bf16[176,2048]{1,0:T(8,128)(2,1)} %get-tuple-element.4.layer_hbm, bf16[512,192]{1,0:T(8,128)(2,1)} %get-tuple-element.5.got_hbm), custom_call_target="tpu_custom_call" | custom-call | tf_op jit(solution)/shard_map/pallas_call | solution.py:699

commit v10 on v9

--- a/solution.py
+++ b/solution.py
@@ -237,7 +237,7 @@
                 device_id_type=MESH,
             )
         )
-    for copy in near_halo + shift:
+    for copy in near_halo + shift + far_halo:
         copy.start()
     residual[my_rows, :] = res[:, mine]
     for load in loads[4:]:
@@ -303,12 +303,7 @@
         copy.wait_recv()
     for copy in by_x + resident:
         copy.start()
-    lax.fori_loop(2, 4, local_block, 0)
-    for copy in near_halo:
-        copy.wait_send()
-    for copy in far_halo:
-        copy.start()
-    lax.fori_loop(4, blocks, local_block, 0)
+    lax.fori_loop(2, blocks, local_block, 0)
 
     def turn(i, carry):
         at = pl.multiple_of(i * 128, 128)
@@ -583,7 +578,7 @@
     got_rows[keep, :] = sorted_rows[keep, :]
     for copy in moves + back:
         copy.wait()
-    for copy in far_halo + shift:
+    for copy in near_halo + far_halo + shift:
         copy.wait_send()
 
 

time: 80.1 us -> 78.4 us (0.979)
  Pallas kernels: 77.9 us -> 76.6 us
    pallas_call x1, Pallas kernels: 75.1 us -> 73.7 us  [body(): pl.pallas_call(functools.partial(layer_kernel, rows, cols, coef), out_sha...]
where the time goes in v10:
time: 78.4 us; the launch traced here: 77.4 us
  Pallas kernels  76.6 us (98%)
  between operations  0.8 us (1%)
    pallas_call x1, Pallas kernels, body(): pl.pallas_call(functools.partial(layer_kernel, rows, cols, coef), out_sha...  73.7 us
    pallas_call x1, Pallas kernels, body(): pl.pallas_call(place_kernel, out_shape=(jax.ShapeDtypeStruct((width, toke...  2.85 us

profile of v10, /device:TPU:0, one launch (start us, length us, event | category | flops | bytes accessed | tf_op | source)
XLA Modules:
  0.0 77.4 jit_solution(13362492480295624172)
XLA Ops:
  0.6 73.7 %shard_map.86 = (bf16[176,2048]{1,0:T(8,128)(2,1)}, bf16[512,192]{1,0:T(8,128)(2,1)}) custom-call(bf16[3,176,2048]{2,1,0:T(8,128)(2,1)} %qkv_hbm.1, bf16[176,2048]{1,0:T(8,128)(2,1)} %residual_hbm.1, bf16[1408,1408]{1,0:T(8,128)(2,1)} %out_weight_hbm.1, bf16[176,5632]{1,0:T(8,128)(2,1)} %merge_weight_hbm.1, f32[11,128]{1,0:T(8,128)} %bitcast.3, ...), custom_call_target="tpu_custom_call" | custom-call | tf_op jit(solution)/shard_map/pallas_call | solution.py:627
  74.4 2.9 %shard_map.87 = (bf16[176,2048]{1,0:T(8,128)(2,1)}, bf16[176,512]{1,0:T(8,128)(2,1)}) custom-call(bf16[176,2048]{1,0:T(8,128)(2,1)} %get-tuple-element.4.layer_hbm, bf16[512,192]{1,0:T(8,128)(2,1)} %get-tuple-element.5.got_hbm), custom_call_target="tpu_custom_call" | custom-call | tf_op jit(solution)/shard_map/pallas_call | solution.py:694

commit v11 on v8

--- a/solution.py
+++ b/solution.py
@@ -158,9 +158,9 @@
             )
         )
     ]
-    for load in loads:
+    for load in loads[:4]:
         load.start()
-    for load in loads[:4]:
+    for load in loads[:2]:
         load.wait()
     pl.semaphore_wait(barrier, rows + cols - 2)
 
@@ -223,10 +223,16 @@
                 device_id_type=MESH,
             )
         )
-    for copy in halo + shift:
+    for copy in halo:
+        copy.start()
+    for load in loads[4:]:
+        load.start()
+    for load in loads[2:4]:
+        load.wait()
+    for copy in shift:
         copy.start()
     residual[my_rows, :] = res[:, mine]
-    for load in loads[4:]:
+    for load in loads[4:6]:
         load.wait()
 
     images = groups_line_ref.shape[1]
@@ -288,6 +294,9 @@
     for copy in resident:
         copy.start()
     lax.fori_loop(blocks // 2, blocks, local_block, 0)
+
+    for load in loads[6:]:
+        load.wait()
 
     def turn(i, carry):
         at = pl.multiple_of(i * 128, 128)

time: 74 us -> 74.3 us (level); the launches traced: 73.9 us -> 73.4 us
  no operation moved by 1% of the time
where the time goes in v11:
time: 74.3 us; the launch traced here: 73.4 us
  Pallas kernels  72.6 us (98%)
  between operations  0.8 us (1%)
    pallas_call x1, Pallas kernels, body(): pl.pallas_call(functools.partial(layer_kernel, rows, cols, coef), out_sha...  69.7 us
    pallas_call x1, Pallas kernels, body(): pl.pallas_call(place_kernel, out_shape=(jax.ShapeDtypeStruct((width, toke...  2.85 us

profile of v11, /device:TPU:0, one launch (start us, length us, event | category | flops | bytes accessed | tf_op | source)
XLA Modules:
  0.0 73.4 jit_solution(6319226283793718185)
XLA Ops:
  0.6 69.7 %shard_map.86 = (bf16[176,2048]{1,0:T(8,128)(2,1)}, bf16[512,192]{1,0:T(8,128)(2,1)}) custom-call(bf16[3,176,2048]{2,1,0:T(8,128)(2,1)} %qkv_hbm.1, bf16[176,2048]{1,0:T(8,128)(2,1)} %residual_hbm.1, bf16[1408,1408]{1,0:T(8,128)(2,1)} %out_weight_hbm.1, bf16[176,5632]{1,0:T(8,128)(2,1)} %merge_weight_hbm.1, f32[11,128]{1,0:T(8,128)} %bitcast.3, ...), custom_call_target="tpu_custom_call" | custom-call | tf_op jit(solution)/shard_map/pallas_call | solution.py:599
  70.4 2.9 %shard_map.87 = (bf16[176,2048]{1,0:T(8,128)(2,1)}, bf16[176,512]{1,0:T(8,128)(2,1)}) custom-call(bf16[176,2048]{1,0:T(8,128)(2,1)} %get-tuple-element.4.layer_hbm, bf16[512,192]{1,0:T(8,128)(2,1)} %get-tuple-element.5.got_hbm), custom_call_target="tpu_custom_call" | custom-call | tf_op jit(solution)/shard_map/pallas_call | solution.py:666

commit v12 on v11

--- a/solution.py
+++ b/solution.py
@@ -335,12 +335,12 @@
     digits = jnp.where(which == 0, slot // 16, jnp.where(which == 1, slot % 16, 0))
     merged[width:, :] = digits.astype(jnp.float32).astype(jnp.bfloat16)
 
+    for copy in halo:
+        copy.wait_recv()
     for copy in shift:
         copy.wait_recv()
     for copy in gather:
         copy.start()
-    for copy in halo:
-        copy.wait_recv()
 
     def prepare_halo(i, carry):
         at = pl.multiple_of(i * QB, QB)

time: 74.3 us -> 74.3 us (level)
  no operation moved by 1% of the time
where the time goes in v12:
time: 74.3 us; the launch traced here: 73.4 us
  Pallas kernels  72.6 us (98%)
  between operations  0.8 us (1%)
    pallas_call x1, Pallas kernels, body(): pl.pallas_call(functools.partial(layer_kernel, rows, cols, coef), out_sha...  69.7 us
    pallas_call x1, Pallas kernels, body(): pl.pallas_call(place_kernel, out_shape=(jax.ShapeDtypeStruct((width, toke...  2.85 us

profile of v12, /device:TPU:0, one launch (start us, length us, event | category | flops | bytes accessed | tf_op | source)
XLA Modules:
  0.0 73.4 jit_solution(3102542921707522012)
XLA Ops:
  0.6 69.7 %shard_map.86 = (bf16[176,2048]{1,0:T(8,128)(2,1)}, bf16[512,192]{1,0:T(8,128)(2,1)}) custom-call(bf16[3,176,2048]{2,1,0:T(8,128)(2,1)} %qkv_hbm.1, bf16[176,2048]{1,0:T(8,128)(2,1)} %residual_hbm.1, bf16[1408,1408]{1,0:T(8,128)(2,1)} %out_weight_hbm.1, bf16[176,5632]{1,0:T(8,128)(2,1)} %merge_weight_hbm.1, f32[11,128]{1,0:T(8,128)} %bitcast.3, ...), custom_call_target="tpu_custom_call" | custom-call | tf_op jit(solution)/shard_map/pallas_call | solution.py:599
  70.4 2.9 %shard_map.87 = (bf16[176,2048]{1,0:T(8,128)(2,1)}, bf16[176,512]{1,0:T(8,128)(2,1)}) custom-call(bf16[176,2048]{1,0:T(8,128)(2,1)} %get-tuple-element.4.layer_hbm, bf16[512,192]{1,0:T(8,128)(2,1)} %get-tuple-element.5.got_hbm), custom_call_target="tpu_custom_call" | custom-call | tf_op jit(solution)/shard_map/pallas_call | solution.py:666

commit v13 on v8

--- a/solution.py
+++ b/solution.py
@@ -469,8 +469,6 @@
             )
             copy.start()
             passed.append(copy)
-    for copy in near:
-        copy.wait_send()
 
     def send_back(p):
         for k in range(1, cols):
@@ -492,6 +490,8 @@
         copy.wait()
     for copy in own + passed:
         copy.wait()
+    for copy in near:
+        copy.wait_send()
 
     total = None
     for j in range(4):

time: 74 us -> 74 us (level)
  no operation moved by 1% of the time
where the time goes in v13:
time: 74 us; the launch traced here: 73.9 us
  Pallas kernels  73.1 us (99%)
  between operations  0.8 us (1%)
    pallas_call x1, Pallas kernels, body(): pl.pallas_call(functools.partial(layer_kernel, rows, cols, coef), out_sha...  70.2 us
    pallas_call x1, Pallas kernels, body(): pl.pallas_call(place_kernel, out_shape=(jax.ShapeDtypeStruct((width, toke...  2.85 us

profile of v13, /device:TPU:0, one launch (start us, length us, event | category | flops | bytes accessed | tf_op | source)
XLA Modules:
  0.0 73.9 jit_solution(5528153494298054854)
XLA Ops:
  0.6 70.2 %shard_map.86 = (bf16[176,2048]{1,0:T(8,128)(2,1)}, bf16[512,192]{1,0:T(8,128)(2,1)}) custom-call(bf16[3,176,2048]{2,1,0:T(8,128)(2,1)} %qkv_hbm.1, bf16[176,2048]{1,0:T(8,128)(2,1)} %residual_hbm.1, bf16[1408,1408]{1,0:T(8,128)(2,1)} %out_weight_hbm.1, bf16[176,5632]{1,0:T(8,128)(2,1)} %merge_weight_hbm.1, f32[11,128]{1,0:T(8,128)} %bitcast.3, ...), custom_call_target="tpu_custom_call" | custom-call | tf_op jit(solution)/shard_map/pallas_call | solution.py:590
  70.9 2.9 %shard_map.87 = (bf16[176,2048]{1,0:T(8,128)(2,1)}, bf16[176,512]{1,0:T(8,128)(2,1)}) custom-call(bf16[176,2048]{1,0:T(8,128)(2,1)} %get-tuple-element.4.layer_hbm, bf16[512,192]{1,0:T(8,128)(2,1)} %get-tuple-element.5.got_hbm), custom_call_target="tpu_custom_call" | custom-call | tf_op jit(solution)/shard_map/pallas_call | solution.py:657
